TPU v7x, 32 devices: a whole 2x2x4 slice. The times are simulated.
32 devices in a mesh: cand: 2 (over y), gx: 4 (over z), gy: 2 (over x), ha: 2 (over core).
Axes of the slice: x: 2, y: 2, z: 4, core: 2. Of those that a mesh axis runs over, the one named last changes fastest.
Arguments:
- forward_field: float32 [4, 2, 3, 32, 16, 256], P('ha', None, None, ('cand', 'gx'), 'gy'), parts along dimension 3, may hold values from -4 to 4
- adjoint_source: float32 [4, 2, 3, 32, 16, 256], P('ha', None, None, ('cand', 'gx'), 'gy'), parts along dimension 3, may hold values from -60 to 60
- permittivity: float32 [32, 16, 256], P(('cand', 'gx'), 'gy'), parts along dimension 0, may hold values from 1 to 12
- frequency: float32 [4], replicated, may hold values from 0.1 to 0.35
- design_tiles: int32 [8, 4], P(('cand', 'gx'), 'gy'), parts along dimension 0, may hold values from 0 to 1, as said below
- mix_pairs: int32 [4, 3, 2], replicated, may hold values from 0 to 3
- pml_width: int32 [3], replicated, may hold values from 2 to 5
Outputs:
- adjoint_field: float32 [4, 2, 3, 32, 16, 256], P('ha', None, None, ('cand', 'gx'), 'gy'), parts along dimension 3
- gradient: float32 [32, 16, 256], P(('cand', 'gx'), 'gy'), parts along dimension 0
There are 2 independent parts, one for each index of `cand`. A program takes and returns all parts, laid end to end along the dimension named above; an argument that names none is the same for every part. Nothing has to cross between parts.
Inputs may be any that keep to these rules, and one draw needn't show every extreme that they name: `design_tiles`: 1 marks a design tile of 4 x 4 columns of cells; all ones lie in one rectangle of tiles that spans 1 to 3 devices' widths along x and 1 to 2 along y, and at least one tile is 1. `mix_pairs`: entries name harmonics.
All inputs are finite; a program needn't handle non-finite values.
Results may differ from a plain program's by a relative error of at most 0.0001.
Values sent between devices are 32-bit elements; how exact they have to be, the bound alone decides.
No kernel may reach another device: no remote copies, remote signals or barrier semaphores. Data moves between devices by JAX's collectives and lax.ppermute only.
A program may use at most 64 MiB of HBM per device.

v0:
```python
import jax
import jax.numpy as jnp
from jax import lax
from jax.sharding import PartitionSpec as P

ITERS = 3
TILE = 4


kerr_coef = 4.0
sigma_peak = 8.0


def extended(array, sides, width):
    for axis, dim in sides:
        count, length = (lax.axis_size(axis), array.shape[dim])
        up = [(i, (i + 1) % count) for i in range(count - 1)]
        down = [(j, i) for i, j in up]
        last = lax.slice_in_dim(array, length - width, length, axis=dim)
        first = lax.slice_in_dim(array, 0, width, axis=dim)
        before = lax.ppermute(last, axis, up)
        after = lax.ppermute(first, axis, down)
        array = jnp.concatenate([before, array, after], axis=dim)
    return array


def zero_rim(values, along):
    return jnp.zeros_like(lax.slice_in_dim(values, 0, 1, axis=along))


def step_ahead(values, upcoming, along):
    rest = lax.slice_in_dim(values, 1, values.shape[along], axis=along)
    return jnp.concatenate([rest, upcoming], axis=along) - values


def step_behind(values, earlier, along):
    rest = lax.slice_in_dim(values, 0, values.shape[along] - 1, axis=along)
    return values - jnp.concatenate([earlier, rest], axis=along)


def curl_ahead(field_x, field_y, field_z, ahead_x, ahead_y, ahead_z):
    first = field_x.ndim - 3
    second = first + 1
    third = first + 2
    mag_x = step_ahead(field_z, ahead_y[1], second) - step_ahead(field_y, ahead_z[1], third)
    mag_y = step_ahead(field_x, ahead_z[0], third) - step_ahead(field_z, ahead_x[1], first)
    mag_z = step_ahead(field_y, ahead_x[0], first) - step_ahead(field_x, ahead_y[0], second)
    return (mag_x, mag_y, mag_z)


def curl_behind(mag_x, mag_y, mag_z, behind_x, behind_y, behind_z):
    first = mag_x.ndim - 3
    second = first + 1
    third = first + 2
    out_x = step_behind(mag_z, behind_y[1], second) - step_behind(mag_y, behind_z[1], third)
    out_y = step_behind(mag_x, behind_z[0], third) - step_behind(mag_z, behind_x[1], first)
    out_z = step_behind(mag_y, behind_x[0], first) - step_behind(mag_x, behind_y[0], second)
    return (out_x, out_y, out_z)


def complex_pairs(chosen_field, chosen_adjoint):
    real = jnp.sum(
        chosen_field[:, :, 0] * chosen_adjoint[:, :, 0]
        - chosen_field[:, :, 1] * chosen_adjoint[:, :, 1],
        axis=1,
    )
    imag = jnp.sum(
        chosen_field[:, :, 0] * chosen_adjoint[:, :, 1]
        + chosen_field[:, :, 1] * chosen_adjoint[:, :, 0],
        axis=1,
    )
    return jnp.stack([real, imag], axis=1)


def absorb_profile(width, count, offset, length):
    place = offset + jnp.arange(length, dtype=jnp.int32)
    reach = jnp.maximum(jnp.maximum(width - place, place - (count - 1 - width)), 0)
    return (reach.astype(jnp.float32) / width.astype(jnp.float32)) ** 2


def tiles_to_cells(tiles, tile):
    rows, cols = tiles.shape
    spread = jnp.broadcast_to(tiles[:, None, :, None], (rows, tile, cols, tile))
    return spread.reshape(rows * tile, cols * tile).astype(jnp.float32)[:, :, None]


def z_plain_ahead(field_x, field_y):
    rim = zero_rim(field_x, field_x.ndim - 1)
    return (rim, rim)


def z_plain_behind(mag_x, mag_y):
    rim = zero_rim(mag_x, mag_x.ndim - 1)
    return (rim, rim)


def curl_corners(adjoint, cells_x, cells_y, z_ahead, z_behind):
    padded = extended(adjoint, (("gx", 3), ("gy", 4)), 1)
    field_x = padded[:, :, 0]
    field_y = padded[:, :, 1]
    field_z = padded[:, :, 2]
    rim_x = zero_rim(field_x, 2)
    rim_y = zero_rim(field_x, 3)
    mag_x, mag_y, mag_z = curl_ahead(
        field_x, field_y, field_z, (rim_x, rim_x), (rim_y, rim_y), z_ahead(field_x, field_y)
    )
    keep_x = ((jnp.arange(cells_x + 2) > 0) | (lax.axis_index("gx") > 0)).astype(jnp.float32)[
        :, None, None
    ]
    keep_y = ((jnp.arange(cells_y + 2) > 0) | (lax.axis_index("gy") > 0)).astype(jnp.float32)[
        :, None
    ]
    keeper = keep_x * keep_y
    mag_x = mag_x * keeper
    mag_y = mag_y * keeper
    mag_z = mag_z * keeper
    out_x, out_y, out_z = curl_behind(
        mag_x, mag_y, mag_z, (rim_x, rim_x), (rim_y, rim_y), z_behind(mag_x, mag_y)
    )
    return jnp.stack([out_x, out_y, out_z], axis=2)[:, :, :, 1:-1, 1:-1]


def shards(
    forward_field, adjoint_source, permittivity, frequency, design_tiles, mix_pairs, pml_width
):
    cells_x, cells_y, cells_z = permittivity.shape
    offset_x = lax.axis_index("gx") * cells_x
    offset_y = lax.axis_index("gy") * cells_y
    mask = tiles_to_cells(design_tiles, TILE)
    fields, sources = (forward_field, adjoint_source)
    offset_z = jnp.zeros((), jnp.int32)
    owned_count = forward_field.shape[0]
    start = lax.axis_index("ha") * owned_count
    squared = lax.dynamic_slice_in_dim(frequency * frequency, start, owned_count, 0)
    everyone = lax.all_gather(forward_field, "ha", axis=0, tiled=True)
    pairs = lax.dynamic_slice_in_dim(mix_pairs, start, owned_count, 0)
    chosen_field = everyone[pairs[:, :, 0]]
    sigma = sigma_peak * (
        absorb_profile(pml_width[0], cells_x * lax.axis_size("gx"), offset_x, cells_x)[
            :, None, None
        ]
        + absorb_profile(pml_width[1], cells_y * lax.axis_size("gy"), offset_y, cells_y)[
            None, :, None
        ]
        + absorb_profile(pml_width[2], cells_z, offset_z, cells_z)[None, None, :]
    )
    weight = squared[:, None, None, None, None, None]
    scale = 10.0 + weight * permittivity
    adjoint = sources / scale
    for sweep in range(ITERS):
        curled = curl_corners(adjoint, cells_x, cells_y, z_plain_ahead, z_plain_behind)
        gathered = lax.all_gather(adjoint, "ha", axis=0, tiled=True)
        kerr = complex_pairs(chosen_field, gathered[pairs[:, :, 1]])
        turned = jnp.stack([-adjoint[:, 1], adjoint[:, 0]], axis=1)
        applied = curled - weight * (
            permittivity * adjoint + sigma * turned + kerr_coef * mask * kerr
        )
        adjoint = adjoint + (sources - applied) / scale
    product = adjoint[:, 0] * fields[:, 0] - adjoint[:, 1] * fields[:, 1]
    partial_grad = mask * jnp.sum(squared[:, None, None, None, None] * product, axis=(0, 1))
    gradient = lax.psum(partial_grad, "ha")
    return (adjoint, gradient)


def solution(mesh):
    return jax.shard_map(
        shards,
        mesh=mesh,
        in_specs=(
            P("ha", None, None, ("cand", "gx"), "gy", None),
            P("ha", None, None, ("cand", "gx"), "gy", None),
            P(("cand", "gx"), "gy", None),
            P(),
            P(("cand", "gx"), "gy"),
            P(),
            P(),
        ),
        out_specs=(P("ha", None, None, ("cand", "gx"), "gy", None), P(("cand", "gx"), "gy", None)),
        check_vma=False,
    )
```

profile of v0, /device:TPU:0, one launch (start us, length us, event | category | flops | bytes accessed | tf_op | source)
XLA Modules:
  0.0 94.7 jit_solution(969377166001247180)
XLA Ops:
  0.6 0.7 mul.290
  1.4 0.8 multiply_add_fusion
  2.9 1.0 %copy_divide_fusion = f32[2,2,3,4,8,256]{5,4,3,0,1,2:T(8,128)S(1)} fusion(f32[2,2,3,4,8,256]{5,4,3,2,1,0:T(8,128)} %param.8, f32[2,4,8,256]{3,2,1,0:T(8,128)S(1)} %multiply_add_fusion), kind=kLoop, calls=%fused_computation.57 | loop fusion | flops 98304 | bytes 851968 | tf_op jit(solution)/shard_map/div | solution.py:149
  4.7 5.6 %collective-permute-start = (f32[2,2,3,1,8,256]{5,4,3,0,1,2:T(8,128)}, f32[2,2,3,1,8,256]{5,4,3,0,1,2:T(8,128)}, u32[]{:S(2)}, u32[]{:S(2)}) collective-permute-start(f32[2,2,3,1,8,256]{5,4,3,0,1,2:T(8,128)} %get-tuple-element.57), channel_id=1, source_target_pairs={{0,4},{4,8},{8,12},{1,5},{5,9},{9,13},{2,6},{6,10},{10,14},{3,7},{... | collective-permute-start | bytes 294920 | tf_op jit(solution)/shard_map/ppermute | solution.py:21
  10.3 1.3 %collective-permute-start.1 = (f32[2,2,3,1,8,256]{5,4,3,0,1,2:T(8,128)}, f32[2,2,3,1,8,256]{5,4,3,0,1,2:T(8,128)}, u32[]{:S(2)}, u32[]{:S(2)}) collective-permute-start(f32[2,2,3,1,8,256]{5,4,3,0,1,2:T(8,128)} %get-tuple-element.58), channel_id=1, source_target_pairs={{4,0},{8,4},{12,8},{5,1},{9,5},{13,9},{6,2},{10,6},{14,10},{7,3},{... | collective-permute-start | bytes 294920 | tf_op jit(solution)/shard_map/ppermute | solution.py:22
  11.6 2.4 %all_gather.13 = f32[4,2,3,4,8,256]{5,4,3,0,1,2:T(8,128)S(1)} all-gather(f32[2,2,3,4,8,256]{5,4,3,0,1,2:T(8,128)S(1)} %copy_divide_fusion), channel_id=1, replica_groups=mesh['cand'=2,'gx'=4,'gy'=2,'ha'=2] {'ha'}, dimensions={0}, use_global_device_ids=true | all-gather | bytes 1179648 | tf_op jit(solution)/shard_map/all_gather | solution.py:152
  17.1 0.8 slice_negate_fusion.2
  18.9 2.4 %all_gather.12 = f32[4,2,3,4,8,256]{5,4,3,2,1,0:T(8,128)S(1)} all-gather(f32[2,2,3,4,8,256]{5,4,3,2,1,0:T(8,128)S(1)} %copy-done.5), channel_id=1, replica_groups=mesh['cand'=2,'gx'=4,'gy'=2,'ha'=2] {'ha'}, dimensions={0}, use_global_device_ids=true | all-gather | bytes 1179648 | tf_op jit(solution)/shard_map/all_gather | solution.py:135
  27.2 1.1 %pad_maximum_fusion.11 = (f32[2,2,3,6,1,256]{5,4,3,0,1,2:T(1,128)S(1)}, f32[2,2,3,6,1,256]{5,4,3,0,1,2:T(1,128)S(1)}) fusion(f32[2,2,3,1,8,256]{5,4,3,0,1,2:T(8,128)} %collective-permute-done.1, f32[2,2,3,4,8,256]{5,4,3,0,1,2:T(8,128)S(1)} %copy_divide_fusion, f32[2,2,3,1,8,256]{5,4,3,0,1,2:T(8,128)} %collective-permute-done), kind=kLoop, calls=%fused_computation.87 | loop fusion | flops 73728 | bytes 737280 | tf_op jit(solution)/shard_map/slice | solution.py:19
  28.4 3.4 %collective-permute-start.2 = (f32[2,2,3,6,1,256]{5,4,3,0,1,2:T(1,128)S(1)}, f32[2,2,3,6,1,256]{5,4,3,0,1,2:T(1,128)S(1)}, u32[]{:S(2)}, u32[]{:S(2)}) collective-permute-start(f32[2,2,3,6,1,256]{5,4,3,0,1,2:T(1,128)S(1)} %get-tuple-element.32), channel_id=1, source_target_pairs={{0,2},{1,3},{4,6},{5,7},{8,10},{9,11},{12,14},{13,15},{16,18},{17,... | collective-permute-start | bytes 221192 | tf_op jit(solution)/shard_map/ppermute | solution.py:21
  31.8 1.3 %collective-permute-start.3 = (f32[2,2,3,6,1,256]{5,4,3,0,1,2:T(1,128)S(1)}, f32[2,2,3,6,1,256]{5,4,3,0,1,2:T(1,128)S(1)}, u32[]{:S(2)}, u32[]{:S(2)}) collective-permute-start(f32[2,2,3,6,1,256]{5,4,3,0,1,2:T(1,128)S(1)} %get-tuple-element.33), channel_id=1, source_target_pairs={{2,0},{3,1},{6,4},{7,5},{10,8},{11,9},{14,12},{15,13},{18,16},{19,... | collective-permute-start | bytes 221192 | tf_op jit(solution)/shard_map/ppermute | solution.py:22
  33.7 4.3 %collective-permute-done.3 = f32[2,2,3,6,1,256]{5,4,3,0,1,2:T(1,128)S(1)} collective-permute-done((f32[2,2,3,6,1,256]{5,4,3,0,1,2:T(1,128)S(1)}, f32[2,2,3,6,1,256]{5,4,3,0,1,2:T(1,128)S(1)}, u32[]{:S(2)}, u32[]{:S(2)}) %collective-permute-start.3) | collective-permute-done | bytes 73760 | tf_op jit(solution)/shard_map/ppermute | solution.py:22
  38.0 1.2 %pad_maximum_fusion = f32[2,2,3,6,10,256]{5,4,3,0,1,2:T(8,128)S(1)} fusion(f32[2,2,3,6,1,256]{5,4,3,0,1,2:T(1,128)S(1)} %collective-permute-done.3, f32[2,2,3,1,8,256]{5,4,3,0,1,2:T(8,128)} %collective-permute-done.1, f32[2,2,3,4,8,256]{5,4,3,0,1,2:T(8,128)S(1)} %copy_divide_fusion, f32[2,2,3,1,8,256]{5,4,3,0,1,2:T(8,128)} %collective-permute-done, ...), kind=kLoop, calls=%fused_computation.4 | loop fusion | flops 737280 | bytes 1474560 | tf_op jit(solution)/shard_map/concatenate | solution.py:23
  42.5 4.6 %collective-permute-start.4 = (f32[2,2,3,1,8,256]{5,4,3,0,1,2:T(8,128)}, f32[2,2,3,1,8,256]{5,4,3,0,1,2:T(8,128)S(1)}, u32[]{:S(2)}, u32[]{:S(2)}) collective-permute-start(f32[2,2,3,1,8,256]{5,4,3,0,1,2:T(8,128)} %get-tuple-element.51), channel_id=1, source_target_pairs={{0,4},{4,8},{8,12},{1,5},{5,9},{9,13},{2,6},{6,10},{10,14},{3,7},{... | collective-permute-start | bytes 294920 | tf_op jit(solution)/shard_map/ppermute | solution.py:21
  47.1 2.4 %all_gather.14 = f32[4,2,3,4,8,256]{5,4,3,2,0,1:T(8,128)S(1)} all-gather(f32[2,2,3,4,8,256]{5,4,3,2,0,1:T(8,128)S(1)} %fusion.10), channel_id=1, replica_groups=mesh['cand'=2,'gx'=4,'gy'=2,'ha'=2] {'ha'}, dimensions={0}, use_global_device_ids=true | all-gather | bytes 1179648 | tf_op jit(solution)/shard_map/all_gather | solution.py:152
  49.4 1.3 %collective-permute-start.5 = (f32[2,2,3,1,8,256]{5,4,3,0,1,2:T(8,128)}, f32[2,2,3,1,8,256]{5,4,3,0,1,2:T(8,128)S(1)}, u32[]{:S(2)}, u32[]{:S(2)}) collective-permute-start(f32[2,2,3,1,8,256]{5,4,3,0,1,2:T(8,128)} %get-tuple-element.50), channel_id=1, source_target_pairs={{4,0},{8,4},{12,8},{5,1},{9,5},{13,9},{6,2},{10,6},{14,10},{7,3},{... | collective-permute-start | bytes 294920 | tf_op jit(solution)/shard_map/ppermute | solution.py:22
  50.7 1.6 %gather_fusion.2 = f32[6,2,3,4,8,256]{5,4,3,2,1,0:T(8,128)} fusion(f32[4,2,3,4,8,256]{5,4,3,2,0,1:T(8,128)S(1)} %all_gather.14, s32[1024]{0:T(1024)S(1)} %pad_clamp_fusion), kind=kCustom, calls=%fused_computation.2 | custom fusion | bytes 2359320 | tf_op jit(solution)/shard_map/gather | solution.py:153
  52.5 3.9 %collective-permute-done.5 = f32[2,2,3,1,8,256]{5,4,3,0,1,2:T(8,128)S(1)} collective-permute-done((f32[2,2,3,1,8,256]{5,4,3,0,1,2:T(8,128)}, f32[2,2,3,1,8,256]{5,4,3,0,1,2:T(8,128)S(1)}, u32[]{:S(2)}, u32[]{:S(2)}) %collective-permute-start.5) | collective-permute-done | bytes 98336 | tf_op jit(solution)/shard_map/ppermute | solution.py:22
  56.5 1.6 %collective-permute-start.6 = (f32[2,2,3,6,1,256]{5,4,3,0,1,2:T(1,128)S(1)}, f32[2,2,3,6,1,256]{5,4,3,0,1,2:T(1,128)S(1)}, u32[]{:S(2)}, u32[]{:S(2)}) collective-permute-start(f32[2,2,3,6,1,256]{5,4,3,0,1,2:T(1,128)S(1)} %get-tuple-element.30), channel_id=1, source_target_pairs={{0,2},{1,3},{4,6},{5,7},{8,10},{9,11},{12,14},{13,15},{16,18},{17,... | collective-permute-start | bytes 221192 | tf_op jit(solution)/shard_map/ppermute | solution.py:21
  58.1 1.3 %collective-permute-start.7 = (f32[2,2,3,6,1,256]{5,4,3,0,1,2:T(1,128)S(1)}, f32[2,2,3,6,1,256]{5,4,3,0,1,2:T(1,128)S(1)}, u32[]{:S(2)}, u32[]{:S(2)}) collective-permute-start(f32[2,2,3,6,1,256]{5,4,3,0,1,2:T(1,128)S(1)} %get-tuple-element.31), channel_id=1, source_target_pairs={{2,0},{3,1},{6,4},{7,5},{10,8},{11,9},{14,12},{15,13},{18,16},{19,... | collective-permute-start | bytes 221192 | tf_op jit(solution)/shard_map/ppermute | solution.py:22
  60.0 4.3 %collective-permute-done.7 = f32[2,2,3,6,1,256]{5,4,3,0,1,2:T(1,128)S(1)} collective-permute-done((f32[2,2,3,6,1,256]{5,4,3,0,1,2:T(1,128)S(1)}, f32[2,2,3,6,1,256]{5,4,3,0,1,2:T(1,128)S(1)}, u32[]{:S(2)}, u32[]{:S(2)}) %collective-permute-start.7) | collective-permute-done | bytes 73760 | tf_op jit(solution)/shard_map/ppermute | solution.py:22
  67.9 4.0 %collective-permute-start.8 = (f32[2,2,3,1,8,256]{5,4,3,0,1,2:T(8,128)}, f32[2,2,3,1,8,256]{5,4,3,0,1,2:T(8,128)}, u32[]{:S(2)}, u32[]{:S(2)}) collective-permute-start(f32[2,2,3,1,8,256]{5,4,3,0,1,2:T(8,128)} %get-tuple-element.42), channel_id=1, source_target_pairs={{0,4},{4,8},{8,12},{1,5},{5,9},{9,13},{2,6},{6,10},{10,14},{3,7},{... | collective-permute-start | bytes 294920 | tf_op jit(solution)/shard_map/ppermute | solution.py:21
  71.9 1.3 %collective-permute-start.9 = (f32[2,2,3,1,8,256]{5,4,3,0,1,2:T(8,128)}, f32[2,2,3,1,8,256]{5,4,3,0,1,2:T(8,128)}, u32[]{:S(2)}, u32[]{:S(2)}) collective-permute-start(f32[2,2,3,1,8,256]{5,4,3,0,1,2:T(8,128)} %get-tuple-element.41), channel_id=1, source_target_pairs={{4,0},{8,4},{12,8},{5,1},{9,5},{13,9},{6,2},{10,6},{14,10},{7,3},{... | collective-permute-start | bytes 294920 | tf_op jit(solution)/shard_map/ppermute | solution.py:22
  73.2 2.4 %all_gather.15 = f32[4,2,3,4,8,256]{5,4,3,2,1,0:T(8,128)S(1)} all-gather(f32[2,2,3,4,8,256]{5,4,3,2,1,0:T(8,128)S(1)} %copy.59), channel_id=1, replica_groups=mesh['cand'=2,'gx'=4,'gy'=2,'ha'=2] {'ha'}, dimensions={0}, use_global_device_ids=true | all-gather | bytes 1179648 | tf_op jit(solution)/shard_map/all_gather | solution.py:152
  75.5 1.6 %gather_fusion.3 = f32[6,2,3,4,8,256]{5,4,3,2,1,0:T(8,128)} fusion(f32[4,2,3,4,8,256]{5,4,3,2,1,0:T(8,128)S(1)} %all_gather.15, s32[1024]{0:T(1024)S(1)} %pad_clamp_fusion), kind=kCustom, calls=%fused_computation.3 | custom fusion | bytes 2359320 | tf_op jit(solution)/shard_map/gather | solution.py:153
  77.2 1.0 %constant_dynamic-update-slice_fusion.5 = f32[2,2,3,6,8,256]{5,4,3,0,1,2:T(8,128)S(1)} fusion(f32[2,2,3,1,8,256]{5,4,3,0,1,2:T(8,128)} %collective-permute-done.8), kind=kLoop, calls=%fused_computation.96 | loop fusion | bytes 196608
  78.7 0.9 constant_dynamic-update-slice_fusion.3
  79.7 1.6 %collective-permute-start.10 = (f32[2,2,3,6,1,256]{5,4,3,0,1,2:T(1,128)S(1)}, f32[2,2,3,6,1,256]{5,4,3,0,1,2:T(1,128)S(1)}, u32[]{:S(2)}, u32[]{:S(2)}) collective-permute-start(f32[2,2,3,6,1,256]{5,4,3,0,1,2:T(1,128)S(1)} %get-tuple-element.28), channel_id=1, source_target_pairs={{0,2},{1,3},{4,6},{5,7},{8,10},{9,11},{12,14},{13,15},{16,18},{17,... | collective-permute-start | bytes 221192 | tf_op jit(solution)/shard_map/ppermute | solution.py:21
  81.3 1.3 %collective-permute-start.11 = (f32[2,2,3,6,1,256]{5,4,3,0,1,2:T(1,128)S(1)}, f32[2,2,3,6,1,256]{5,4,3,0,1,2:T(1,128)S(1)}, u32[]{:S(2)}, u32[]{:S(2)}) collective-permute-start(f32[2,2,3,6,1,256]{5,4,3,0,1,2:T(1,128)S(1)} %get-tuple-element.29), channel_id=1, source_target_pairs={{2,0},{3,1},{6,4},{7,5},{10,8},{11,9},{14,12},{15,13},{18,16},{19,... | collective-permute-start | bytes 221192 | tf_op jit(solution)/shard_map/ppermute | solution.py:22
  83.2 4.3 %collective-permute-done.11 = f32[2,2,3,6,1,256]{5,4,3,0,1,2:T(1,128)S(1)} collective-permute-done((f32[2,2,3,6,1,256]{5,4,3,0,1,2:T(1,128)S(1)}, f32[2,2,3,6,1,256]{5,4,3,0,1,2:T(1,128)S(1)}, u32[]{:S(2)}, u32[]{:S(2)}) %collective-permute-start.11) | collective-permute-done | bytes 73760 | tf_op jit(solution)/shard_map/ppermute | solution.py:22
  89.7 0.8 copy.64
  90.7 4.0 %psum.7 = f32[4,8,256]{2,1,0:T(8,128)} all-reduce(f32[4,8,256]{2,1,0:T(8,128)S(1)} %broadcast_multiply_fusion), channel_id=1, replica_groups=mesh['cand'=2,'gx'=4,'gy'=2,'ha'=2] {'ha'}, use_global_device_ids=true, to_apply=%region_7.0 | all-reduce | flops 8192 | bytes 65536 | tf_op jit(solution)/shard_map/psum | solution.py:161
  (124 shorter events, 19.4 us)
Async XLA Ops:
  2.3 0.6 copy-start.3
  2.9 11.0 %copy-start.13 = (s32[3]{0:T(128)S(1)}, s32[3]{0:T(128)}, u32[]{:S(2)}) copy-start(s32[3]{0:T(128)} %param.13) | copy-start | bytes 40
  4.0 14.0 %copy-start.14 = (s32[4,3,2]{0,2,1:T(2,128)S(1)}, s32[4,3,2]{0,2,1:T(2,128)}, u32[]{:S(2)}) copy-start(s32[4,3,2]{0,2,1:T(2,128)} %param.12) | copy-start | bytes 292
  4.0 14.9 %copy-start.5 = (f32[2,2,3,4,8,256]{5,4,3,2,1,0:T(8,128)S(1)}, f32[2,2,3,4,8,256]{5,4,3,2,1,0:T(8,128)}, u32[]{:S(2)}) copy-start(f32[2,2,3,4,8,256]{5,4,3,2,1,0:T(8,128)} %param.7) | copy-start | bytes 1179652
  4.7 22.5 %collective-permute-start = (f32[2,2,3,1,8,256]{5,4,3,0,1,2:T(8,128)}, f32[2,2,3,1,8,256]{5,4,3,0,1,2:T(8,128)}, u32[]{:S(2)}, u32[]{:S(2)}) collective-permute-start(f32[2,2,3,1,8,256]{5,4,3,0,1,2:T(8,128)} %get-tuple-element.57), channel_id=1, source_target_pairs={{0,4},{4,8},{8,12},{1,5},{5,9},{9,13},{2,6},{6,10},{10,14},{3,7},{... | collective-permute-start | bytes 294920 | tf_op jit(solution)/shard_map/ppermute | solution.py:21
  10.3 16.9 %collective-permute-start.1 = (f32[2,2,3,1,8,256]{5,4,3,0,1,2:T(8,128)}, f32[2,2,3,1,8,256]{5,4,3,0,1,2:T(8,128)}, u32[]{:S(2)}, u32[]{:S(2)}) collective-permute-start(f32[2,2,3,1,8,256]{5,4,3,0,1,2:T(8,128)} %get-tuple-element.58), channel_id=1, source_target_pairs={{4,0},{8,4},{12,8},{5,1},{9,5},{13,9},{6,2},{10,6},{14,10},{7,3},{... | collective-permute-start | bytes 294920 | tf_op jit(solution)/shard_map/ppermute | solution.py:22
  13.9 8.5 %copy-start.18 = (s32[1,2]{1,0:T(1,128)S(1)}, s32[1,2]{1,0:T(1,128)}, u32[]{:S(2)}) copy-start(s32[1,2]{1,0:T(1,128)} %param.11) | copy-start | bytes 28
  22.6 1.2 %copy-start.15 = (f32[8]{0:T(128)}, f32[8]{0:T(128)S(1)}, u32[]{:S(2)}) copy-start(f32[8]{0:T(128)S(1)} %convert_element_type.73) | copy-start | bytes 100
  23.2 3.3 %copy-start.17 = (s32[6]{0:T(128)S(1)}, s32[6]{0:T(128)}, u32[]{:S(2)}) copy-start(s32[6]{0:T(128)} %reshape.171) | copy-start | bytes 76
  28.4 5.4 %collective-permute-start.2 = (f32[2,2,3,6,1,256]{5,4,3,0,1,2:T(1,128)S(1)}, f32[2,2,3,6,1,256]{5,4,3,0,1,2:T(1,128)S(1)}, u32[]{:S(2)}, u32[]{:S(2)}) collective-permute-start(f32[2,2,3,6,1,256]{5,4,3,0,1,2:T(1,128)S(1)} %get-tuple-element.32), channel_id=1, source_target_pairs={{0,2},{1,3},{4,6},{5,7},{8,10},{9,11},{12,14},{13,15},{16,18},{17,... | collective-permute-start | bytes 221192 | tf_op jit(solution)/shard_map/ppermute | solution.py:21
  31.8 6.2 %collective-permute-start.3 = (f32[2,2,3,6,1,256]{5,4,3,0,1,2:T(1,128)S(1)}, f32[2,2,3,6,1,256]{5,4,3,0,1,2:T(1,128)S(1)}, u32[]{:S(2)}, u32[]{:S(2)}) collective-permute-start(f32[2,2,3,6,1,256]{5,4,3,0,1,2:T(1,128)S(1)} %get-tuple-element.33), channel_id=1, source_target_pairs={{2,0},{3,1},{6,4},{7,5},{10,8},{11,9},{14,12},{15,13},{18,16},{19,... | collective-permute-start | bytes 221192 | tf_op jit(solution)/shard_map/ppermute | solution.py:22
  40.3 1.0 %copy-start = (f32[2,2,3,4,8,256]{5,4,3,2,1,0:T(8,128)S(1)}, f32[2,2,3,4,8,256]{5,4,3,2,1,0:T(8,128)}, u32[]{:S(2)}) copy-start(f32[2,2,3,4,8,256]{5,4,3,2,1,0:T(8,128)} %param.8) | copy-start | bytes 1179652
  40.3 1.0 %copy-start.4 = (f32[2,4,8,256]{3,2,1,0:T(8,128)S(1)}, f32[2,4,8,256]{3,2,1,0:T(8,128)}, u32[]{:S(2)}) copy-start(f32[2,4,8,256]{3,2,1,0:T(8,128)} %copy-done.3) | copy-start | bytes 196612
  40.3 1.1 %copy-start.7 = (f32[2,1,3,4,8,256]{5,4,3,0,1,2:T(8,128)S(1)}, f32[2,1,3,4,8,256]{5,4,3,0,1,2:T(8,128)}, u32[]{:S(2)}) copy-start(f32[2,1,3,4,8,256]{5,4,3,0,1,2:T(8,128)} %get-tuple-element.52) | copy-start | bytes 589828
  40.3 1.1 %copy-start.8 = (f32[2,1,3,4,8,256]{5,4,3,0,1,2:T(8,128)S(1)}, f32[2,1,3,4,8,256]{5,4,3,0,1,2:T(8,128)}, u32[]{:S(2)}) copy-start(f32[2,1,3,4,8,256]{5,4,3,0,1,2:T(8,128)} %get-tuple-element.53) | copy-start | bytes 589828
  40.4 1.1 %copy-start.10 = (f32[4,8,256]{2,1,0:T(8,128)S(1)}, f32[4,8,256]{2,1,0:T(8,128)}, u32[]{:S(2)}) copy-start(f32[4,8,256]{2,1,0:T(8,128)} %param.9) | copy-start | bytes 98308
  40.4 1.1 %copy-start.11 = (f32[4,8,256]{2,1,0:T(8,128)S(1)}, f32[4,8,256]{2,1,0:T(8,128)}, u32[]{:S(2)}) copy-start(f32[4,8,256]{2,1,0:T(8,128)} %add_multiply_fusion) | copy-start | bytes 98308
  40.4 1.1 %copy-start.12 = (f32[8]{0:T(128)S(1)}, f32[8]{0:T(128)}, u32[]{:S(2)}) copy-start(f32[8]{0:T(128)} %broadcast_multiply_fusion.2) | copy-start | bytes 100
  42.5 9.9 %collective-permute-start.4 = (f32[2,2,3,1,8,256]{5,4,3,0,1,2:T(8,128)}, f32[2,2,3,1,8,256]{5,4,3,0,1,2:T(8,128)S(1)}, u32[]{:S(2)}, u32[]{:S(2)}) collective-permute-start(f32[2,2,3,1,8,256]{5,4,3,0,1,2:T(8,128)} %get-tuple-element.51), channel_id=1, source_target_pairs={{0,4},{4,8},{8,12},{1,5},{5,9},{9,13},{2,6},{6,10},{10,14},{3,7},{... | collective-permute-start | bytes 294920 | tf_op jit(solution)/shard_map/ppermute | solution.py:21
  49.4 6.9 %collective-permute-start.5 = (f32[2,2,3,1,8,256]{5,4,3,0,1,2:T(8,128)}, f32[2,2,3,1,8,256]{5,4,3,0,1,2:T(8,128)S(1)}, u32[]{:S(2)}, u32[]{:S(2)}) collective-permute-start(f32[2,2,3,1,8,256]{5,4,3,0,1,2:T(8,128)} %get-tuple-element.50), channel_id=1, source_target_pairs={{4,0},{8,4},{12,8},{5,1},{9,5},{13,9},{6,2},{10,6},{14,10},{7,3},{... | collective-permute-start | bytes 294920 | tf_op jit(solution)/shard_map/ppermute | solution.py:22
  52.4 7.0 %copy-start.2 = (f32[6,2,3,4,8,256]{5,4,3,2,1,0:T(8,128)S(1)}, f32[6,2,3,4,8,256]{5,4,3,2,1,0:T(8,128)}, u32[]{:S(2)}) copy-start(f32[6,2,3,4,8,256]{5,4,3,2,1,0:T(8,128)} %gather_fusion.2) | copy-start | bytes 3538948
  56.5 3.5 %collective-permute-start.6 = (f32[2,2,3,6,1,256]{5,4,3,0,1,2:T(1,128)S(1)}, f32[2,2,3,6,1,256]{5,4,3,0,1,2:T(1,128)S(1)}, u32[]{:S(2)}, u32[]{:S(2)}) collective-permute-start(f32[2,2,3,6,1,256]{5,4,3,0,1,2:T(1,128)S(1)} %get-tuple-element.30), channel_id=1, source_target_pairs={{0,2},{1,3},{4,6},{5,7},{8,10},{9,11},{12,14},{13,15},{16,18},{17,... | collective-permute-start | bytes 221192 | tf_op jit(solution)/shard_map/ppermute | solution.py:21
  58.1 6.2 %collective-permute-start.7 = (f32[2,2,3,6,1,256]{5,4,3,0,1,2:T(1,128)S(1)}, f32[2,2,3,6,1,256]{5,4,3,0,1,2:T(1,128)S(1)}, u32[]{:S(2)}, u32[]{:S(2)}) collective-permute-start(f32[2,2,3,6,1,256]{5,4,3,0,1,2:T(1,128)S(1)} %get-tuple-element.31), channel_id=1, source_target_pairs={{2,0},{3,1},{6,4},{7,5},{10,8},{11,9},{14,12},{15,13},{18,16},{19,... | collective-permute-start | bytes 221192 | tf_op jit(solution)/shard_map/ppermute | solution.py:22
  67.9 9.3 %collective-permute-start.8 = (f32[2,2,3,1,8,256]{5,4,3,0,1,2:T(8,128)}, f32[2,2,3,1,8,256]{5,4,3,0,1,2:T(8,128)}, u32[]{:S(2)}, u32[]{:S(2)}) collective-permute-start(f32[2,2,3,1,8,256]{5,4,3,0,1,2:T(8,128)} %get-tuple-element.42), channel_id=1, source_target_pairs={{0,4},{4,8},{8,12},{1,5},{5,9},{9,13},{2,6},{6,10},{10,14},{3,7},{... | collective-permute-start | bytes 294920 | tf_op jit(solution)/shard_map/ppermute | solution.py:21
  71.9 6.8 %collective-permute-start.9 = (f32[2,2,3,1,8,256]{5,4,3,0,1,2:T(8,128)}, f32[2,2,3,1,8,256]{5,4,3,0,1,2:T(8,128)}, u32[]{:S(2)}, u32[]{:S(2)}) collective-permute-start(f32[2,2,3,1,8,256]{5,4,3,0,1,2:T(8,128)} %get-tuple-element.41), channel_id=1, source_target_pairs={{4,0},{8,4},{12,8},{5,1},{9,5},{13,9},{6,2},{10,6},{14,10},{7,3},{... | collective-permute-start | bytes 294920 | tf_op jit(solution)/shard_map/ppermute | solution.py:22
  75.5 2.6 %copy-start.9 = (f32[2,1,3,4,8,256]{5,4,3,0,1,2:T(8,128)S(1)}, f32[2,1,3,4,8,256]{5,4,3,0,1,2:T(8,128)}, u32[]{:S(2)}) copy-start(f32[2,1,3,4,8,256]{5,4,3,0,1,2:T(8,128)} %get-tuple-element.37) | copy-start | bytes 589828
  77.2 5.4 %copy-start.1 = (f32[6,2,3,4,8,256]{5,4,3,2,1,0:T(8,128)S(1)}, f32[6,2,3,4,8,256]{5,4,3,2,1,0:T(8,128)}, u32[]{:S(2)}) copy-start(f32[6,2,3,4,8,256]{5,4,3,2,1,0:T(8,128)} %gather_fusion.3) | copy-start | bytes 3538948
  79.7 3.5 %collective-permute-start.10 = (f32[2,2,3,6,1,256]{5,4,3,0,1,2:T(1,128)S(1)}, f32[2,2,3,6,1,256]{5,4,3,0,1,2:T(1,128)S(1)}, u32[]{:S(2)}, u32[]{:S(2)}) collective-permute-start(f32[2,2,3,6,1,256]{5,4,3,0,1,2:T(1,128)S(1)} %get-tuple-element.28), channel_id=1, source_target_pairs={{0,2},{1,3},{4,6},{5,7},{8,10},{9,11},{12,14},{13,15},{16,18},{17,... | collective-permute-start | bytes 221192 | tf_op jit(solution)/shard_map/ppermute | solution.py:21
  81.3 6.2 %collective-permute-start.11 = (f32[2,2,3,6,1,256]{5,4,3,0,1,2:T(1,128)S(1)}, f32[2,2,3,6,1,256]{5,4,3,0,1,2:T(1,128)S(1)}, u32[]{:S(2)}, u32[]{:S(2)}) collective-permute-start(f32[2,2,3,6,1,256]{5,4,3,0,1,2:T(1,128)S(1)} %get-tuple-element.29), channel_id=1, source_target_pairs={{2,0},{3,1},{6,4},{7,5},{10,8},{11,9},{14,12},{15,13},{18,16},{19,... | collective-permute-start | bytes 221192 | tf_op jit(solution)/shard_map/ppermute | solution.py:22
  89.4 1.1 %copy-start.6 = (f32[2,2,3,4,8,256]{5,4,3,2,1,0:T(8,128)S(1)}, f32[2,2,3,4,8,256]{5,4,3,2,1,0:T(8,128)}, u32[]{:S(2)}) copy-start(f32[2,2,3,4,8,256]{5,4,3,2,1,0:T(8,128)} %param.7) | copy-start | bytes 1179652
  89.7 0.9 copy-start.16
where the time goes:
time: 95.4 us; the launch traced here: 94.7 us
  starting transfers between devices  28.4 us (30%)
  waiting for transfers between devices  18.3 us (19%)
  other arithmetic  15.3 us (16%)
  local copies, waits for them, and re-layouts  14.2 us (15%)
  blocking collectives  13.4 us (14%)
  between operations  5.08 us (5%)
    ppermute x6, starting transfers between devices, extended(): before = lax.ppermute(last, axis, up)  20.6 us
    ppermute x6, waiting for transfers between devices, extended(): after = lax.ppermute(first, axis, down)  17.2 us
    ppermute x6, starting transfers between devices, extended(): after = lax.ppermute(first, axis, down)  7.72 us
    all_gather x3, blocking collectives, shards(): gathered = lax.all_gather(adjoint, 'ha', axis=0, tiled=True)  7.11 us
    psum x1, blocking collectives, shards(): gradient = lax.psum(partial_grad, 'ha')  3.99 us
    gather x3, local copies, waits for them, and re-layouts, shards(): kerr = complex_pairs(chosen_field, gathered[pairs[:, :, 1]])  3.9 us
    unnamed x41, local copies, waits for them, and re-layouts  3.04 us
    all_gather x1, blocking collectives, shards(): everyone = lax.all_gather(forward_field, 'ha', axis=0, tiled=True)  2.36 us
  transfers between devices with their start and end apart: 12, of which 8 were waited for; matrix products, arithmetic and copies ran while one was open for 13% of the time, Pallas kernels for 0%

commit v1 on v0

v1 whole, which is shorter than its diff:
```python
import functools

import jax
import jax.numpy as jnp
from jax import lax
from jax.experimental import pallas as pl
from jax.experimental.pallas import tpu as pltpu
from jax.sharding import PartitionSpec as P

ITERS = 3
TILE = 4
DEEP = ITERS
NEAR = ITERS - 1

kerr_coef = 4.0
sigma_peak = 8.0

VMEM = pl.BlockSpec(memory_space=pltpu.VMEM)
SMEM = pl.BlockSpec(memory_space=pltpu.SMEM)


def round_up(value, unit):
    return (value + unit - 1) // unit * unit


def tile_mask(tiles_ref, plane, rows, lanes):
    place = lax.broadcasted_iota(jnp.int32, (rows, lanes), 0) // TILE
    mask = jnp.zeros((rows, lanes), jnp.float32)
    for col in range(rows // TILE):
        cell = tiles_ref[plane // TILE, col].astype(jnp.float32)
        mask = jnp.where(place == col, cell, mask)
    return mask


class Sizes:
    def __init__(self, owned, cells, counts):
        self.owned = owned
        self.values = owned * 6
        self.cx, self.cy, self.cz = cells
        self.gx, self.gy, self.ha = counts
        self.y_rows = round_up(self.cx * (self.values * (DEEP + NEAR) + DEEP), 8)
        self.d_rows = round_up(self.values * (DEEP**2 + NEAR**2) + DEEP**2, 8)
        self.x_tiles = self.values * (DEEP + NEAR) + DEEP


def edge_planes(cx, upper, depth):
    return list(range(cx - depth, cx)) if upper else list(range(depth))


def pack_kernel(sz, src_ref, fwd_ref, eps_ref, tiles_ref, *out_refs):
    pair = sz.gy == 2
    low_y = lax.axis_index("gy") == 0
    masks = [kerr_coef * tile_mask(tiles_ref, x, sz.cy, sz.cz) for x in range(sz.cx)]
    kinds = [(h, r, c) for h in range(sz.owned) for r in range(2) for c in range(3)]

    def x_face(ref, upper):
        at = 0
        for h, r, c in kinds:
            for x in edge_planes(sz.cx, upper, DEEP):
                ref[at] = src_ref[h, r, c, x]
                at += 1
        for h, r, c in kinds:
            for x in edge_planes(sz.cx, upper, NEAR):
                ref[at] = fwd_ref[h, r, c, x] * masks[x]
                at += 1
        for x in edge_planes(sz.cx, upper, DEEP):
            ref[at] = eps_ref[x]
            at += 1

    def rows_of(tile, top, depth):
        return tile[sz.cy - depth :] if top else tile[:depth]

    def y_part(planes_deep, planes_near, top):
        for h, r, c in kinds:
            for x in planes_deep:
                yield rows_of(src_ref[h, r, c, x], top, DEEP)
        for h, r, c in kinds:
            for x in planes_near:
                yield rows_of(fwd_ref[h, r, c, x] * masks[x], top, NEAR)
        for x in planes_deep:
            yield rows_of(eps_ref[x], top, DEEP)

    def write(ref, parts, others=None, choose=None):
        at = 0
        for part in parts:
            if others is not None:
                part = jnp.where(choose, part, next(others))
            ref[at : at + part.shape[0]] = part
            at += part.shape[0]
        if at < ref.shape[0]:
            ref[at:] = jnp.zeros((ref.shape[0] - at, sz.cz), jnp.float32)

    everywhere = list(range(sz.cx))

    def corner(upper, top):
        return y_part(edge_planes(sz.cx, upper, DEEP), edge_planes(sz.cx, upper, NEAR), top)

    x_face(out_refs[0], True)
    x_face(out_refs[1], False)
    if pair:
        write(
            out_refs[2],
            y_part(everywhere, everywhere, True),
            y_part(everywhere, everywhere, False),
            low_y,
        )
        write(out_refs[3], corner(False, True), corner(True, False), low_y)
        write(out_refs[4], corner(True, True), corner(False, False), low_y)
    else:
        write(out_refs[2], y_part(everywhere, everywhere, True))
        write(out_refs[3], y_part(everywhere, everywhere, False))
        write(out_refs[4], corner(True, False))
        write(out_refs[5], corner(False, True))
        write(out_refs[6], corner(True, True))
        write(out_refs[7], corner(False, False))


def sweep_kernel(
    sz, mix_ref, freq_ref, pml_ref, tiles_ref, eps_ref, *refs
):
    cx, cy, cz = sz.cx, sz.cy, sz.cz
    rows = cy + 8
    wide = cx + 2 * DEEP
    harmonics = sz.owned * sz.ha
    per_core = 10
    sides = [refs[per_core * s : per_core * (s + 1)] for s in range(sz.ha)]
    out_ref, grad_ref = refs[per_core * sz.ha : per_core * sz.ha + 2]
    base, first, second, fwd, invs, mags, eps_all = refs[per_core * sz.ha + 2 :]

    at_x, at_y, at_h = lax.axis_index("gx"), lax.axis_index("gy"), lax.axis_index("ha")
    pair = sz.gy == 2
    start = at_h * sz.owned

    def from_own(index):
        return lax.rem(index - start + harmonics, harmonics)

    def globally(position):
        return lax.rem(position + start, harmonics)

    squared = [freq_ref[globally(h)] * freq_ref[globally(h)] for h in range(harmonics)]

    sub = lax.broadcasted_iota(jnp.int32, (rows, cz), 0)
    lane = lax.broadcasted_iota(jnp.int32, (rows, cz), 1)
    row = jnp.where(sub < cy + 4, sub, sub - rows)
    place_y = row + at_y * cy
    keep_y = jnp.where((place_y >= 0) & (place_y < cy * sz.gy), 1.0, 0.0)

    def profile(width, place, count):
        reach = jnp.maximum(jnp.maximum(width - place, place - (count - 1 - width)), 0)
        return (reach.astype(jnp.float32) / jnp.full(reach.shape, width).astype(jnp.float32)) ** 2

    sigma_y = profile(pml_ref[1], place_y, cy * sz.gy)
    sigma_z = profile(pml_ref[2], lane, cz)

    def sigma_at(x):
        place = jnp.full((rows, cz), x - DEEP + at_x * cx)
        return sigma_peak * (profile(pml_ref[0], place, cx * sz.gx) + sigma_y + sigma_z)

    def keep_at(x):
        place = x - DEEP + at_x * cx
        inside = jnp.where((place >= 0) & (place < cx * sz.gx), 1.0, 0.0)
        return keep_y * inside

    def gate(value, low):
        if not pair:
            return value
        return jnp.where((at_y == 0) != low, value, 0.0)

    def halo(high, low):
        depth = high.shape[0]
        gap = jnp.zeros((8 - 2 * depth, cz), jnp.float32)
        return jnp.concatenate([gate(high, False), gap, gate(low, True)], axis=0)

    kinds = [(h, r, c) for h in range(sz.owned) for r in range(2) for c in range(3)]

    def x_index(field, kind, plane):
        n = kinds.index(kind)
        if field == 0:
            return n * DEEP + plane
        return sz.values * DEEP + n * NEAR + plane

    def y_rows_at(field, kind, plane, planes_deep, planes_near):
        n = kinds.index(kind)
        if field == 0:
            return (n * planes_deep + plane) * DEEP
        return sz.values * planes_deep * DEEP + (n * planes_near + plane) * NEAR

    def eps_rows_at(plane, planes_deep, planes_near):
        return sz.values * (planes_deep * DEEP + planes_near * NEAR) + plane * DEEP

    def take(ref, at, depth):
        return ref[at : at + depth]

    _, _, x_lo, x_hi, y_hi, y_lo, c_lo_hi, c_lo_lo, c_hi_hi, c_hi_lo = sides[0]
    tail = sz.values * (DEEP + NEAR)
    for d in range(DEEP):
        at = eps_rows_at(d, DEEP, NEAR)
        eps_all[d, :cy] = x_lo[tail + d]
        eps_all[d, cy:] = halo(take(c_lo_hi, at, DEEP), take(c_lo_lo, at, DEEP))
        eps_all[DEEP + cx + d, :cy] = x_hi[tail + d]
        eps_all[DEEP + cx + d, cy:] = halo(take(c_hi_hi, at, DEEP), take(c_hi_lo, at, DEEP))
    for x in range(cx):
        at = eps_rows_at(x, cx, cx)
        eps_all[DEEP + x, :cy] = eps_ref[x]
        eps_all[DEEP + x, cy:] = halo(take(y_hi, at, DEEP), take(y_lo, at, DEEP))

    def scales(x, _):
        eps = eps_all[x]
        for h in range(harmonics):
            invs[h, x] = 1.0 / (10.0 + squared[h] * eps)
        return 0

    lax.fori_loop(0, wide, scales, 0)

    masks = [kerr_coef * tile_mask(tiles_ref, x, cy, cz) for x in range(cx)]
    for s, side in enumerate(sides):
        own_src, own_fwd, x_lo, x_hi, y_hi, y_lo, c_lo_hi, c_lo_lo, c_hi_hi, c_hi_lo = side
        for kind in kinds:
            h, r, c = kind
            g = s * sz.owned + h
            for d in range(DEEP):
                at = y_rows_at(0, kind, d, DEEP, NEAR)
                x = d
                base[g, r, c, x, :cy] = x_lo[x_index(0, kind, d)] * invs[g, x, :cy]
                base[g, r, c, x, cy:] = (
                    halo(take(c_lo_hi, at, DEEP), take(c_lo_lo, at, DEEP)) * invs[g, x, cy:]
                )
                x = DEEP + cx + d
                base[g, r, c, x, :cy] = x_hi[x_index(0, kind, d)] * invs[g, x, :cy]
                base[g, r, c, x, cy:] = (
                    halo(take(c_hi_hi, at, DEEP), take(c_hi_lo, at, DEEP)) * invs[g, x, cy:]
                )
            for d in range(NEAR):
                at = y_rows_at(1, kind, d, DEEP, NEAR)
                fwd[g, r, c, d, :cy] = x_lo[x_index(1, kind, d)]
                fwd[g, r, c, d, cy:] = halo(take(c_lo_hi, at, NEAR), take(c_lo_lo, at, NEAR))
                fwd[g, r, c, NEAR + cx + d, :cy] = x_hi[x_index(1, kind, d)]
                fwd[g, r, c, NEAR + cx + d, cy:] = halo(
                    take(c_hi_hi, at, NEAR), take(c_hi_lo, at, NEAR)
                )
            for x in range(cx):
                at = y_rows_at(0, kind, x, cx, cx)
                base[g, r, c, DEEP + x, :cy] = own_src[h, r, c, x] * invs[g, DEEP + x, :cy]
                base[g, r, c, DEEP + x, cy:] = (
                    halo(take(y_hi, at, DEEP), take(y_lo, at, DEEP)) * invs[g, DEEP + x, cy:]
                )
                at = y_rows_at(1, kind, x, cx, cx)
                fwd[g, r, c, NEAR + x, :cy] = own_fwd[h, r, c, x] * masks[x]
                fwd[g, r, c, NEAR + x, cy:] = halo(take(y_hi, at, NEAR), take(y_lo, at, NEAR))

    def y_ahead(v):
        return pltpu.roll(v, rows - 1, 0)

    def y_behind(v):
        return pltpu.roll(v, 1, 0)

    def z_ahead(v):
        return jnp.where(lane == cz - 1, 0.0, pltpu.roll(v, cz - 1, 1))

    def z_behind(v):
        return jnp.where(lane == 0, 0.0, pltpu.roll(v, 1, 1))

    def forward_mags(v_ref, h, r, x, keep):
        fx, fy, fz = v_ref[h, r, 0, x], v_ref[h, r, 1, x], v_ref[h, r, 2, x]
        next_y, next_z = v_ref[h, r, 1, x + 1], v_ref[h, r, 2, x + 1]
        mag_y = ((z_ahead(fx) - fx) - (next_z - fz)) * keep
        mag_z = ((next_y - fy) - (y_ahead(fx) - fx)) * keep
        return fx, fy, fz, mag_y, mag_z

    pairs = [
        (from_own(mix_ref[globally(h), p, 0]), from_own(mix_ref[globally(h), p, 1]))
        for h in range(harmonics)
        for p in range(mix_ref.shape[1])
    ]
    count = mix_ref.shape[1]

    def sweep(k, v_ref, store):
        lo, hi = k + 1, wide - 1 - k

        keep = keep_at(k)
        for h in range(harmonics):
            for r in range(2):
                _, _, _, mag_y, mag_z = forward_mags(v_ref, h, r, k, keep)
                mags[h, r, 0] = mag_y
                mags[h, r, 1] = mag_z

        def body(x, _):
            keep = keep_at(x)
            sigma = sigma_at(x)
            results = []
            for h in range(harmonics):
                inv = invs[h, x]
                slope = 2.0 - 10.0 * inv
                absorb = squared[h] * sigma
                curls = []
                here = []
                for r in range(2):
                    fx, fy, fz, mag_y, mag_z = forward_mags(v_ref, h, r, x, keep)
                    mag_x = ((y_ahead(fz) - fz) - (z_ahead(fy) - fy)) * keep
                    past_y, past_z = mags[h, r, 0], mags[h, r, 1]
                    mags[h, r, 0] = mag_y
                    mags[h, r, 1] = mag_z
                    curls.append(
                        (
                            (mag_z - y_behind(mag_z)) - (mag_y - z_behind(mag_y)),
                            (mag_x - z_behind(mag_x)) - (mag_z - past_z),
                            (mag_y - past_y) - (mag_x - y_behind(mag_x)),
                        )
                    )
                    here.append((fx, fy, fz))
                for c in range(3):
                    real = imag = None
                    for p in range(count):
                        a, b = pairs[h * count + p]
                        fr, fi = fwd[a, 0, c, x - 1], fwd[a, 1, c, x - 1]
                        vr, vi = v_ref[b, 0, c, x], v_ref[b, 1, c, x]
                        one = fr * vr - fi * vi
                        two = fr * vi + fi * vr
                        real = one if real is None else real + one
                        imag = two if imag is None else imag + two
                    vr, vi = here[0][c], here[1][c]
                    new_r = (
                        base[h, 0, c, x]
                        + vr * slope
                        + inv * (squared[h] * real - absorb * vi - curls[0][c])
                    )
                    new_i = (
                        base[h, 1, c, x]
                        + vi * slope
                        + inv * (squared[h] * imag + absorb * vr - curls[1][c])
                    )
                    results.append((h, c, new_r, new_i))
                store(x, keep, results)
                results = []
            return 0

        lax.fori_loop(lo, hi, body, 0)

    def store_in(ref):
        def store(x, keep, results):
            for h, c, new_r, new_i in results:
                ref[h, 0, c, x] = new_r * keep
                ref[h, 1, c, x] = new_i * keep

        return store

    def store_out(x, keep, results):
        for h, c, new_r, new_i in results:
            new_r, new_i = new_r[:cy], new_i[:cy]
            if h < sz.owned:
                out_ref[h, 0, c, x - DEEP] = new_r
                out_ref[h, 1, c, x - DEEP] = new_i
            term = (squared[h] / kerr_coef) * (
                new_r * fwd[h, 0, c, x - 1, :cy] - new_i * fwd[h, 1, c, x - 1, :cy]
            )
            if h == 0 and c == 0:
                grad_ref[x - DEEP] = term
            else:
                grad_ref[x - DEEP] += term

    sweep(0, base, store_in(first))
    sweep(1, first, store_in(second))
    sweep(2, second, store_out)


def chain(count_x, count_y, step_x, step_y):
    sends = []
    for x in range(count_x):
        for y in range(count_y):
            to_x, to_y = x + step_x, y + step_y
            if 0 <= to_x < count_x and 0 <= to_y < count_y:
                sends.append((x * count_y + y, to_x * count_y + to_y))
    return sends


def shards(
    forward_field, adjoint_source, permittivity, frequency, design_tiles, mix_pairs, pml_width
):
    counts = tuple(lax.axis_size(name) for name in ("gx", "gy", "ha"))
    sz = Sizes(forward_field.shape[0], permittivity.shape, counts)
    pair = sz.gy == 2
    f32 = jnp.float32
    x_buf = jax.ShapeDtypeStruct((sz.x_tiles, sz.cy, sz.cz), f32)
    y_buf = jax.ShapeDtypeStruct((sz.y_rows, sz.cz), f32)
    d_buf = jax.ShapeDtypeStruct((sz.d_rows, sz.cz), f32)
    n_y, n_d = (1, 2) if pair else (2, 4)
    packed = pl.pallas_call(
        functools.partial(pack_kernel, sz),
        out_shape=[x_buf, x_buf] + [y_buf] * n_y + [d_buf] * n_d,
        in_specs=[VMEM, VMEM, VMEM, SMEM],
        out_specs=[VMEM] * (2 + n_y + n_d),
        name="pack",
    )(adjoint_source, forward_field, permittivity, design_tiles)

    def send(buffer, *steps):
        pairs = [edge for step in steps for edge in chain(sz.gx, sz.gy, *step)]
        return lax.ppermute(buffer, ("gx", "gy"), pairs)

    x_lo = send(packed[0], (1, 0))
    x_hi = send(packed[1], (-1, 0))
    if pair:
        y_any = send(packed[2], (0, 1), (0, -1))
        anti = send(packed[3], (-1, 1), (1, -1))
        main = send(packed[4], (1, 1), (-1, -1))
        got = [x_lo, x_hi, y_any, anti, main]
        order = (0, 1, 2, 2, 3, 4, 4, 3)
    else:
        got = [
            x_lo,
            x_hi,
            send(packed[3], (0, -1)),
            send(packed[2], (0, 1)),
            send(packed[4], (1, -1)),
            send(packed[6], (1, 1)),
            send(packed[7], (-1, -1)),
            send(packed[5], (-1, 1)),
        ]
        order = (0, 1, 2, 3, 4, 5, 6, 7)

    own = [adjoint_source, forward_field] + got
    flip = [(i, sz.ha - 1 - i) for i in range(sz.ha)]
    other = [lax.ppermute(buffer, "ha", flip) for buffer in own]

    def spread(buffers):
        return buffers[:2] + [buffers[2 + i] for i in order]

    rows, wide, harmonics = sz.cy + 8, sz.cx + 2 * DEEP, sz.owned * sz.ha
    field = (harmonics, 2, 3, wide, rows, sz.cz)
    near = (harmonics, 2, 3, wide - 2, rows, sz.cz)
    adjoint, gradient = pl.pallas_call(
        functools.partial(sweep_kernel, sz),
        out_shape=[
            jax.ShapeDtypeStruct(adjoint_source.shape, f32),
            jax.ShapeDtypeStruct(permittivity.shape, f32),
        ],
        in_specs=[SMEM] * 4 + [VMEM] * 21,
        out_specs=[VMEM, VMEM],
        scratch_shapes=[
            pltpu.VMEM(field, f32),
            pltpu.VMEM(field, f32),
            pltpu.VMEM(field, f32),
            pltpu.VMEM(near, f32),
            pltpu.VMEM((harmonics, wide, rows, sz.cz), f32),
            pltpu.VMEM((harmonics, 2, 2, rows, sz.cz), f32),
            pltpu.VMEM((wide, rows, sz.cz), f32),
        ],
        compiler_params=pltpu.CompilerParams(vmem_limit_bytes=48 * 1024 * 1024),
        name="sweeps",
    )(
        mix_pairs,
        frequency,
        pml_width,
        design_tiles,
        permittivity,
        *spread(own),
        *spread(other),
    )
    return (adjoint, gradient)


def solution(mesh):
    return jax.shard_map(
        shards,
        mesh=mesh,
        in_specs=(
            P("ha", None, None, ("cand", "gx"), "gy", None),
            P("ha", None, None, ("cand", "gx"), "gy", None),
            P(("cand", "gx"), "gy", None),
            P(),
            P(("cand", "gx"), "gy"),
            P(),
            P(),
        ),
        out_specs=(P("ha", None, None, ("cand", "gx"), "gy", None), P(("cand", "gx"), "gy", None)),
        check_vma=False,
    )
```

time: 95.4 us -> 46 us (0.48)
  other arithmetic: 15.3 us -> 0 us
  Pallas kernels: 0 us -> 14.1 us
  blocking collectives: 13.4 us -> 0 us
  starting transfers between devices: 28.4 us -> 16.1 us
  local copies, waits for them, and re-layouts: 14.2 us -> 3.52 us
  waiting for transfers between devices: 18.3 us -> 10.9 us
  between operations: 5.08 us -> 0.71 us
    pallas_call x0 -> x2, Pallas kernels: none -> 14.1 us  [the longest x1 11.7 us: shards(): pl.pallas_call(functools.partial(sweep_kernel, sz), out_shape=[jax.ShapeD...]
    ppermute x12, starting transfers between devices: 28.4 us -> 16.1 us  [the longest x5 15.3 us: send(): return lax.ppermute(buffer, ('gx', 'gy'), pairs)]
    all_gather x4 -> x0, blocking collectives: 9.46 us -> none  [the longest x3 7.11 us: shards(): gathered = lax.all_gather(adjoint, 'ha', axis=0, tiled=True)]
    ppermute x12, waiting for transfers between devices: 18.3 us -> 10.9 us  [the longest x5 9.54 us: send(): return lax.ppermute(buffer, ('gx', 'gy'), pairs)]
    gather x4 -> x0, local copies, waits for them, and re-layouts: 4.52 us -> none  [the longest x3 3.9 us: shards(): kerr = complex_pairs(chosen_field, gathered[pairs[:, :, 1]])]
    slice x30 -> x0, local copies, waits for them, and re-layouts: 4.35 us -> none  [the longest x2 1.4 us: extended(): first = lax.slice_in_dim(array, 0, width, axis=dim)]
    psum x1 -> x0, blocking collectives: 3.99 us -> none  [shards(): gradient = lax.psum(partial_grad, 'ha')]
    mul x8 -> x0, other arithmetic: 3.53 us -> none  [the longest x3 1.43 us: curl_corners(): mag_z = mag_z * keeper]
  transfers between devices with their start and end apart: 12 -> 12, of which waited for: 8 -> 6; matrix products, arithmetic and copies ran while one was open for 13% -> 2% of each run, Pallas kernels for 0% -> 0%
where the time goes in v1:
time: 46 us; the launch traced here: 45.4 us
  starting transfers between devices  16.1 us (35%)
  Pallas kernels  14.1 us (31%)
  waiting for transfers between devices  10.9 us (24%)
  local copies, waits for them, and re-layouts  3.52 us (8%)
  between operations  0.71 us (2%)
    ppermute x5, starting transfers between devices, send(): return lax.ppermute(buffer, ('gx', 'gy'), pairs)  15.3 us
    pallas_call x1, Pallas kernels, shards(): pl.pallas_call(functools.partial(sweep_kernel, sz), out_shape=[jax.ShapeD...  11.7 us
    ppermute x5, waiting for transfers between devices, send(): return lax.ppermute(buffer, ('gx', 'gy'), pairs)  9.54 us
    unnamed x13, local copies, waits for them, and re-layouts  3.52 us
    pallas_call x1, Pallas kernels, shards(): pl.pallas_call(functools.partial(pack_kernel, sz), out_shape=[x_buf, x_bu...  2.41 us
    ppermute x7, waiting for transfers between devices, shards(): other = [lax.ppermute(buffer, 'ha', flip) for buffer in own]  1.41 us
  transfers between devices with their start and end apart: 12, of which 6 were waited for; matrix products, arithmetic and copies ran while one was open for 2% of the time, Pallas kernels for 0%

profile of v1, /device:TPU:0, one launch (start us, length us, event | category | flops | bytes accessed | tf_op | source)
XLA Modules:
  0.0 45.4 jit_solution(5086563552181515032)
XLA Ops:
  0.6 0.0 copy-start
  0.6 2.4 %pack.1 = (f32[63,8,256]{2,1,0:T(8,128)}, f32[63,8,256]{2,1,0:T(8,128)}, f32[256,256]{1,0:T(8,128)}, f32[168,256]{1,0:T(8,128)}, f32[168,256]{1,0:T(8,128)}) custom-call(f32[2,2,3,4,8,256]{5,4,3,2,1,0:T(8,128)} %refs_0_.1, f32[2,2,3,4,8,256]{5,4,3,2,1,0:T(8,128)} %refs_1_.1, f32[4,8,256]{2,1,0:T(8,128)} %eps_ref.3, s32[1,2]{1,0:T(1,128)} %tiles_ref.3), custom_call_target="tpu_custom_call" | custom-call | tf_op jit(solution)/shard_map/pack/pallas_call | solution.py:387
  3.1 5.0 %collective-permute-start = (f32[63,8,256]{2,1,0:T(8,128)}, f32[63,8,256]{2,1,0:T(8,128)S(1)}, u32[]{:S(2)}, u32[]{:S(2)}) collective-permute-start(f32[63,8,256]{2,1,0:T(8,128)} %get-tuple-element.7), channel_id=1, source_target_pairs={{0,4},{2,6},{4,8},{6,10},{8,12},{10,14},{1,5},{3,7},{5,9},{7,11},{... | collective-permute-start | bytes 1548296 | tf_op jit(solution)/shard_map/ppermute | solution.py:397
  8.0 1.3 %collective-permute-start.1 = (f32[63,8,256]{2,1,0:T(8,128)}, f32[63,8,256]{2,1,0:T(8,128)S(1)}, u32[]{:S(2)}, u32[]{:S(2)}) collective-permute-start(f32[63,8,256]{2,1,0:T(8,128)} %get-tuple-element.8), channel_id=1, source_target_pairs={{4,0},{6,2},{8,4},{10,6},{12,8},{14,10},{5,1},{7,3},{9,5},{11,7},{... | collective-permute-start | bytes 1548296 | tf_op jit(solution)/shard_map/ppermute | solution.py:397
  9.3 0.7 %collective-permute-start.3 = (f32[168,256]{1,0:T(8,128)}, f32[168,256]{1,0:T(8,128)S(1)}, u32[]{:S(2)}, u32[]{:S(2)}) collective-permute-start(f32[168,256]{1,0:T(8,128)} %get-tuple-element.10), channel_id=1, source_target_pairs={{4,2},{8,6},{12,10},{2,4},{6,8},{10,12},{5,3},{9,7},{13,11},{3,5},... | collective-permute-start | bytes 516104 | tf_op jit(solution)/shard_map/ppermute | solution.py:397
  10.0 5.4 %collective-permute-start.2 = (f32[256,256]{1,0:T(8,128)}, f32[256,256]{1,0:T(8,128)S(1)}, u32[]{:S(2)}, u32[]{:S(2)}) collective-permute-start(f32[256,256]{1,0:T(8,128)} %get-tuple-element.9), channel_id=1, source_target_pairs={{0,2},{4,6},{8,10},{12,14},{2,0},{6,4},{10,8},{14,12},{1,3},{5,7},... | collective-permute-start | bytes 786440 | tf_op jit(solution)/shard_map/ppermute | solution.py:397
  15.4 2.9 %collective-permute-start.4 = (f32[168,256]{1,0:T(8,128)}, f32[168,256]{1,0:T(8,128)S(1)}, u32[]{:S(2)}, u32[]{:S(2)}) collective-permute-start(f32[168,256]{1,0:T(8,128)} %get-tuple-element.11), channel_id=1, source_target_pairs={{0,6},{4,10},{8,14},{6,0},{10,4},{14,8},{1,7},{5,11},{9,15},{7,1},... | collective-permute-start | bytes 516104 | tf_op jit(solution)/shard_map/ppermute | solution.py:397
  18.3 0.0 collective-permute-done.3.refs_6_.refs_9_
  18.4 0.1 collective-permute-start.10
  18.4 2.0 %collective-permute-done.refs_2_ = f32[63,8,256]{2,1,0:T(8,128)S(1)} collective-permute-done((f32[63,8,256]{2,1,0:T(8,128)}, f32[63,8,256]{2,1,0:T(8,128)S(1)}, u32[]{:S(2)}, u32[]{:S(2)}) %collective-permute-start) | collective-permute-done | bytes 516128 | tf_op jit(solution)/shard_map/ppermute | solution.py:397
  20.4 0.0 collective-permute-start.7
  20.4 4.3 %collective-permute-done.1.refs_3_ = f32[63,8,256]{2,1,0:T(8,128)S(1)} collective-permute-done((f32[63,8,256]{2,1,0:T(8,128)}, f32[63,8,256]{2,1,0:T(8,128)S(1)}, u32[]{:S(2)}, u32[]{:S(2)}) %collective-permute-start.1) | collective-permute-done | bytes 516128 | tf_op jit(solution)/shard_map/ppermute | solution.py:397
  24.8 0.0 collective-permute-start.8
  24.8 3.2 %collective-permute-done.4.refs_7_.refs_8_ = f32[168,256]{1,0:T(8,128)S(1)} collective-permute-done((f32[168,256]{1,0:T(8,128)}, f32[168,256]{1,0:T(8,128)S(1)}, u32[]{:S(2)}, u32[]{:S(2)}) %collective-permute-start.4) | collective-permute-done | bytes 172064 | tf_op jit(solution)/shard_map/ppermute | solution.py:397
  28.0 0.0 collective-permute-start.11
  28.0 0.0 collective-permute-done.2.refs_4_.refs_5_
  28.0 0.5 %collective-permute-start.6 = (f32[2,2,3,4,8,256]{5,4,3,2,1,0:T(8,128)S(1)}, f32[2,2,3,4,8,256]{5,4,3,2,1,0:T(8,128)}, u32[]{:S(2)}, u32[]{:S(2)}) collective-permute-start(f32[2,2,3,4,8,256]{5,4,3,2,1,0:T(8,128)S(1)} %copy-done.1), channel_id=1, source_target_pairs={{0,1},{1,0},{2,3},{3,2},{4,5},{5,4},{6,7},{7,6},{8,9},{9,8},{10,11... | collective-permute-start | bytes 1179656 | tf_op jit(solution)/shard_map/ppermute | solution.py:422
  28.5 0.0 collective-permute-done.10.refs_16_.refs_19_
  28.5 0.1 collective-permute-start.5
  28.6 0.8 %collective-permute-done.11.refs_17_.refs_18_ = f32[168,256]{1,0:T(8,128)S(1)} collective-permute-done((f32[168,256]{1,0:T(8,128)S(1)}, f32[168,256]{1,0:T(8,128)S(1)}, u32[]{:S(2)}, u32[]{:S(2)}) %collective-permute-start.11) | collective-permute-done | bytes 172064 | tf_op jit(solution)/shard_map/ppermute | solution.py:422
  29.4 0.1 collective-permute-start.9
  29.5 0.8 %copy.9.mix_ref = s32[4,3,2]{2,1,0:T(4,128)S(1)} copy(s32[4,3,2]{0,2,1:T(2,128)} %param.12) | data formatting | bytes 192 | tf_op args[5]
  30.3 0.0 collective-permute-done.6.refs_11_
  30.3 0.3 collective-permute-done.5.refs_10_
  30.6 0.3 collective-permute-done.9.refs_14_.refs_15_
  30.9 0.0 collective-permute-done.7.refs_12_
  30.9 0.0 collective-permute-done.8.refs_13_
  30.9 0.8 %copy-done.2 = f32[4,8,256]{2,1,0:T(8,128)S(1)} copy-done((f32[4,8,256]{2,1,0:T(8,128)S(1)}, f32[4,8,256]{2,1,0:T(8,128)}, u32[]{:S(2)}) %copy-start.2) | copy-done | bytes 32792
  31.7 0.7 %copy-done.3 = s32[1,2]{1,0:T(1,128)S(1)} copy-done((s32[1,2]{1,0:T(1,128)S(1)}, s32[1,2]{1,0:T(1,128)}, u32[]{:S(2)}) %copy-start.3) | copy-done | bytes 32
  32.3 0.7 %copy-done.4 = f32[4]{0:T(128)S(1)} copy-done((f32[4]{0:T(128)S(1)}, f32[4]{0:T(128)}, u32[]{:S(2)}) %copy-start.4) | copy-done | bytes 40
  33.0 0.7 %copy-done.5 = s32[3]{0:T(128)S(1)} copy-done((s32[3]{0:T(128)S(1)}, s32[3]{0:T(128)}, u32[]{:S(2)}) %copy-start.5) | copy-done | bytes 36
  33.6 11.7 %sweeps.1 = (f32[2,2,3,4,8,256]{5,4,3,2,1,0:T(8,128)}, f32[4,8,256]{2,1,0:T(8,128)}) custom-call(s32[4,3,2]{2,1,0:T(4,128)S(1)} %copy.9.mix_ref, f32[4]{0:T(128)S(1)} %copy-done.4, s32[3]{0:T(128)S(1)} %copy-done.5, s32[1,2]{1,0:T(1,128)S(1)} %copy-done.3, f32[4,8,256]{2,1,0:T(8,128)S(1)} %copy-done.2, f32[2,2,3,4,8,256]{5,4,3,2,1,0:T(8,128)S(1)} %copy-done, ...), custom_call_target="tpu_custom_call" | custom-call | tf_op jit(solution)/shard_map/sweeps/pallas_call | solution.py:430
  (7 shorter events, 0.0 us)
Async XLA Ops:
  0.6 27.9 %copy-start = (f32[2,2,3,4,8,256]{5,4,3,2,1,0:T(8,128)S(1)}, f32[2,2,3,4,8,256]{5,4,3,2,1,0:T(8,128)}, u32[]{:S(2)}) copy-start(f32[2,2,3,4,8,256]{5,4,3,2,1,0:T(8,128)} %refs_0_.1) | copy-start | bytes 1179652
  0.6 27.3 %copy-start.1 = (f32[2,2,3,4,8,256]{5,4,3,2,1,0:T(8,128)S(1)}, f32[2,2,3,4,8,256]{5,4,3,2,1,0:T(8,128)}, u32[]{:S(2)}) copy-start(f32[2,2,3,4,8,256]{5,4,3,2,1,0:T(8,128)} %refs_1_.1) | copy-start | bytes 1179652
  3.1 17.4 %collective-permute-start = (f32[63,8,256]{2,1,0:T(8,128)}, f32[63,8,256]{2,1,0:T(8,128)S(1)}, u32[]{:S(2)}, u32[]{:S(2)}) collective-permute-start(f32[63,8,256]{2,1,0:T(8,128)} %get-tuple-element.7), channel_id=1, source_target_pairs={{0,4},{2,6},{4,8},{6,10},{8,12},{10,14},{1,5},{3,7},{5,9},{7,11},{... | collective-permute-start | bytes 1548296 | tf_op jit(solution)/shard_map/ppermute | solution.py:397
  8.0 16.7 %collective-permute-start.1 = (f32[63,8,256]{2,1,0:T(8,128)}, f32[63,8,256]{2,1,0:T(8,128)S(1)}, u32[]{:S(2)}, u32[]{:S(2)}) collective-permute-start(f32[63,8,256]{2,1,0:T(8,128)} %get-tuple-element.8), channel_id=1, source_target_pairs={{4,0},{6,2},{8,4},{10,6},{12,8},{14,10},{5,1},{7,3},{9,5},{11,7},{... | collective-permute-start | bytes 1548296 | tf_op jit(solution)/shard_map/ppermute | solution.py:397
  9.3 9.0 %collective-permute-start.3 = (f32[168,256]{1,0:T(8,128)}, f32[168,256]{1,0:T(8,128)S(1)}, u32[]{:S(2)}, u32[]{:S(2)}) collective-permute-start(f32[168,256]{1,0:T(8,128)} %get-tuple-element.10), channel_id=1, source_target_pairs={{4,2},{8,6},{12,10},{2,4},{6,8},{10,12},{5,3},{9,7},{13,11},{3,5},... | collective-permute-start | bytes 516104 | tf_op jit(solution)/shard_map/ppermute | solution.py:397
  10.0 18.0 %collective-permute-start.2 = (f32[256,256]{1,0:T(8,128)}, f32[256,256]{1,0:T(8,128)S(1)}, u32[]{:S(2)}, u32[]{:S(2)}) collective-permute-start(f32[256,256]{1,0:T(8,128)} %get-tuple-element.9), channel_id=1, source_target_pairs={{0,2},{4,6},{8,10},{12,14},{2,0},{6,4},{10,8},{14,12},{1,3},{5,7},... | collective-permute-start | bytes 786440 | tf_op jit(solution)/shard_map/ppermute | solution.py:397
  15.4 12.5 %collective-permute-start.4 = (f32[168,256]{1,0:T(8,128)}, f32[168,256]{1,0:T(8,128)S(1)}, u32[]{:S(2)}, u32[]{:S(2)}) collective-permute-start(f32[168,256]{1,0:T(8,128)} %get-tuple-element.11), channel_id=1, source_target_pairs={{0,6},{4,10},{8,14},{6,0},{10,4},{14,8},{1,7},{5,11},{9,15},{7,1},... | collective-permute-start | bytes 516104 | tf_op jit(solution)/shard_map/ppermute | solution.py:397
  18.4 10.1 %collective-permute-start.10 = (f32[168,256]{1,0:T(8,128)S(1)}, f32[168,256]{1,0:T(8,128)S(1)}, u32[]{:S(2)}, u32[]{:S(2)}) collective-permute-start(f32[168,256]{1,0:T(8,128)S(1)} %collective-permute-done.3.refs_6_.refs_9_), channel_id=1, source_target_pairs={{0,1},{1,0},{2,3},{3,2},{4,5},{5,4},{6,7},{7,6},{8,9},{9,8},{10,11... | collective-permute-start | bytes 516104 | tf_op jit(solution)/shard_map/ppermute | solution.py:422
  20.4 10.5 %collective-permute-start.7 = (f32[63,8,256]{2,1,0:T(8,128)S(1)}, f32[63,8,256]{2,1,0:T(8,128)S(1)}, u32[]{:S(2)}, u32[]{:S(2)}) collective-permute-start(f32[63,8,256]{2,1,0:T(8,128)S(1)} %collective-permute-done.refs_2_), channel_id=1, source_target_pairs={{0,1},{1,0},{2,3},{3,2},{4,5},{5,4},{6,7},{7,6},{8,9},{9,8},{10,11... | collective-permute-start | bytes 1548296 | tf_op jit(solution)/shard_map/ppermute | solution.py:422
  24.8 6.2 %collective-permute-start.8 = (f32[63,8,256]{2,1,0:T(8,128)S(1)}, f32[63,8,256]{2,1,0:T(8,128)}, u32[]{:S(2)}, u32[]{:S(2)}) collective-permute-start(f32[63,8,256]{2,1,0:T(8,128)S(1)} %collective-permute-done.1.refs_3_), channel_id=1, source_target_pairs={{0,1},{1,0},{2,3},{3,2},{4,5},{5,4},{6,7},{7,6},{8,9},{9,8},{10,11... | collective-permute-start | bytes 1548296 | tf_op jit(solution)/shard_map/ppermute | solution.py:422
  28.0 1.4 %collective-permute-start.11 = (f32[168,256]{1,0:T(8,128)S(1)}, f32[168,256]{1,0:T(8,128)S(1)}, u32[]{:S(2)}, u32[]{:S(2)}) collective-permute-start(f32[168,256]{1,0:T(8,128)S(1)} %collective-permute-done.4.refs_7_.refs_8_), channel_id=1, source_target_pairs={{0,1},{1,0},{2,3},{3,2},{4,5},{5,4},{6,7},{7,6},{8,9},{9,8},{10,11... | collective-permute-start | bytes 516104 | tf_op jit(solution)/shard_map/ppermute | solution.py:422
  28.0 2.3 %collective-permute-start.6 = (f32[2,2,3,4,8,256]{5,4,3,2,1,0:T(8,128)S(1)}, f32[2,2,3,4,8,256]{5,4,3,2,1,0:T(8,128)}, u32[]{:S(2)}, u32[]{:S(2)}) collective-permute-start(f32[2,2,3,4,8,256]{5,4,3,2,1,0:T(8,128)S(1)} %copy-done.1), channel_id=1, source_target_pairs={{0,1},{1,0},{2,3},{3,2},{4,5},{5,4},{6,7},{7,6},{8,9},{9,8},{10,11... | collective-permute-start | bytes 1179656 | tf_op jit(solution)/shard_map/ppermute | solution.py:422
  28.5 2.1 %collective-permute-start.5 = (f32[2,2,3,4,8,256]{5,4,3,2,1,0:T(8,128)S(1)}, f32[2,2,3,4,8,256]{5,4,3,2,1,0:T(8,128)}, u32[]{:S(2)}, u32[]{:S(2)}) collective-permute-start(f32[2,2,3,4,8,256]{5,4,3,2,1,0:T(8,128)S(1)} %copy-done), channel_id=1, source_target_pairs={{0,1},{1,0},{2,3},{3,2},{4,5},{5,4},{6,7},{7,6},{8,9},{9,8},{10,11... | collective-permute-start | bytes 1179656 | tf_op jit(solution)/shard_map/ppermute | solution.py:422
  29.4 1.5 %collective-permute-start.9 = (f32[256,256]{1,0:T(8,128)S(1)}, f32[256,256]{1,0:T(8,128)S(1)}, u32[]{:S(2)}, u32[]{:S(2)}) collective-permute-start(f32[256,256]{1,0:T(8,128)S(1)} %collective-permute-done.2.refs_4_.refs_5_), channel_id=1, source_target_pairs={{0,1},{1,0},{2,3},{3,2},{4,5},{5,4},{6,7},{7,6},{8,9},{9,8},{10,11... | collective-permute-start | bytes 786440 | tf_op jit(solution)/shard_map/ppermute | solution.py:422
  30.9 0.8 %copy-start.2 = (f32[4,8,256]{2,1,0:T(8,128)S(1)}, f32[4,8,256]{2,1,0:T(8,128)}, u32[]{:S(2)}) copy-start(f32[4,8,256]{2,1,0:T(8,128)} %eps_ref.3) | copy-start | bytes 98308
  31.7 0.7 %copy-start.3 = (s32[1,2]{1,0:T(1,128)S(1)}, s32[1,2]{1,0:T(1,128)}, u32[]{:S(2)}) copy-start(s32[1,2]{1,0:T(1,128)} %tiles_ref.3) | copy-start | bytes 28
  32.3 0.7 %copy-start.4 = (f32[4]{0:T(128)S(1)}, f32[4]{0:T(128)}, u32[]{:S(2)}) copy-start(f32[4]{0:T(128)} %freq_ref.1) | copy-start | bytes 52
  33.0 0.7 %copy-start.5 = (s32[3]{0:T(128)S(1)}, s32[3]{0:T(128)}, u32[]{:S(2)}) copy-start(s32[3]{0:T(128)} %pml_ref.1) | copy-start | bytes 40

commit v2 on v0

v2 whole, which is shorter than its diff:
```python
import functools

import jax
import jax.numpy as jnp
from jax import lax
from jax.experimental import pallas as pl
from jax.experimental.pallas import tpu as pltpu
from jax.sharding import PartitionSpec as P

ITERS = 3
TILE = 4
DEEP = ITERS
NEAR = ITERS - 1
LANES = 128
SUBS = 8

kerr_coef = 4.0
sigma_peak = 8.0

VMEM = pl.BlockSpec(memory_space=pltpu.VMEM)
SMEM = pl.BlockSpec(memory_space=pltpu.SMEM)
ANY = pl.BlockSpec(memory_space=pl.ANY)


class Sizes:
    def __init__(self, owned, cells, counts):
        self.owned = owned
        self.cx, self.cy, self.cz = cells
        self.gx, self.gy, self.ha = counts
        self.harmonics = owned * self.ha
        self.halves = self.cz // LANES
        self.wide = self.cx + 2 * DEEP
        self.rows = self.cy + 2 * DEEP + 2
        self.kinds = [(h, r, c) for h in range(owned) for r in range(2) for c in range(3)]
        self.colours = (0,) if self.gy == 2 else (0, 1)
        self.x_tiles = len(self.kinds) * (DEEP + NEAR) + DEEP
        whole = [(x, DEEP) for x in range(self.cx)]
        self.side = self.groups(whole, [(x, NEAR) for x in range(self.cx)])
        anti = [(d, DEEP) for d in range(DEEP)]
        self.anti = self.groups(anti, [(d, NEAR) for d in range(NEAR)])
        main = [(d, DEEP - 1 - d) for d in range(DEEP - 1)]
        self.main = self.groups(main, [(d, NEAR - 1 - d) for d in range(NEAR - 1)])

    def groups(self, deep, near):
        listed, at = [], SUBS
        for field, planes in ((0, deep), (1, near)):
            for kind in self.kinds:
                for plane, depth in planes:
                    listed.append((field, kind, plane, depth, at))
                    at += depth
        for plane, depth in deep:
            listed.append((2, None, plane, depth, at))
            at += depth
        return listed

    def length(self, groups):
        last = groups[-1]
        return (last[4] + SUBS + SUBS - 1) // SUBS * SUBS


def half(z):
    return slice(z * LANES, (z + 1) * LANES)


def tile_mask(tiles_ref, plane, rows):
    place = lax.broadcasted_iota(jnp.int32, (rows, LANES), 0) // TILE
    mask = jnp.zeros((rows, LANES), jnp.float32)
    for col in range(rows // TILE):
        cell = tiles_ref[plane // TILE, col].astype(jnp.float32)
        mask = jnp.where(place == col, cell, mask)
    return mask


def plane_mask(tiles_ref, plane, sz):
    mask = tile_mask(tiles_ref, 0, sz.cy)
    for x in range(TILE, sz.cx, TILE):
        mask = jnp.where(plane >= x, tile_mask(tiles_ref, x, sz.cy), mask)
    return kerr_coef * mask


def x_is_high(colour):
    return lax.rem(lax.axis_index("gx") + colour, 2) == 0


def y_is_high(colour):
    return lax.rem(lax.axis_index("gy") + colour, 2) == 0


def pack_x_kernel(sz, src_ref, fwd_ref, eps_ref, tiles_ref, even_ref, odd_ref):
    for colour, ref in ((0, even_ref), (1, odd_ref)):
        high = x_is_high(colour)
        deep = jnp.where(high, sz.cx - DEEP, 0)
        near = jnp.where(high, sz.cx - NEAR, 0)
        at = 0
        for h, r, c in sz.kinds:
            for d in range(DEEP):
                ref[at] = src_ref[h, r, c, deep + d]
                at += 1
        masks = [plane_mask(tiles_ref, near + d, sz) for d in range(NEAR)]
        for h, r, c in sz.kinds:
            for d in range(NEAR):
                for z in range(sz.halves):
                    ref[at, :, half(z)] = fwd_ref[h, r, c, near + d, :, half(z)] * masks[d]
                at += 1
        for d in range(DEEP):
            ref[at] = eps_ref[deep + d]
            at += 1


def pack_y_kernel(sz, src_ref, fwd_ref, eps_ref, tiles_ref, *out_refs):
    outs = iter(out_refs)

    def fill(ref, groups, top, plane_of):
        for field, kind, plane, depth, at in reversed(groups):
            x = plane_of(plane)
            shift = sz.cy - depth
            for z in range(sz.halves):
                if field == 2:
                    tile = eps_ref[x, :, half(z)]
                elif field == 0:
                    tile = src_ref[(*kind, x, slice(None), half(z))]
                else:
                    tile = fwd_ref[(*kind, x, slice(None), half(z))] * plane_mask(tiles_ref, x, sz)
                tile = jnp.where(top, tile, pltpu.roll(tile, shift, 0))
                ref[z, at - shift : at + depth] = tile

    for colour in sz.colours:
        top = y_is_high(colour)
        fill(next(outs), sz.side, top, lambda plane: plane)
        for groups, upper in ((sz.anti, jnp.logical_not(top)), (sz.main, top)):
            fill(
                next(outs),
                groups,
                top,
                lambda plane, upper=upper: jnp.where(upper, sz.cx - 1 - plane, plane),
            )


def sweep_kernel(sz, mix_hbm, freq_hbm, pml_hbm, tiles_hbm, eps_hbm, *refs):
    cx, cy, cz, halves = sz.cx, sz.cy, sz.cz, sz.halves
    wide, harmonics = sz.wide, sz.harmonics
    per_core = 4 + 3 * len(sz.colours)
    sides = [refs[per_core * s : per_core * (s + 1)] for s in range(sz.ha)]
    out_ref, grad_ref = refs[per_core * sz.ha : per_core * sz.ha + 2]
    scratch = refs[per_core * sz.ha + 2 :]
    base, first, second, fwd, invs, mags, eps_all = scratch[:7]
    mix_ref, freq_ref, pml_ref, tiles_ref, eps_ref, sems = scratch[7:]

    copies = [
        pltpu.make_async_copy(source, target, sems.at[i])
        for i, (source, target) in enumerate(
            (
                (mix_hbm, mix_ref),
                (freq_hbm, freq_ref),
                (pml_hbm, pml_ref),
                (tiles_hbm, tiles_ref),
                (eps_hbm, eps_ref),
            )
        )
    ]
    for copy in copies:
        copy.start()

    at_x, at_y, at_h = lax.axis_index("gx"), lax.axis_index("gy"), lax.axis_index("ha")
    start = at_h * sz.owned

    def from_own(index):
        return lax.rem(index - start + harmonics, harmonics)

    def globally(position):
        return lax.rem(position + start, harmonics)

    nothing = jnp.zeros((DEEP, LANES), jnp.float32)
    for g in range(harmonics):
        for r in range(2):
            for z in range(halves):
                for c in range(3):
                    for x in range(wide):
                        base[g, r, c, x, z, :DEEP] = nothing
                        base[g, r, c, x, z, DEEP + cy : DEEP + cy + DEEP] = nothing
                    for x in range(wide - 2):
                        fwd[g, r, c, x, z, :DEEP] = nothing
                        fwd[g, r, c, x, z, DEEP + cy : DEEP + cy + DEEP] = nothing
    for x in range(wide):
        for z in range(halves):
            eps_all[x, z] = jnp.zeros((sz.rows, LANES), jnp.float32)

    for copy in copies:
        copy.wait()

    squared = [freq_ref[globally(h)] * freq_ref[globally(h)] for h in range(harmonics)]
    lane = lax.broadcasted_iota(jnp.int32, (SUBS, LANES), 1)
    sub = lax.broadcasted_iota(jnp.int32, (SUBS, LANES), 0)

    def x_start(colour, depth):
        return jnp.where(x_is_high(colour), DEEP + cx, DEEP - depth)

    def y_spots(colour, corner=None):
        high_y = y_is_high(colour)
        if corner is None:
            plane_of = lambda plane: DEEP + plane
        else:
            high_x = jnp.logical_not(high_y) if corner == "anti" else high_y
            plane_of = lambda plane: jnp.where(high_x, DEEP + cx + plane, DEEP - 1 - plane)
        row_of = lambda depth: jnp.where(high_y, DEEP + cy, DEEP - depth)
        return plane_of, row_of

    def row_buffers(side):
        buffers = side[4:]
        for i, colour in enumerate(sz.colours):
            yield buffers[3 * i], sz.side, y_spots(colour)
            yield buffers[3 * i + 1], sz.anti, y_spots(colour, "anti")
            yield buffers[3 * i + 2], sz.main, y_spots(colour, "main")

    count = len(sz.kinds)
    for colour in (0, 1):
        buffer, x0 = sides[0][2 + colour], x_start(colour, DEEP)
        for d in range(DEEP):
            for z in range(halves):
                eps_all[x0 + d, z, DEEP : DEEP + cy] = buffer[count * (DEEP + NEAR) + d, :, half(z)]
    for x in range(cx):
        for z in range(halves):
            eps_all[DEEP + x, z, DEEP : DEEP + cy] = eps_ref[x, :, half(z)]
    for buffer, groups, (plane_of, row_of) in row_buffers(sides[0]):
        for field, kind, plane, depth, at in groups:
            if field == 2:
                for z in range(halves):
                    eps_all[plane_of(plane), z, pl.ds(row_of(depth), depth)] = buffer[
                        z, at : at + depth
                    ]

    def keep_rows(row):
        place = sub + (row - DEEP) + at_y * cy
        return (place >= 0) & (place < cy * sz.gy)

    def keep_plane(x):
        place = x - DEEP + at_x * cx
        return (place >= 0) & (place < cx * sz.gx)

    def scales(x, _):
        inside = jnp.where(keep_plane(x), 1.0, 0.0)
        for row in (0, SUBS):
            keep = jnp.where(keep_rows(row), inside, 0.0)
            for z in range(halves):
                eps = eps_all[x, z, row : row + SUBS]
                for h in range(harmonics):
                    invs[h, x, z, row : row + SUBS] = keep / (10.0 + squared[h] * eps)
        return 0

    lax.fori_loop(0, wide, scales, 0)

    masks = [kerr_coef * tile_mask(tiles_ref, x, cy) for x in range(cx)]
    inner = slice(DEEP, DEEP + cy)
    for s, side in enumerate(sides):
        own_src, own_fwd = side[:2]
        for n, kind in enumerate(sz.kinds):
            h, r, c = kind
            g = s * sz.owned + h
            for z in range(halves):
                for x in range(cx):
                    base[g, r, c, DEEP + x, z, inner] = (
                        own_src[h, r, c, x, :, half(z)] * invs[g, DEEP + x, z, inner]
                    )
                    fwd[g, r, c, NEAR + x, z, inner] = own_fwd[h, r, c, x, :, half(z)] * masks[x]
                for colour in (0, 1):
                    buffer = side[2 + colour]
                    x0, x1 = x_start(colour, DEEP), x_start(colour, NEAR) - 1
                    for d in range(DEEP):
                        base[g, r, c, x0 + d, z, inner] = (
                            buffer[n * DEEP + d, :, half(z)] * invs[g, x0 + d, z, inner]
                        )
                    for d in range(NEAR):
                        fwd[g, r, c, x1 + d, z, inner] = buffer[
                            count * DEEP + n * NEAR + d, :, half(z)
                        ]
        for buffer, groups, (plane_of, row_of) in row_buffers(side):
            for field, kind, plane, depth, at in groups:
                if field == 2:
                    continue
                h, r, c = kind
                g = s * sz.owned + h
                x, rows = plane_of(plane), pl.ds(row_of(depth), depth)
                for z in range(halves):
                    got = buffer[z, at : at + depth]
                    if field == 0:
                        base[g, r, c, x, z, rows] = got * invs[g, x, z, rows]
                    else:
                        fwd[g, r, c, x - 1, z, rows] = got

    def profile(width, place, cells):
        reach = jnp.maximum(jnp.maximum(width - place, place - (cells - 1 - width)), 0)
        return (reach.astype(jnp.float32) / jnp.full(reach.shape, width).astype(jnp.float32)) ** 2

    sigma_z = [profile(pml_ref[2], lane + z * LANES, cz) for z in range(halves)]

    def z_ahead(parts):
        turned = [pltpu.roll(v, LANES - 1, 1) for v in parts]
        following = turned[1:] + [0.0]
        return [jnp.where(lane == LANES - 1, f, t) for t, f in zip(turned, following)]

    def z_behind(parts):
        turned = [pltpu.roll(v, 1, 1) for v in parts]
        previous = [0.0] + turned[:-1]
        return [jnp.where(lane == 0, p, t) for t, p in zip(turned, previous)]

    pairs = [
        (from_own(mix_ref[p, 0, globally(h)]), from_own(mix_ref[p, 1, globally(h)]))
        for h in range(harmonics)
        for p in range(mix_ref.shape[0])
    ]
    mixes = mix_ref.shape[0]
    zs = range(halves)

    def sweep(k, v_ref, store):
        lo, hi = k + 1, wide - 1 - k
        top = DEEP + cy + NEAR - k
        out_rows = sorted({k + 1, top - SUBS})
        mag_rows = sorted({k, top - SUBS})
        sigma_y = {
            row: profile(pml_ref[1], sub + (row - DEEP) + at_y * cy, cy * sz.gy) for row in out_rows
        }

        def write_mags(x, comps):
            slot = lax.rem(x, 2)
            inside = x - DEEP + at_x * cx >= 0
            for row in mag_rows:
                mask = (sub + (row - DEEP) + at_y * cy >= 0) & inside
                for g in range(harmonics):
                    for r in range(2):
                        here = [
                            [v_ref[g, r, c, x, z, row : row + SUBS] for z in zs] for c in range(3)
                        ]
                        next_y, next_z = [
                            [v_ref[g, r, c, x + 1, z, row : row + SUBS] for z in zs] for c in (1, 2)
                        ]
                        above_x, above_z = [
                            [v_ref[g, r, c, x, z, row + 1 : row + 1 + SUBS] for z in zs]
                            for c in (0, 2)
                        ]
                        fx, fy, fz = here
                        after_x = z_ahead(fx)
                        found = {}
                        if 0 in comps:
                            after_y = z_ahead(fy)
                            found[0] = [
                                (above_z[z] - fz[z]) - (after_y[z] - fy[z]) for z in zs
                            ]
                        found[1] = [(after_x[z] - fx[z]) - (next_z[z] - fz[z]) for z in zs]
                        found[2] = [(next_y[z] - fy[z]) - (above_x[z] - fx[z]) for z in zs]
                        for c, parts in found.items():
                            for z in zs:
                                pltpu.store(
                                    mags.at[slot, g, r, c, z, row : row + SUBS],
                                    parts[z],
                                    mask=mask,
                                )

        for slot in range(2):
            for g in range(harmonics):
                for r in range(2):
                    for c in range(3):
                        for z in zs:
                            mags[slot, g, r, c, z] = jnp.zeros((sz.rows, LANES), jnp.float32)
        write_mags(k, (1, 2))

        def body(x, _):
            write_mags(x, (0, 1, 2))
            slot, past = lax.rem(x, 2), lax.rem(x + 1, 2)
            twice = jnp.where(keep_plane(x), 2.0, 0.0)
            place = jnp.full((SUBS, LANES), x - DEEP + at_x * cx)
            sigma_x = profile(pml_ref[0], place, cx * sz.gx)
            for row in out_rows:
                span, below = slice(row, row + SUBS), slice(row - 1, row - 1 + SUBS)
                double = jnp.where(keep_rows(row), twice, 0.0)
                sigma = [sigma_peak * (sigma_x + sigma_y[row] + sigma_z[z]) for z in zs]
                for h in range(harmonics):
                    curls = []
                    for r in range(2):
                        mag = [[mags[slot, h, r, c, z, span] for z in zs] for c in range(3)]
                        low_x, low_z = [
                            [mags[slot, h, r, c, z, below] for z in zs] for c in (0, 2)
                        ]
                        past_y, past_z = [
                            [mags[past, h, r, c, z, span] for z in zs] for c in (1, 2)
                        ]
                        before_x, before_y = z_behind(mag[0]), z_behind(mag[1])
                        curls.append(
                            [
                                [
                                    (mag[2][z] - low_z[z]) - (mag[1][z] - before_y[z]),
                                    (mag[0][z] - before_x[z]) - (mag[2][z] - past_z[z]),
                                    (mag[1][z] - past_y[z]) - (mag[0][z] - low_x[z]),
                                ]
                                for z in zs
                            ]
                        )
                    for z in zs:
                        inv = invs[h, x, z, span]
                        slope = double - 10.0 * inv
                        absorb = squared[h] * sigma[z]
                        for c in range(3):
                            real = imag = None
                            for p in range(mixes):
                                a, b = pairs[h * mixes + p]
                                fr, fi = [fwd[a, r, c, x - 1, z, span] for r in range(2)]
                                vr, vi = [v_ref[b, r, c, x, z, span] for r in range(2)]
                                one, two = fr * vr - fi * vi, fr * vi + fi * vr
                                real = one if real is None else real + one
                                imag = two if imag is None else imag + two
                            vr, vi = [v_ref[h, r, c, x, z, span] for r in range(2)]
                            new_r = (
                                base[h, 0, c, x, z, span]
                                + vr * slope
                                + inv * (squared[h] * real - absorb * vi - curls[0][z][c])
                            )
                            new_i = (
                                base[h, 1, c, x, z, span]
                                + vi * slope
                                + inv * (squared[h] * imag + absorb * vr - curls[1][z][c])
                            )
                            store(h, c, x, z, span, new_r, new_i)
            return 0

        lax.fori_loop(lo, hi, body, 0)

    def store_in(ref):
        def store(h, c, x, z, span, new_r, new_i):
            ref[h, 0, c, x, z, span] = new_r
            ref[h, 1, c, x, z, span] = new_i

        return store

    sums = {}

    def store_out(h, c, x, z, span, new_r, new_i):
        if h < sz.owned:
            out_ref[h, 0, c, x - DEEP, :, half(z)] = new_r
            out_ref[h, 1, c, x - DEEP, :, half(z)] = new_i
        term = (squared[h] / kerr_coef) * (
            new_r * fwd[h, 0, c, x - 1, z, span] - new_i * fwd[h, 1, c, x - 1, z, span]
        )
        if h == 0 and c == 0:
            sums[z] = term
        else:
            sums[z] = sums[z] + term
        if h == harmonics - 1 and c == 2:
            grad_ref[x - DEEP, :, half(z)] = sums[z]

    sweep(0, base, store_in(first))
    sweep(1, first, store_in(second))
    sweep(2, second, store_out)


def swaps(count_x, count_y, partner):
    sends = []
    for x in range(count_x):
        for y in range(count_y):
            to_x, to_y = partner(x, y)
            if 0 <= to_x < count_x and 0 <= to_y < count_y:
                sends.append((x * count_y + y, to_x * count_y + to_y))
    return sends


def shards(
    forward_field, adjoint_source, permittivity, frequency, design_tiles, mix_pairs, pml_width
):
    counts = tuple(lax.axis_size(name) for name in ("gx", "gy", "ha"))
    sz = Sizes(forward_field.shape[0], permittivity.shape, counts)
    f32 = jnp.float32
    x_buf = jax.ShapeDtypeStruct((sz.x_tiles, sz.cy, sz.cz), f32)
    even, odd = pl.pallas_call(
        functools.partial(pack_x_kernel, sz),
        out_shape=[x_buf, x_buf],
        in_specs=[VMEM, VMEM, VMEM, SMEM],
        out_specs=[VMEM, VMEM],
        name="pack_x",
    )(adjoint_source, forward_field, permittivity, design_tiles)
    row_bufs = [
        jax.ShapeDtypeStruct((sz.halves, sz.length(groups), LANES), f32)
        for groups in (sz.side, sz.anti, sz.main)
    ] * len(sz.colours)
    packed = pl.pallas_call(
        functools.partial(pack_y_kernel, sz),
        out_shape=row_bufs,
        in_specs=[VMEM, VMEM, VMEM, SMEM],
        out_specs=[VMEM] * len(row_bufs),
        name="pack_y",
    )(adjoint_source, forward_field, permittivity, design_tiles)

    def send(buffer, partner):
        return lax.ppermute(buffer, ("gx", "gy"), swaps(sz.gx, sz.gy, partner))

    def step(place, colour):
        return 1 if (place + colour) % 2 == 0 else -1

    got = [
        send(even, lambda x, y: (x + step(x, 0), y)),
        send(odd, lambda x, y: (x + step(x, 1), y)),
    ]
    for i, colour in enumerate(sz.colours):
        got += [
            send(packed[3 * i], lambda x, y: (x, y + step(y, colour))),
            send(packed[3 * i + 1], lambda x, y: (x - step(y, colour), y + step(y, colour))),
            send(packed[3 * i + 2], lambda x, y: (x + step(y, colour), y + step(y, colour))),
        ]

    own = [adjoint_source, forward_field] + got
    flip = [(i, sz.ha - 1 - i) for i in range(sz.ha)]
    other = [lax.ppermute(buffer, "ha", flip) for buffer in own]

    def field(planes):
        return pltpu.VMEM((sz.harmonics, 2, 3, planes, sz.halves, sz.rows, LANES), f32)

    mix_by_pair = jnp.transpose(mix_pairs, (1, 2, 0))
    adjoint, gradient = pl.pallas_call(
        functools.partial(sweep_kernel, sz),
        out_shape=[
            jax.ShapeDtypeStruct(adjoint_source.shape, f32),
            jax.ShapeDtypeStruct(permittivity.shape, f32),
        ],
        in_specs=[ANY] * 5 + [VMEM] * (2 * len(own)),
        out_specs=[VMEM, VMEM],
        scratch_shapes=[
            field(sz.wide),
            field(sz.wide),
            field(sz.wide),
            field(sz.wide - 2),
            pltpu.VMEM((sz.harmonics, sz.wide, sz.halves, sz.rows, LANES), f32),
            pltpu.VMEM((2, sz.harmonics, 2, 3, sz.halves, sz.rows, LANES), f32),
            pltpu.VMEM((sz.wide, sz.halves, sz.rows, LANES), f32),
            pltpu.SMEM(mix_by_pair.shape, jnp.int32),
            pltpu.SMEM(frequency.shape, f32),
            pltpu.SMEM(pml_width.shape, jnp.int32),
            pltpu.SMEM(design_tiles.shape, jnp.int32),
            pltpu.VMEM(permittivity.shape, f32),
            pltpu.SemaphoreType.DMA((5,)),
        ],
        compiler_params=pltpu.CompilerParams(vmem_limit_bytes=32 * 1024 * 1024),
        name="sweeps",
    )(mix_by_pair, frequency, pml_width, design_tiles, permittivity, *own, *other)
    return (adjoint, gradient)


def solution(mesh):
    return jax.shard_map(
        shards,
        mesh=mesh,
        in_specs=(
            P("ha", None, None, ("cand", "gx"), "gy", None),
            P("ha", None, None, ("cand", "gx"), "gy", None),
            P(("cand", "gx"), "gy", None),
            P(),
            P(("cand", "gx"), "gy"),
            P(),
            P(),
        ),
        out_specs=(P("ha", None, None, ("cand", "gx"), "gy", None), P(("cand", "gx"), "gy", None)),
        check_vma=False,
    )
```

time: 95.4 us -> 40.6 us (0.43)
  the two profiles are of different devices: /device:TPU:0 before, /device:TPU:17 now
where the time goes in v2:
time: 40.6 us; the launch traced here: 40.4 us
  starting transfers between devices  19.1 us (47%)
  Pallas kernels  16.4 us (40%)
  waiting for transfers between devices  4.16 us (10%)
  between operations  0.73 us (2%)
    pallas_call x1, Pallas kernels, shards(): pl.pallas_call(functools.partial(sweep_kernel, sz), out_shape=[jax.ShapeD...  12.2 us
    ppermute x5, starting transfers between devices, send(): return lax.ppermute(buffer, ('gx', 'gy'), swaps(sz.gx, sz.gy, partner))  9.92 us
    ppermute x7, starting transfers between devices, shards(): other = [lax.ppermute(buffer, 'ha', flip) for buffer in own]  9.15 us
    ppermute x5, waiting for transfers between devices, send(): return lax.ppermute(buffer, ('gx', 'gy'), swaps(sz.gx, sz.gy, partner))  2.35 us
    pallas_call x1, Pallas kernels, shards(): pl.pallas_call(functools.partial(pack_x_kernel, sz), out_shape=[x_buf, x_...  2.18 us
    pallas_call x1, Pallas kernels, shards(): pl.pallas_call(functools.partial(pack_y_kernel, sz), out_shape=row_bufs,...  2.06 us
    ppermute x7, waiting for transfers between devices, shards(): other = [lax.ppermute(buffer, 'ha', flip) for buffer in own]  1.8 us
  transfers between devices with their start and end apart: 12, of which 7 were waited for; matrix products, arithmetic and copies ran while one was open for 0% of the time, Pallas kernels for 5%

profile of v2, /device:TPU:17, one launch (start us, length us, event | category | flops | bytes accessed | tf_op | source)
XLA Modules:
  0.0 40.4 jit_solution(15417208689469761621)
XLA Ops:
  0.6 2.2 %pack_x.1 = (f32[63,8,256]{2,1,0:T(8,128)}, f32[63,8,256]{2,1,0:T(8,128)}) custom-call(f32[2,2,3,4,8,256]{5,4,3,2,1,0:T(8,128)} %refs_0_.1, f32[2,2,3,4,8,256]{5,4,3,2,1,0:T(8,128)} %refs_1_.1, f32[4,8,256]{2,1,0:T(8,128)} %eps_hbm.1, s32[1,2]{1,0:T(1,128)} %tiles_hbm.1), custom_call_target="tpu_custom_call" | custom-call | tf_op jit(solution)/shard_map/pack_x/pallas_call | solution.py:471
  2.8 1.3 %collective-permute-start = (f32[63,8,256]{2,1,0:T(8,128)}, f32[63,8,256]{2,1,0:T(8,128)S(1)}, u32[]{:S(2)}, u32[]{:S(2)}) collective-permute-start(f32[63,8,256]{2,1,0:T(8,128)} %get-tuple-element.7), channel_id=1, source_target_pairs={{0,4},{2,6},{4,0},{6,2},{8,12},{10,14},{12,8},{14,10},{1,5},{3,7},... | collective-permute-start | bytes 1548296 | tf_op jit(solution)/shard_map/ppermute | solution.py:491
  4.1 2.0 %collective-permute-start.1 = (f32[63,8,256]{2,1,0:T(8,128)}, f32[63,8,256]{2,1,0:T(8,128)S(1)}, u32[]{:S(2)}, u32[]{:S(2)}) collective-permute-start(f32[63,8,256]{2,1,0:T(8,128)} %get-tuple-element.8), channel_id=1, source_target_pairs={{4,8},{6,10},{8,4},{10,6},{5,9},{7,11},{9,5},{11,7},{20,24},{22,26... | collective-permute-start | bytes 1548296 | tf_op jit(solution)/shard_map/ppermute | solution.py:491
  6.2 2.1 %pack_y.1 = (f32[2,272,128]{2,1,0:T(8,128)}, f32[2,184,128]{2,1,0:T(8,128)}, f32[2,72,128]{2,1,0:T(8,128)}) custom-call(f32[2,2,3,4,8,256]{5,4,3,2,1,0:T(8,128)} %refs_0_.1, f32[2,2,3,4,8,256]{5,4,3,2,1,0:T(8,128)} %refs_1_.1, f32[4,8,256]{2,1,0:T(8,128)} %eps_hbm.1, s32[1,2]{1,0:T(1,128)} %tiles_hbm.1), custom_call_target="tpu_custom_call" | custom-call | tf_op jit(solution)/shard_map/pack_y/pallas_call | solution.py:482
  8.2 1.2 %collective-permute-start.2 = (f32[2,272,128]{2,1,0:T(8,128)}, f32[2,272,128]{2,1,0:T(8,128)S(1)}, u32[]{:S(2)}, u32[]{:S(2)}) collective-permute-start(f32[2,272,128]{2,1,0:T(8,128)} %get-tuple-element.9), channel_id=1, source_target_pairs={{0,2},{2,0},{4,6},{6,4},{8,10},{10,8},{12,14},{14,12},{1,3},{3,1},... | collective-permute-start | bytes 835592 | tf_op jit(solution)/shard_map/ppermute | solution.py:491
  9.4 3.3 %collective-permute-start.3 = (f32[2,184,128]{2,1,0:T(8,128)}, f32[2,184,128]{2,1,0:T(8,128)S(1)}, u32[]{:S(2)}, u32[]{:S(2)}) collective-permute-start(f32[2,184,128]{2,1,0:T(8,128)} %get-tuple-element.10), channel_id=1, source_target_pairs={{2,4},{4,2},{6,8},{8,6},{10,12},{12,10},{3,5},{5,3},{7,9},{9,7},{1... | collective-permute-start | bytes 565256 | tf_op jit(solution)/shard_map/ppermute | solution.py:491
  12.8 0.0 copy-start.3
  12.8 0.0 copy-start.5
  12.8 0.0 copy-start.6
  12.8 2.1 %collective-permute-start.4 = (f32[2,72,128]{2,1,0:T(8,128)}, f32[2,72,128]{2,1,0:T(8,128)S(1)}, u32[]{:S(2)}, u32[]{:S(2)}) collective-permute-start(f32[2,72,128]{2,1,0:T(8,128)} %get-tuple-element.11), channel_id=1, source_target_pairs={{0,6},{4,10},{6,0},{8,14},{10,4},{14,8},{1,7},{5,11},{7,1},{9,15},... | collective-permute-start | bytes 221192 | tf_op jit(solution)/shard_map/ppermute | solution.py:491
  14.9 0.8 %collective-permute-done.refs_2_ = f32[63,8,256]{2,1,0:T(8,128)S(1)} collective-permute-done((f32[63,8,256]{2,1,0:T(8,128)}, f32[63,8,256]{2,1,0:T(8,128)S(1)}, u32[]{:S(2)}, u32[]{:S(2)}) %collective-permute-start) | collective-permute-done | bytes 516128 | tf_op jit(solution)/shard_map/ppermute | solution.py:491
  15.7 2.7 %collective-permute-start.7 = (f32[63,8,256]{2,1,0:T(8,128)S(1)}, f32[63,8,256]{2,1,0:T(8,128)S(1)}, u32[]{:S(2)}, u32[]{:S(2)}) collective-permute-start(f32[63,8,256]{2,1,0:T(8,128)S(1)} %collective-permute-done.refs_2_), channel_id=1, source_target_pairs={{0,1},{1,0},{2,3},{3,2},{4,5},{5,4},{6,7},{7,6},{8,9},{9,8},{10,11... | collective-permute-start | bytes 1548296 | tf_op jit(solution)/shard_map/ppermute | solution.py:509
  18.3 0.4 collective-permute-done.1.refs_3_
  18.7 2.6 %collective-permute-start.8 = (f32[63,8,256]{2,1,0:T(8,128)S(1)}, f32[63,8,256]{2,1,0:T(8,128)S(1)}, u32[]{:S(2)}, u32[]{:S(2)}) collective-permute-start(f32[63,8,256]{2,1,0:T(8,128)S(1)} %collective-permute-done.1.refs_3_), channel_id=1, source_target_pairs={{0,1},{1,0},{2,3},{3,2},{4,5},{5,4},{6,7},{7,6},{8,9},{9,8},{10,11... | collective-permute-start | bytes 1548296 | tf_op jit(solution)/shard_map/ppermute | solution.py:509
  21.3 0.0 collective-permute-done.4.refs_6_
  21.3 1.2 %collective-permute-start.11 = (f32[2,72,128]{2,1,0:T(8,128)S(1)}, f32[2,72,128]{2,1,0:T(8,128)S(1)}, u32[]{:S(2)}, u32[]{:S(2)}) collective-permute-start(f32[2,72,128]{2,1,0:T(8,128)S(1)} %collective-permute-done.4.refs_6_), channel_id=1, source_target_pairs={{0,1},{1,0},{2,3},{3,2},{4,5},{5,4},{6,7},{7,6},{8,9},{9,8},{10,11... | collective-permute-start | bytes 221192 | tf_op jit(solution)/shard_map/ppermute | solution.py:509
  22.5 1.2 %collective-permute-done.3.refs_5_ = f32[2,184,128]{2,1,0:T(8,128)S(1)} collective-permute-done((f32[2,184,128]{2,1,0:T(8,128)}, f32[2,184,128]{2,1,0:T(8,128)S(1)}, u32[]{:S(2)}, u32[]{:S(2)}) %collective-permute-start.3) | collective-permute-done | bytes 188448 | tf_op jit(solution)/shard_map/ppermute | solution.py:491
  23.7 1.8 %collective-permute-start.10 = (f32[2,184,128]{2,1,0:T(8,128)S(1)}, f32[2,184,128]{2,1,0:T(8,128)S(1)}, u32[]{:S(2)}, u32[]{:S(2)}) collective-permute-start(f32[2,184,128]{2,1,0:T(8,128)S(1)} %collective-permute-done.3.refs_5_), channel_id=1, source_target_pairs={{0,1},{1,0},{2,3},{3,2},{4,5},{5,4},{6,7},{7,6},{8,9},{9,8},{10,11... | collective-permute-start | bytes 565256 | tf_op jit(solution)/shard_map/ppermute | solution.py:509
  25.5 0.0 collective-permute-done.11.refs_13_
  25.5 0.0 copy-done.1
  25.5 0.1 collective-permute-start.6
  25.6 0.0 collective-permute-done.2.refs_4_
  25.6 0.0 copy-done
  25.6 0.4 %collective-permute-start.5 = (f32[2,2,3,4,8,256]{5,4,3,2,1,0:T(8,128)S(1)}, f32[2,2,3,4,8,256]{5,4,3,2,1,0:T(8,128)S(1)}, u32[]{:S(2)}, u32[]{:S(2)}) collective-permute-start(f32[2,2,3,4,8,256]{5,4,3,2,1,0:T(8,128)S(1)} %copy-done), channel_id=1, source_target_pairs={{0,1},{1,0},{2,3},{3,2},{4,5},{5,4},{6,7},{7,6},{8,9},{9,8},{10,11... | collective-permute-start | bytes 1179656 | tf_op jit(solution)/shard_map/ppermute | solution.py:509
  26.0 0.5 %collective-permute-done.10.refs_12_ = f32[2,184,128]{2,1,0:T(8,128)S(1)} collective-permute-done((f32[2,184,128]{2,1,0:T(8,128)S(1)}, f32[2,184,128]{2,1,0:T(8,128)S(1)}, u32[]{:S(2)}, u32[]{:S(2)}) %collective-permute-start.10) | collective-permute-done | bytes 188448 | tf_op jit(solution)/shard_map/ppermute | solution.py:509
  26.5 0.4 collective-permute-start.9
  26.9 0.3 collective-permute-done.6.refs_8_
  27.2 0.6 %collective-permute-done.5.refs_7_ = f32[2,2,3,4,8,256]{5,4,3,2,1,0:T(8,128)S(1)} collective-permute-done((f32[2,2,3,4,8,256]{5,4,3,2,1,0:T(8,128)S(1)}, f32[2,2,3,4,8,256]{5,4,3,2,1,0:T(8,128)S(1)}, u32[]{:S(2)}, u32[]{:S(2)}) %collective-permute-start.5) | collective-permute-done | bytes 393248 | tf_op jit(solution)/shard_map/ppermute | solution.py:509
  27.8 0.4 collective-permute-done.9.refs_11_
  28.2 0.0 collective-permute-done.7.refs_9_
  28.2 0.0 collective-permute-done.8.refs_10_
  28.2 12.2 %sweeps.1 = (f32[2,2,3,4,8,256]{5,4,3,2,1,0:T(8,128)}, f32[4,8,256]{2,1,0:T(8,128)}) custom-call(s32[3,2,4]{2,1,0:T(2,128)S(1)} %bitcast.1, f32[4]{0:T(128)S(1)} %copy-done.5, s32[3]{0:T(128)S(1)} %copy-done.6, s32[1,2]{1,0:T(1,128)S(1)} %copy-done.3, f32[4,8,256]{2,1,0:T(8,128)S(1)} %copy-done.2, f32[2,2,3,4,8,256]{5,4,3,2,1,0:T(8,128)S(1)} %copy-done, ...), custom_call_target="tpu_custom_call" | custom-call | tf_op jit(solution)/shard_map/sweeps/pallas_call | solution.py:515
  (9 shorter events, 0.0 us)
Async XLA Ops:
  2.8 12.8 %collective-permute-start = (f32[63,8,256]{2,1,0:T(8,128)}, f32[63,8,256]{2,1,0:T(8,128)S(1)}, u32[]{:S(2)}, u32[]{:S(2)}) collective-permute-start(f32[63,8,256]{2,1,0:T(8,128)} %get-tuple-element.7), channel_id=1, source_target_pairs={{0,4},{2,6},{4,0},{6,2},{8,12},{10,14},{12,8},{14,10},{1,5},{3,7},... | collective-permute-start | bytes 1548296 | tf_op jit(solution)/shard_map/ppermute | solution.py:491
  4.1 21.4 %copy-start.1 = (f32[2,2,3,4,8,256]{5,4,3,2,1,0:T(8,128)S(1)}, f32[2,2,3,4,8,256]{5,4,3,2,1,0:T(8,128)}, u32[]{:S(2)}) copy-start(f32[2,2,3,4,8,256]{5,4,3,2,1,0:T(8,128)} %refs_1_.1) | copy-start | bytes 1179652
  4.1 21.5 %copy-start = (f32[2,2,3,4,8,256]{5,4,3,2,1,0:T(8,128)S(1)}, f32[2,2,3,4,8,256]{5,4,3,2,1,0:T(8,128)}, u32[]{:S(2)}) copy-start(f32[2,2,3,4,8,256]{5,4,3,2,1,0:T(8,128)} %refs_0_.1) | copy-start | bytes 1179652
  4.1 24.1 %copy-start.2 = (f32[4,8,256]{2,1,0:T(8,128)S(1)}, f32[4,8,256]{2,1,0:T(8,128)}, u32[]{:S(2)}) copy-start(f32[4,8,256]{2,1,0:T(8,128)} %eps_hbm.1) | copy-start | bytes 98308
  4.1 14.6 %collective-permute-start.1 = (f32[63,8,256]{2,1,0:T(8,128)}, f32[63,8,256]{2,1,0:T(8,128)S(1)}, u32[]{:S(2)}, u32[]{:S(2)}) collective-permute-start(f32[63,8,256]{2,1,0:T(8,128)} %get-tuple-element.8), channel_id=1, source_target_pairs={{4,8},{6,10},{8,4},{10,6},{5,9},{7,11},{9,5},{11,7},{20,24},{22,26... | collective-permute-start | bytes 1548296 | tf_op jit(solution)/shard_map/ppermute | solution.py:491
  8.2 20.0 %copy-start.4 = (s32[4,3,2]{0,2,1:T(2,128)S(1)}, s32[4,3,2]{0,2,1:T(2,128)}, u32[]{:S(2)}) copy-start(s32[4,3,2]{0,2,1:T(2,128)} %param.12) | copy-start | bytes 292
  8.2 17.3 %collective-permute-start.2 = (f32[2,272,128]{2,1,0:T(8,128)}, f32[2,272,128]{2,1,0:T(8,128)S(1)}, u32[]{:S(2)}, u32[]{:S(2)}) collective-permute-start(f32[2,272,128]{2,1,0:T(8,128)} %get-tuple-element.9), channel_id=1, source_target_pairs={{0,2},{2,0},{4,6},{6,4},{8,10},{10,8},{12,14},{14,12},{1,3},{3,1},... | collective-permute-start | bytes 835592 | tf_op jit(solution)/shard_map/ppermute | solution.py:491
  9.4 14.2 %collective-permute-start.3 = (f32[2,184,128]{2,1,0:T(8,128)}, f32[2,184,128]{2,1,0:T(8,128)S(1)}, u32[]{:S(2)}, u32[]{:S(2)}) collective-permute-start(f32[2,184,128]{2,1,0:T(8,128)} %get-tuple-element.10), channel_id=1, source_target_pairs={{2,4},{4,2},{6,8},{8,6},{10,12},{12,10},{3,5},{5,3},{7,9},{9,7},{1... | collective-permute-start | bytes 565256 | tf_op jit(solution)/shard_map/ppermute | solution.py:491
  12.8 15.4 %copy-start.3 = (s32[1,2]{1,0:T(1,128)S(1)}, s32[1,2]{1,0:T(1,128)}, u32[]{:S(2)}) copy-start(s32[1,2]{1,0:T(1,128)} %tiles_hbm.1) | copy-start | bytes 28
  12.8 15.4 %copy-start.5 = (f32[4]{0:T(128)S(1)}, f32[4]{0:T(128)}, u32[]{:S(2)}) copy-start(f32[4]{0:T(128)} %freq_hbm.1) | copy-start | bytes 52
  12.8 15.4 %copy-start.6 = (s32[3]{0:T(128)S(1)}, s32[3]{0:T(128)}, u32[]{:S(2)}) copy-start(s32[3]{0:T(128)} %pml_hbm.1) | copy-start | bytes 40
  12.8 8.5 %collective-permute-start.4 = (f32[2,72,128]{2,1,0:T(8,128)}, f32[2,72,128]{2,1,0:T(8,128)S(1)}, u32[]{:S(2)}, u32[]{:S(2)}) collective-permute-start(f32[2,72,128]{2,1,0:T(8,128)} %get-tuple-element.11), channel_id=1, source_target_pairs={{0,6},{4,10},{6,0},{8,14},{10,4},{14,8},{1,7},{5,11},{7,1},{9,15},... | collective-permute-start | bytes 221192 | tf_op jit(solution)/shard_map/ppermute | solution.py:491
  15.7 12.5 %collective-permute-start.7 = (f32[63,8,256]{2,1,0:T(8,128)S(1)}, f32[63,8,256]{2,1,0:T(8,128)S(1)}, u32[]{:S(2)}, u32[]{:S(2)}) collective-permute-start(f32[63,8,256]{2,1,0:T(8,128)S(1)} %collective-permute-done.refs_2_), channel_id=1, source_target_pairs={{0,1},{1,0},{2,3},{3,2},{4,5},{5,4},{6,7},{7,6},{8,9},{9,8},{10,11... | collective-permute-start | bytes 1548296 | tf_op jit(solution)/shard_map/ppermute | solution.py:509
  18.7 9.5 %collective-permute-start.8 = (f32[63,8,256]{2,1,0:T(8,128)S(1)}, f32[63,8,256]{2,1,0:T(8,128)S(1)}, u32[]{:S(2)}, u32[]{:S(2)}) collective-permute-start(f32[63,8,256]{2,1,0:T(8,128)S(1)} %collective-permute-done.1.refs_3_), channel_id=1, source_target_pairs={{0,1},{1,0},{2,3},{3,2},{4,5},{5,4},{6,7},{7,6},{8,9},{9,8},{10,11... | collective-permute-start | bytes 1548296 | tf_op jit(solution)/shard_map/ppermute | solution.py:509
  21.3 4.2 %collective-permute-start.11 = (f32[2,72,128]{2,1,0:T(8,128)S(1)}, f32[2,72,128]{2,1,0:T(8,128)S(1)}, u32[]{:S(2)}, u32[]{:S(2)}) collective-permute-start(f32[2,72,128]{2,1,0:T(8,128)S(1)} %collective-permute-done.4.refs_6_), channel_id=1, source_target_pairs={{0,1},{1,0},{2,3},{3,2},{4,5},{5,4},{6,7},{7,6},{8,9},{9,8},{10,11... | collective-permute-start | bytes 221192 | tf_op jit(solution)/shard_map/ppermute | solution.py:509
  23.7 2.9 %collective-permute-start.10 = (f32[2,184,128]{2,1,0:T(8,128)S(1)}, f32[2,184,128]{2,1,0:T(8,128)S(1)}, u32[]{:S(2)}, u32[]{:S(2)}) collective-permute-start(f32[2,184,128]{2,1,0:T(8,128)S(1)} %collective-permute-done.3.refs_5_), channel_id=1, source_target_pairs={{0,1},{1,0},{2,3},{3,2},{4,5},{5,4},{6,7},{7,6},{8,9},{9,8},{10,11... | collective-permute-start | bytes 565256 | tf_op jit(solution)/shard_map/ppermute | solution.py:509
  25.5 1.7 %collective-permute-start.6 = (f32[2,2,3,4,8,256]{5,4,3,2,1,0:T(8,128)S(1)}, f32[2,2,3,4,8,256]{5,4,3,2,1,0:T(8,128)S(1)}, u32[]{:S(2)}, u32[]{:S(2)}) collective-permute-start(f32[2,2,3,4,8,256]{5,4,3,2,1,0:T(8,128)S(1)} %copy-done.1), channel_id=1, source_target_pairs={{0,1},{1,0},{2,3},{3,2},{4,5},{5,4},{6,7},{7,6},{8,9},{9,8},{10,11... | collective-permute-start | bytes 1179656 | tf_op jit(solution)/shard_map/ppermute | solution.py:509
  25.6 2.2 %collective-permute-start.5 = (f32[2,2,3,4,8,256]{5,4,3,2,1,0:T(8,128)S(1)}, f32[2,2,3,4,8,256]{5,4,3,2,1,0:T(8,128)S(1)}, u32[]{:S(2)}, u32[]{:S(2)}) collective-permute-start(f32[2,2,3,4,8,256]{5,4,3,2,1,0:T(8,128)S(1)} %copy-done), channel_id=1, source_target_pairs={{0,1},{1,0},{2,3},{3,2},{4,5},{5,4},{6,7},{7,6},{8,9},{9,8},{10,11... | collective-permute-start | bytes 1179656 | tf_op jit(solution)/shard_map/ppermute | solution.py:509
  26.5 1.6 %collective-permute-start.9 = (f32[2,272,128]{2,1,0:T(8,128)S(1)}, f32[2,272,128]{2,1,0:T(8,128)S(1)}, u32[]{:S(2)}, u32[]{:S(2)}) collective-permute-start(f32[2,272,128]{2,1,0:T(8,128)S(1)} %collective-permute-done.2.refs_4_), channel_id=1, source_target_pairs={{0,1},{1,0},{2,3},{3,2},{4,5},{5,4},{6,7},{7,6},{8,9},{9,8},{10,11... | collective-permute-start | bytes 835592 | tf_op jit(solution)/shard_map/ppermute | solution.py:509

commit v3 on v2

v3 whole, which is shorter than its diff:
```python
import functools

import jax
import jax.numpy as jnp
from jax import lax
from jax.experimental import pallas as pl
from jax.experimental.pallas import tpu as pltpu
from jax.sharding import PartitionSpec as P


ITERS = 3
TILE = 4
DEEP = ITERS
NEAR = ITERS - 1
LANES = 128
SUBS = 8

kerr_coef = 4.0
sigma_peak = 8.0

VMEM = pl.BlockSpec(memory_space=pltpu.VMEM)
SMEM = pl.BlockSpec(memory_space=pltpu.SMEM)


class Sizes:
    def __init__(self, owned, cells, counts):
        self.owned = owned
        self.cx, self.cy, self.cz = cells
        self.gx, self.gy, self.ha = counts
        self.harmonics = owned * self.ha
        self.halves = self.cz // LANES
        self.wide = self.cx + 2 * DEEP
        self.rows = self.cy + 2 * DEEP + 2
        self.kinds = [(h, r, c) for h in range(owned) for r in range(2) for c in range(3)]
        self.colours = (0,) if self.gy == 2 else (0, 1)
        assert self.cy == SUBS and self.cx >= DEEP
        planes = range(self.cx)
        self.side, self.side_rows = self.groups(
            [(x, 0, DEEP) for x in planes], [(x, 0, NEAR) for x in planes]
        )
        self.main, at = self.groups(
            [(p, 0, DEEP - 1 - p) for p in range(DEEP - 1)],
            [(p, 0, NEAR - 1 - p) for p in range(NEAR - 1)],
        )
        rest, self.corner_rows = self.groups(
            [(p, DEEP - 1 - p, DEEP) for p in range(DEEP)],
            [(p, NEAR - 1 - p, NEAR) for p in range(NEAR)],
            at,
        )
        self.corner = self.main + rest
        self.main_rows = round_up(at)
        edges = len(self.colours) - 1
        self.far, self.far_rows = self.groups(
            [(p, DEEP, self.cy - edges * DEEP) for p in range(DEEP)],
            [(p, NEAR, self.cy - edges * NEAR) for p in range(NEAR)],
        )

    def groups(self, deep, near, at=SUBS):
        listed = []
        for field, kinds, planes in ((0, self.kinds, deep), (1, self.kinds, near), (2, [()], deep)):
            for kind in kinds:
                for plane, low, high in planes:
                    listed.append((field, kind, plane, low, high, at))
                    at += high - low
        return listed, at


def round_up(rows):
    return (rows + SUBS - 1) // SUBS * SUBS


def half(z):
    return slice(z * LANES, (z + 1) * LANES)


def tile_mask(tiles_ref, plane, rows):
    place = lax.broadcasted_iota(jnp.int32, (rows, LANES), 0) // TILE
    mask = jnp.zeros((rows, LANES), jnp.float32)
    for col in range(rows // TILE):
        cell = tiles_ref[plane // TILE, col].astype(jnp.float32)
        mask = jnp.where(place == col, cell, mask)
    return mask


def plane_mask(tiles_ref, plane, sz):
    mask = tile_mask(tiles_ref, 0, sz.cy)
    for x in range(TILE, sz.cx, TILE):
        mask = jnp.where(plane >= x, tile_mask(tiles_ref, x, sz.cy), mask)
    return kerr_coef * mask


def x_is_high(colour):
    return lax.rem(lax.axis_index("gx") + colour, 2) == 0


def y_is_high(colour):
    return lax.rem(lax.axis_index("gy") + colour, 2) == 0


def fill(sz, ref, groups, top, plane_of, inputs):
    src_ref, fwd_ref, eps_ref, tiles_ref = inputs
    mask = plane_mask(tiles_ref, 0, sz) if sz.cx <= TILE else None
    for field, kind, plane, low, high, at in reversed(groups):
        x = plane_of(plane)
        room = sz.cy - (high - low)
        for z in range(sz.halves):
            if field == 2:
                tile = eps_ref[x, :, half(z)]
            elif field == 0:
                tile = src_ref[(*kind, x, slice(None), half(z))]
            else:
                scale = plane_mask(tiles_ref, x, sz) if mask is None else mask
                tile = fwd_ref[(*kind, x, slice(None), half(z))] * scale
            if_top = pltpu.roll(tile, low, 0) if low else tile
            if_not = pltpu.roll(tile, sz.cy - high, 0) if high < sz.cy else tile
            ref[z, at - room : at + high - low] = jnp.where(top, if_top, if_not)


def from_face(sz, colour):
    upper = x_is_high(colour)
    return lambda plane: jnp.where(upper, sz.cx - 1 - plane, plane)


def pack_kernel(
    sz, src_ref, fwd_ref, eps_ref, tiles_ref, freq_ref, mix_ref, pml_ref, *out_refs
):
    inputs = (src_ref, fwd_ref, eps_ref, tiles_ref)
    outs = iter(out_refs)
    for colour in sz.colours:
        top = y_is_high(colour)
        for pairing in (0, 1):
            fill(sz, next(outs), sz.corner, top, from_face(sz, pairing), inputs)
        fill(sz, next(outs), sz.side, top, lambda plane: plane, inputs)
    for pairing in (0, 1):
        fill(sz, next(outs), sz.far, y_is_high(0), from_face(sz, pairing), inputs)
    swap_ref, table_ref = outs

    at_row = lax.broadcasted_iota(jnp.int32, (SUBS, LANES), 0)
    at_lane = lax.broadcasted_iota(jnp.int32, (SUBS, LANES), 1)
    table = jnp.zeros((SUBS, LANES), jnp.float32)
    for row, lane, value in scalars(sz, freq_ref, mix_ref, pml_ref):
        table = jnp.where((at_row == row) & (at_lane == lane), value, table)
    table_ref[...] = table

    _, globally = harmonic_order(sz)
    masks = [kerr_coef * tile_mask(tiles_ref, x, sz.cy) for x in range(sz.cx)]
    for h in range(sz.owned):
        squared = freq_ref[globally(h)] * freq_ref[globally(h)]
        for z in range(sz.halves):
            for x in range(sz.cx):
                inv = 1.0 / (10.0 + squared * eps_ref[x, :, half(z)])
                for r in range(2):
                    for c in range(3):
                        first = src_ref[h, r, c, x, :, half(z)] * inv
                        masked = fwd_ref[h, r, c, x, :, half(z)] * masks[x]
                        swap_ref[0, h, r, c, x, z] = first
                        swap_ref[1, h, r, c, x, z] = masked


def scalars(sz, freq_ref, mix_ref, pml_ref):
    for h in range(sz.harmonics):
        yield 0, h, freq_ref[h] * freq_ref[h]
    for axis in range(3):
        yield 1, axis, pml_ref[axis].astype(jnp.float32)
    for p in range(mix_ref.shape[0]):
        for side in range(2):
            for h in range(sz.harmonics):
                yield 2 + side, p * sz.harmonics + h, mix_ref[p, side, h].astype(jnp.float32)


def relay_kernel(sz, colour, even_ref, odd_ref, anti_ref, main_ref):
    same = x_is_high(0) == y_is_high(colour)

    @pl.when(same)
    def _():
        anti_ref[...] = even_ref[...]
        main_ref[...] = odd_ref[:, : sz.main_rows]

    @pl.when(jnp.logical_not(same))
    def _():
        anti_ref[...] = odd_ref[...]
        main_ref[...] = even_ref[:, : sz.main_rows]


def harmonic_order(sz):
    start = lax.axis_index("ha") * sz.owned
    from_own = lambda index: lax.rem(index - start + sz.harmonics, sz.harmonics)
    globally = lambda position: lax.rem(position + start, sz.harmonics)
    return from_own, globally


def sweep_kernel(sz, mixes, table_ref, eps_ref, *refs):
    cx, cy, cz, halves = sz.cx, sz.cy, sz.cz, sz.halves
    wide, harmonics = sz.wide, sz.harmonics
    blocks, refs = refs[:2], refs[2:]
    per_core = 2 + 5 * len(sz.colours)
    sides = [refs[per_core * s : per_core * (s + 1)] for s in range(sz.ha)]
    out_ref, grad_ref = refs[per_core * sz.ha : per_core * sz.ha + 2]
    base, first, second, fwd, invs, mags, eps_all, table, sem = refs[per_core * sz.ha + 2 :]
    copy = pltpu.make_async_copy(table_ref, table, sem)
    copy.start()

    at_x, at_y = lax.axis_index("gx"), lax.axis_index("gy")
    from_own, globally = harmonic_order(sz)

    nothing = jnp.zeros((DEEP, LANES), jnp.float32)
    low_rows, high_rows = pl.ds(0, DEEP), pl.ds(DEEP + cy, DEEP)
    spots = []
    for x in range(wide):
        for rows in (low_rows, high_rows):
            if len(sz.colours) > 1:
                spots.append((x, rows))
    if len(sz.colours) == 1:
        low = at_y == 0
        there = jnp.where(low, 0, DEEP + cy)
        here = jnp.where(low, DEEP + cy, 0)
        spots += [(x, pl.ds(there, DEEP)) for x in range(wide)]
        corner_at = jnp.where(low, DEEP + cx, 0)
        spots += [(corner_at + d, pl.ds(here, DEEP)) for d in range(DEEP)]
    for x, rows in spots:
        for z in range(halves):
            eps_all[x, z, rows] = nothing
            for g in range(harmonics):
                for r in range(2):
                    for c in range(3):
                        base[g, r, c, x, z, rows] = nothing
                        if isinstance(x, int) and not 1 <= x < wide - 1:
                            continue
                        at = x - 1 if isinstance(x, int) else jnp.clip(x - 1, 0, wide - 3)
                        fwd[g, r, c, at, z, rows] = nothing
    for x in range(wide):
        for z in range(halves):
            eps_all[x, z, sz.rows - 2 :] = jnp.zeros((2, LANES), jnp.float32)
            if DEEP <= x < DEEP + cx:
                eps_all[x, z, DEEP : DEEP + cy] = eps_ref[x - DEEP, :, half(z)]
    copy.wait()

    squared = [table[0, globally(h)] for h in range(harmonics)]
    widths = [table[1, axis].astype(jnp.int32) for axis in range(3)]
    lane = lax.broadcasted_iota(jnp.int32, (SUBS, LANES), 1)
    sub = lax.broadcasted_iota(jnp.int32, (SUBS, LANES), 0)

    def face_spots(pairing, colour):
        high_x, top = x_is_high(pairing), y_is_high(colour)
        plane_of = lambda plane: jnp.where(high_x, DEEP + cx + plane, DEEP - 1 - plane)
        row_of = lambda low, high: jnp.where(top, DEEP + cy - high, DEEP + low)
        return plane_of, row_of

    def side_spots(colour, corner=None):
        high_y = y_is_high(colour)
        if corner is None:
            plane_of = lambda plane: DEEP + plane
        else:
            high_x = jnp.logical_not(high_y) if corner == "anti" else high_y
            plane_of = lambda plane: jnp.where(high_x, DEEP + cx + plane, DEEP - 1 - plane)
        row_of = lambda low, high: jnp.where(high_y, DEEP + cy + low, DEEP - high)
        return plane_of, row_of

    def row_buffers(side):
        buffers = side
        for pairing in (0, 1):
            yield buffers[pairing], sz.far, face_spots(pairing, 0)
        for i, colour in enumerate(sz.colours):
            even, odd, edge, anti, main = buffers[2 + 5 * i : 7 + 5 * i]
            yield even, sz.corner, face_spots(0, colour)
            yield odd, sz.corner, face_spots(1, colour)
            yield edge, sz.side, side_spots(colour)
            yield anti, sz.corner, side_spots(colour, "anti")
            yield main, sz.main, side_spots(colour, "main")

    for buffer, groups, (plane_of, row_of) in row_buffers(sides[0]):
        for field, kind, plane, low, high, at in groups:
            if field == 2:
                for z in range(halves):
                    eps_all[plane_of(plane), z, pl.ds(row_of(low, high), high - low)] = buffer[
                        z, at : at + high - low
                    ]

    def keep_rows(row):
        place = sub + (row - DEEP) + at_y * cy
        return (place >= 0) & (place < cy * sz.gy)

    def keep_plane(x):
        place = x - DEEP + at_x * cx
        return (place >= 0) & (place < cx * sz.gx)

    def scales(x, _):
        inside = jnp.where(keep_plane(x), 1.0, 0.0)
        for row in (0, SUBS):
            keep = jnp.where(keep_rows(row), inside, 0.0)
            for z in range(halves):
                eps = eps_all[x, z, row : row + SUBS]
                for h in range(harmonics):
                    invs[h, x, z, row : row + SUBS] = keep / (10.0 + squared[h] * eps)
        return 0

    lax.fori_loop(0, wide, scales, 0)

    for s, block in enumerate(blocks):
        for h, r, c in sz.kinds:
            g = s * sz.owned + h
            for x in range(cx):
                for z in range(halves):
                    rows = slice(DEEP, DEEP + cy)
                    base[g, r, c, DEEP + x, z, rows] = block[0, h, r, c, x, z]
                    fwd[g, r, c, NEAR + x, z, rows] = block[1, h, r, c, x, z]
    for s, side in enumerate(sides):
        for buffer, groups, (plane_of, row_of) in row_buffers(side):
            for field, kind, plane, low, high, at in groups:
                if field == 2:
                    continue
                h, r, c = kind
                g = s * sz.owned + h
                x, rows = plane_of(plane), pl.ds(row_of(low, high), high - low)
                for z in range(halves):
                    got = buffer[z, at : at + high - low]
                    if field == 0:
                        base[g, r, c, x, z, rows] = got * invs[g, x, z, rows]
                    else:
                        fwd[g, r, c, x - 1, z, rows] = got

    def profile(width, place, cells):
        reach = jnp.maximum(jnp.maximum(width - place, place - (cells - 1 - width)), 0)
        return (reach.astype(jnp.float32) / jnp.full(reach.shape, width).astype(jnp.float32)) ** 2

    sigma_z = [profile(widths[2], lane + z * LANES, cz) for z in range(halves)]

    def z_ahead(parts):
        turned = [pltpu.roll(v, LANES - 1, 1) for v in parts]
        following = turned[1:] + [0.0]
        return [jnp.where(lane == LANES - 1, f, t) for t, f in zip(turned, following)]

    def z_behind(parts):
        turned = [pltpu.roll(v, 1, 1) for v in parts]
        previous = [0.0] + turned[:-1]
        return [jnp.where(lane == 0, p, t) for t, p in zip(turned, previous)]

    def mixed(side, h, p):
        return from_own(table[2 + side, p * harmonics + globally(h)].astype(jnp.int32))

    pairs = [(mixed(0, h, p), mixed(1, h, p)) for h in range(harmonics) for p in range(mixes)]
    zs = range(halves)

    def sweep(k, v_ref, store):
        lo, hi = k + 1, wide - 1 - k
        top = DEEP + cy + NEAR - k
        out_rows = sorted({k + 1, top - SUBS})
        mag_rows = sorted({k, top - SUBS})
        sigma_y = {
            row: profile(widths[1], sub + (row - DEEP) + at_y * cy, cy * sz.gy) for row in out_rows
        }

        def write_mags(x, g, comps):
            slot = lax.rem(x, 2)
            inside = x - DEEP + at_x * cx >= 0
            for r in range(2):
                for row in mag_rows:
                    mask = (sub + (row - DEEP) + at_y * cy >= 0) & inside
                    fx, fy, fz = [
                        [v_ref[g, r, c, x, z, row : row + SUBS] for z in zs] for c in range(3)
                    ]
                    next_y, next_z = [
                        [v_ref[g, r, c, x + 1, z, row : row + SUBS] for z in zs] for c in (1, 2)
                    ]
                    above_x, above_z = [
                        [v_ref[g, r, c, x, z, row + 1 : row + 1 + SUBS] for z in zs] for c in (0, 2)
                    ]
                    after_x = z_ahead(fx)
                    found = {}
                    if 0 in comps:
                        after_y = z_ahead(fy)
                        found[0] = [(above_z[z] - fz[z]) - (after_y[z] - fy[z]) for z in zs]
                    found[1] = [(after_x[z] - fx[z]) - (next_z[z] - fz[z]) for z in zs]
                    found[2] = [(next_y[z] - fy[z]) - (above_x[z] - fx[z]) for z in zs]
                    for c, parts in found.items():
                        for z in zs:
                            pltpu.store(
                                mags.at[slot, g, r, c, z, row : row + SUBS], parts[z], mask=mask
                            )

        for slot in range(2):
            for g in range(harmonics):
                for r in range(2):
                    for c in range(3):
                        for z in zs:
                            mags[slot, g, r, c, z] = jnp.zeros((sz.rows, LANES), jnp.float32)
        for g in range(harmonics):
            write_mags(k, g, (1, 2))

        def body(x, _):
            slot, past = lax.rem(x, 2), lax.rem(x + 1, 2)
            twice = jnp.where(keep_plane(x), 2.0, 0.0)
            place = jnp.full((SUBS, LANES), x - DEEP + at_x * cx)
            sigma_x = profile(widths[0], place, cx * sz.gx)
            spots = [(row, z) for row in out_rows for z in zs]
            sigma = {
                (row, z): sigma_peak * (sigma_x + sigma_y[row] + sigma_z[z]) for row, z in spots
            }
            double = {row: jnp.where(keep_rows(row), twice, 0.0) for row in out_rows}
            for h in range(harmonics):
                write_mags(x, h, (0, 1, 2))
                curls = {}
                for row in out_rows:
                    span, below = slice(row, row + SUBS), slice(row - 1, row - 1 + SUBS)
                    for r in range(2):
                        mag = [[mags[slot, h, r, c, z, span] for z in zs] for c in range(3)]
                        low_x, low_z = [
                            [mags[slot, h, r, c, z, below] for z in zs] for c in (0, 2)
                        ]
                        past_y, past_z = [
                            [mags[past, h, r, c, z, span] for z in zs] for c in (1, 2)
                        ]
                        before_x, before_y = z_behind(mag[0]), z_behind(mag[1])
                        for z in zs:
                            curls[row, z, r] = [
                                (mag[2][z] - low_z[z]) - (mag[1][z] - before_y[z]),
                                (mag[0][z] - before_x[z]) - (mag[2][z] - past_z[z]),
                                (mag[1][z] - past_y[z]) - (mag[0][z] - low_x[z]),
                            ]
                inv = {(row, z): invs[h, x, z, row : row + SUBS] for row, z in spots}
                slope = {(row, z): double[row] - 10.0 * inv[row, z] for row, z in spots}
                absorb = {spot: squared[h] * sigma[spot] for spot in spots}
                for c in range(3):
                    real, imag = {}, {}
                    for p in range(mixes):
                        a, b = pairs[h * mixes + p]
                        for row, z in spots:
                            span = slice(row, row + SUBS)
                            fr, fi = [fwd[a, r, c, x - 1, z, span] for r in range(2)]
                            vr, vi = [v_ref[b, r, c, x, z, span] for r in range(2)]
                            one, two = fr * vr - fi * vi, fr * vi + fi * vr
                            real[row, z] = real[row, z] + one if p else one
                            imag[row, z] = imag[row, z] + two if p else two
                    for row, z in spots:
                        span = slice(row, row + SUBS)
                        vr, vi = [v_ref[h, r, c, x, z, span] for r in range(2)]
                        new_r = (
                            base[h, 0, c, x, z, span]
                            + vr * slope[row, z]
                            + inv[row, z]
                            * (squared[h] * real[row, z] - absorb[row, z] * vi - curls[row, z, 0][c])
                        )
                        new_i = (
                            base[h, 1, c, x, z, span]
                            + vi * slope[row, z]
                            + inv[row, z]
                            * (squared[h] * imag[row, z] + absorb[row, z] * vr - curls[row, z, 1][c])
                        )
                        store(h, c, x, z, span, new_r, new_i)
            return 0

        lax.fori_loop(lo, hi, body, 0)

    def store_in(ref):
        def store(h, c, x, z, span, new_r, new_i):
            ref[h, 0, c, x, z, span] = new_r
            ref[h, 1, c, x, z, span] = new_i

        return store

    sums = {}

    def store_out(h, c, x, z, span, new_r, new_i):
        if h < sz.owned:
            out_ref[h, 0, c, x - DEEP, :, half(z)] = new_r
            out_ref[h, 1, c, x - DEEP, :, half(z)] = new_i
        term = (squared[h] / kerr_coef) * (
            new_r * fwd[h, 0, c, x - 1, z, span] - new_i * fwd[h, 1, c, x - 1, z, span]
        )
        if h == 0 and c == 0:
            sums[z] = term
        else:
            sums[z] = sums[z] + term
        if h == harmonics - 1 and c == 2:
            grad_ref[x - DEEP, :, half(z)] = sums[z]

    sweep(0, base, store_in(first))
    sweep(1, first, store_in(second))
    sweep(2, second, store_out)


def swaps(count_x, count_y, partner):
    sends = []
    for x in range(count_x):
        for y in range(count_y):
            to_x, to_y = partner(x, y)
            if 0 <= to_x < count_x and 0 <= to_y < count_y:
                sends.append((x * count_y + y, to_x * count_y + to_y))
    return sends


def shards(
    forward_field, adjoint_source, permittivity, frequency, design_tiles, mix_pairs, pml_width
):
    counts = tuple(lax.axis_size(name) for name in ("gx", "gy", "ha"))
    sz = Sizes(forward_field.shape[0], permittivity.shape, counts)
    f32 = jnp.float32

    def rows_buffer(rows):
        return jax.ShapeDtypeStruct((sz.halves, round_up(rows), LANES), f32)

    def field(planes):
        return pltpu.VMEM((sz.harmonics, 2, 3, planes, sz.halves, sz.rows, LANES), f32)

    swapped = jax.ShapeDtypeStruct((2, sz.owned, 2, 3, sz.cx, sz.halves, sz.cy, LANES), f32)

    def send(buffer, partner):
        return lax.ppermute(buffer, ("gx", "gy"), swaps(sz.gx, sz.gy, partner))

    def step(place, colour):
        return 1 if (place + colour) % 2 == 0 else -1

    def along_x(buffer, pairing):
        return send(buffer, lambda x, y: (x + step(x, pairing), y))

    def along_y(buffer, colour):
        return send(buffer, lambda x, y: (x, y + step(y, colour)))

    corner, edge = rows_buffer(sz.corner_rows), rows_buffer(sz.side_rows)
    mix_by_pair = jnp.transpose(mix_pairs, (1, 2, 0))
    far_buf, table = rows_buffer(sz.far_rows), jax.ShapeDtypeStruct((SUBS, LANES), f32)
    shapes = [corner, corner, edge] * len(sz.colours)
    shapes += [far_buf, far_buf, swapped, table]
    packed = pl.pallas_call(
        functools.partial(pack_kernel, sz),
        out_shape=shapes,
        in_specs=[VMEM] * 3 + [SMEM] * 4,
        out_specs=[VMEM] * len(shapes),
        name="pack",
    )(adjoint_source, forward_field, permittivity, design_tiles, frequency, mix_by_pair, pml_width)
    near = packed[: 3 * len(sz.colours)]
    *far, mine, table = packed[3 * len(sz.colours) :]
    got = []
    for i, colour in enumerate(sz.colours):
        even = along_x(near[3 * i], 0)
        odd = along_x(near[3 * i + 1], 1)
        side = along_y(near[3 * i + 2], colour)
        anti, main = pl.pallas_call(
            functools.partial(relay_kernel, sz, colour),
            out_shape=[corner, rows_buffer(sz.main_rows)],
            in_specs=[VMEM, VMEM],
            out_specs=[VMEM, VMEM],
            compiler_params=pltpu.CompilerParams(vmem_limit_bytes=4 * 1024 * 1024),
            name="relay",
        )(even, odd)
        anti = along_y(anti, colour)
        main = along_y(main, colour)
        got += [even, odd, side, anti, main]
    far_even = along_x(far[0], 0)
    far_odd = along_x(far[1], 1)
    own = [mine, far_even, far_odd] + got
    flip = [(i, sz.ha - 1 - i) for i in range(sz.ha)]
    other = []
    for buffer in own:
        other.append(lax.ppermute(buffer, "ha", flip))

    buffers = own[:1] + other[:1] + own[1:] + other[1:]
    adjoint, gradient = pl.pallas_call(
        functools.partial(sweep_kernel, sz, mix_pairs.shape[1]),
        out_shape=[
            jax.ShapeDtypeStruct(adjoint_source.shape, f32),
            jax.ShapeDtypeStruct(permittivity.shape, f32),
        ],
        in_specs=[VMEM] * (2 + len(buffers)),
        out_specs=[VMEM] * 2,
        scratch_shapes=[
            field(sz.wide),
            field(sz.wide),
            field(sz.wide),
            field(sz.wide - 2),
            pltpu.VMEM((sz.harmonics, sz.wide, sz.halves, sz.rows, LANES), f32),
            pltpu.VMEM((2, sz.harmonics, 2, 3, sz.halves, sz.rows, LANES), f32),
            pltpu.VMEM((sz.wide, sz.halves, sz.rows, LANES), f32),
            pltpu.SMEM((SUBS, LANES), f32),
            pltpu.SemaphoreType.DMA,
        ],
        compiler_params=pltpu.CompilerParams(vmem_limit_bytes=32 * 1024 * 1024),
        name="sweeps",
    )(table, permittivity, *buffers)
    return (adjoint, gradient)


def solution(mesh):
    return jax.shard_map(
        shards,
        mesh=mesh,
        in_specs=(
            P("ha", None, None, ("cand", "gx"), "gy", None),
            P("ha", None, None, ("cand", "gx"), "gy", None),
            P(("cand", "gx"), "gy", None),
            P(),
            P(("cand", "gx"), "gy"),
            P(),
            P(),
        ),
        out_specs=(P("ha", None, None, ("cand", "gx"), "gy", None), P(("cand", "gx"), "gy", None)),
        check_vma=False,
    )
```

time: 40.6 us -> 41.9 us (1.032)
  the two profiles are of different devices: /device:TPU:17 before, /device:TPU:0 now
where the time goes in v3:
time: 41.9 us; the launch traced here: 41.6 us
  Pallas kernels  15.1 us (36%)
  starting transfers between devices  13 us (31%)
  waiting for transfers between devices  11.8 us (28%)
  local copies, waits for them, and re-layouts  1.14 us (3%)
  between operations  0.72 us (2%)
    pallas_call x1, Pallas kernels, shards(): pl.pallas_call(functools.partial(sweep_kernel, sz, mix_pairs.shape[1]), o...  12.2 us
    ppermute x7, starting transfers between devices, send(): return lax.ppermute(buffer, ('gx', 'gy'), swaps(sz.gx, sz.gy, partner))  11.6 us
    ppermute x7, waiting for transfers between devices, send(): return lax.ppermute(buffer, ('gx', 'gy'), swaps(sz.gx, sz.gy, partner))  9.33 us
    pallas_call x1, Pallas kernels, shards(): pl.pallas_call(functools.partial(pack_kernel, sz), out_shape=shapes, in_s...  2.8 us
    ppermute x8, waiting for transfers between devices, shards(): other.append(lax.ppermute(buffer, 'ha', flip))  2.43 us
    ppermute x8, starting transfers between devices, shards(): other.append(lax.ppermute(buffer, 'ha', flip))  1.35 us
    unnamed x6, local copies, waits for them, and re-layouts  1.14 us
  transfers between devices with their start and end apart: 15, of which 5 were waited for; matrix products, arithmetic and copies ran while one was open for 0% of the time, Pallas kernels for 0%

profile of v3, /device:TPU:0, one launch (start us, length us, event | category | flops | bytes accessed | tf_op | source)
XLA Modules:
  0.0 41.6 jit_solution(13734994788265518856)
XLA Ops:
  0.6 2.8 %pack.1 = (f32[2,176,128]{2,1,0:T(8,128)}, f32[2,176,128]{2,1,0:T(8,128)}, f32[2,264,128]{2,1,0:T(8,128)}, f32[2,352,128]{2,1,0:T(8,128)}, f32[2,352,128]{2,1,0:...) custom-call(f32[2,2,3,4,8,256]{5,4,3,2,1,0:T(8,128)} %src_ref.1, f32[2,2,3,4,8,256]{5,4,3,2,1,0:T(8,128)} %fwd_ref.1, ...), custom_call_target="tpu_custom_call" | custom-call | tf_op jit(solution)/shard_map/pack/pallas_call | solution.py:524
  3.4 3.1 %collective-permute-start.3 = (f32[2,176,128]{2,1,0:T(8,128)}, f32[2,176,128]{2,1,0:T(8,128)S(1)}, u32[]{:S(2)}, u32[]{:S(2)}) collective-permute-start(f32[2,176,128]{2,1,0:T(8,128)} %get-tuple-element.15), channel_id=1, source_target_pairs={{0,4},{2,6},{4,0},{6,2},{8,12},{10,14},{12,8},{14,10},{1,5},{3,7},... | collective-permute-start | bytes 540680 | tf_op jit(solution)/shard_map/ppermute | solution.py:508
  6.5 0.7 %collective-permute-start.4 = (f32[2,176,128]{2,1,0:T(8,128)}, f32[2,176,128]{2,1,0:T(8,128)S(1)}, u32[]{:S(2)}, u32[]{:S(2)}) collective-permute-start(f32[2,176,128]{2,1,0:T(8,128)} %get-tuple-element.16), channel_id=1, source_target_pairs={{4,8},{6,10},{8,4},{10,6},{5,9},{7,11},{9,5},{11,7},{20,24},{22,26... | collective-permute-start | bytes 540680 | tf_op jit(solution)/shard_map/ppermute | solution.py:508
  7.2 1.6 %collective-permute-start.5 = (f32[2,264,128]{2,1,0:T(8,128)}, f32[2,264,128]{2,1,0:T(8,128)S(1)}, u32[]{:S(2)}, u32[]{:S(2)}) collective-permute-start(f32[2,264,128]{2,1,0:T(8,128)} %get-tuple-element.17), channel_id=1, source_target_pairs={{0,2},{2,0},{4,6},{6,4},{8,10},{10,8},{12,14},{14,12},{1,3},{3,1},... | collective-permute-start | bytes 811016 | tf_op jit(solution)/shard_map/ppermute | solution.py:508
  8.7 0.0 collective-permute-start
  8.7 4.4 %collective-permute-start.1 = (f32[2,352,128]{2,1,0:T(8,128)}, f32[2,352,128]{2,1,0:T(8,128)S(1)}, u32[]{:S(2)}, u32[]{:S(2)}) collective-permute-start(f32[2,352,128]{2,1,0:T(8,128)} %get-tuple-element.13), channel_id=1, source_target_pairs={{0,4},{2,6},{4,0},{6,2},{8,12},{10,14},{12,8},{14,10},{1,5},{3,7},... | collective-permute-start | bytes 1081352 | tf_op jit(solution)/shard_map/ppermute | solution.py:508
  13.1 0.0 collective-permute-done.3.even_ref.refs_4_
  13.1 0.8 %collective-permute-start.2 = (f32[2,352,128]{2,1,0:T(8,128)}, f32[2,352,128]{2,1,0:T(8,128)S(1)}, u32[]{:S(2)}, u32[]{:S(2)}) collective-permute-start(f32[2,352,128]{2,1,0:T(8,128)} %get-tuple-element.14), channel_id=1, source_target_pairs={{4,8},{6,10},{8,4},{10,6},{5,9},{7,11},{9,5},{11,7},{20,24},{22,26... | collective-permute-start | bytes 1081352 | tf_op jit(solution)/shard_map/ppermute | solution.py:508
  13.9 0.0 collective-permute-done.4.odd_ref.refs_5_
  14.0 0.0 copy-start.2
  14.0 0.6 %collective-permute-start.7 = (f32[2,64,128]{2,1,0:T(8,128)S(1)}, f32[2,64,128]{2,1,0:T(8,128)S(1)}, u32[]{:S(2)}, u32[]{:S(2)}) collective-permute-start(f32[2,64,128]{2,1,0:T(8,128)S(1)} %get-tuple-element.19), channel_id=1, source_target_pairs={{0,2},{2,0},{4,6},{6,4},{8,10},{10,8},{12,14},{14,12},{1,3},{3,1},... | collective-permute-start | bytes 196616 | tf_op jit(solution)/shard_map/ppermute | solution.py:508
  14.6 3.7 %collective-permute-done.7.refs_8_ = f32[2,64,128]{2,1,0:T(8,128)S(1)} collective-permute-done((f32[2,64,128]{2,1,0:T(8,128)S(1)}, f32[2,64,128]{2,1,0:T(8,128)S(1)}, u32[]{:S(2)}, u32[]{:S(2)}) %collective-permute-start.7) | collective-permute-done | bytes 65568 | tf_op jit(solution)/shard_map/ppermute | solution.py:508
  18.3 0.0 collective-permute-start.10
  18.3 0.0 collective-permute-done.5.refs_6_
  18.3 0.5 %collective-permute-start.14 = (f32[2,64,128]{2,1,0:T(8,128)S(1)}, f32[2,64,128]{2,1,0:T(8,128)S(1)}, u32[]{:S(2)}, u32[]{:S(2)}) collective-permute-start(f32[2,64,128]{2,1,0:T(8,128)S(1)} %collective-permute-done.7.refs_8_), channel_id=1, source_target_pairs={{0,1},{1,0},{2,3},{3,2},{4,5},{5,4},{6,7},{7,6},{8,9},{9,8},{10,11... | collective-permute-start | bytes 196616 | tf_op jit(solution)/shard_map/ppermute | solution.py:555
  18.8 1.0 %collective-permute-done.14.refs_15_ = f32[2,64,128]{2,1,0:T(8,128)S(1)} collective-permute-done((f32[2,64,128]{2,1,0:T(8,128)S(1)}, f32[2,64,128]{2,1,0:T(8,128)S(1)}, u32[]{:S(2)}, u32[]{:S(2)}) %collective-permute-start.14) | collective-permute-done | bytes 65568 | tf_op jit(solution)/shard_map/ppermute | solution.py:555
  19.8 0.3 collective-permute-start.11
  20.1 0.0 collective-permute-done.10.refs_11_
  20.1 0.5 %collective-permute-start.6 = (f32[2,176,128]{2,1,0:T(8,128)S(1)}, f32[2,176,128]{2,1,0:T(8,128)S(1)}, u32[]{:S(2)}, u32[]{:S(2)}) collective-permute-start(f32[2,176,128]{2,1,0:T(8,128)S(1)} %get-tuple-element.18), channel_id=1, source_target_pairs={{0,2},{2,0},{4,6},{6,4},{8,10},{10,8},{12,14},{14,12},{1,3},{3,1},... | collective-permute-start | bytes 540680 | tf_op jit(solution)/shard_map/ppermute | solution.py:508
  20.6 1.8 %collective-permute-done.1.refs_2_ = f32[2,352,128]{2,1,0:T(8,128)S(1)} collective-permute-done((f32[2,352,128]{2,1,0:T(8,128)}, f32[2,352,128]{2,1,0:T(8,128)S(1)}, u32[]{:S(2)}, u32[]{:S(2)}) %collective-permute-start.1) | collective-permute-done | bytes 360480 | tf_op jit(solution)/shard_map/ppermute | solution.py:508
  22.4 0.0 collective-permute-start.8
  22.4 0.5 %collective-permute-start.9 = (f32[2,352,128]{2,1,0:T(8,128)S(1)}, f32[2,352,128]{2,1,0:T(8,128)S(1)}, u32[]{:S(2)}, u32[]{:S(2)}) collective-permute-start(f32[2,352,128]{2,1,0:T(8,128)S(1)} %collective-permute-done.2.refs_3_), channel_id=1, source_target_pairs={{0,1},{1,0},{2,3},{3,2},{4,5},{5,4},{6,7},{7,6},{8,9},{9,8},{10,11... | collective-permute-start | bytes 1081352 | tf_op jit(solution)/shard_map/ppermute | solution.py:555
  22.9 0.1 collective-permute-start.12
  23.0 3.8 %collective-permute-done.6.refs_7_ = f32[2,176,128]{2,1,0:T(8,128)S(1)} collective-permute-done((f32[2,176,128]{2,1,0:T(8,128)S(1)}, f32[2,176,128]{2,1,0:T(8,128)S(1)}, u32[]{:S(2)}, u32[]{:S(2)}) %collective-permute-start.6) | collective-permute-done | bytes 180256 | tf_op jit(solution)/shard_map/ppermute | solution.py:508
  26.8 0.0 collective-permute-start.13
  26.8 1.4 %collective-permute-done.13.refs_14_ = f32[2,176,128]{2,1,0:T(8,128)S(1)} collective-permute-done((f32[2,176,128]{2,1,0:T(8,128)S(1)}, f32[2,176,128]{2,1,0:T(8,128)S(1)}, u32[]{:S(2)}, u32[]{:S(2)}) %collective-permute-start.13) | collective-permute-done | bytes 180256 | tf_op jit(solution)/shard_map/ppermute | solution.py:555
  28.2 0.0 collective-permute-done.12.refs_13_
  28.2 0.0 collective-permute-done.8.refs_9_
  28.2 0.0 collective-permute-done.9.refs_10_
  28.2 0.0 collective-permute-done.refs_1_
  28.3 1.1 %copy-done = f32[2,2,2,3,4,2,8,128]{7,6,5,4,3,2,1,0:T(8,128)S(1)} copy-done((f32[2,2,2,3,4,2,8,128]{7,6,5,4,3,2,1,0:T(8,128)S(1)}, f32[2,2,2,3,4,2,8,128]{7,6,5,4,3,2,1,0:T(8,128)}, u32[]{:S(2)}) %copy-start) | copy-done | bytes 786456
  29.4 12.2 %sweeps.1 = (f32[2,2,3,4,8,256]{5,4,3,2,1,0:T(8,128)}, f32[4,8,256]{2,1,0:T(8,128)}) custom-call(f32[8,128]{1,0:T(8,128)S(1)} %copy-done.2, f32[4,8,256]{2,1,0:T(8,128)S(1)} %copy-done.1, f32[2,2,2,3,4,2,8,128]{7,6,5,4,3,2,1,0:T(8,128)S(1)} %copy-done, f32[2,2,2,3,4,2,8,128]{7,6,5,4,3,2,1,0:T(8,128)S(1)} %collective-permute-done.refs_1_, ...), custom_call_target="tpu_custom_call" | custom-call | tf_op jit(solution)/shard_map/sweeps/pallas_call | solution.py:558
  (7 shorter events, 0.1 us)
Async XLA Ops:
  3.4 9.7 %collective-permute-start.3 = (f32[2,176,128]{2,1,0:T(8,128)}, f32[2,176,128]{2,1,0:T(8,128)S(1)}, u32[]{:S(2)}, u32[]{:S(2)}) collective-permute-start(f32[2,176,128]{2,1,0:T(8,128)} %get-tuple-element.15), channel_id=1, source_target_pairs={{0,4},{2,6},{4,0},{6,2},{8,12},{10,14},{12,8},{14,10},{1,5},{3,7},... | collective-permute-start | bytes 540680 | tf_op jit(solution)/shard_map/ppermute | solution.py:508
  6.5 7.4 %collective-permute-start.4 = (f32[2,176,128]{2,1,0:T(8,128)}, f32[2,176,128]{2,1,0:T(8,128)S(1)}, u32[]{:S(2)}, u32[]{:S(2)}) collective-permute-start(f32[2,176,128]{2,1,0:T(8,128)} %get-tuple-element.16), channel_id=1, source_target_pairs={{4,8},{6,10},{8,4},{10,6},{5,9},{7,11},{9,5},{11,7},{20,24},{22,26... | collective-permute-start | bytes 540680 | tf_op jit(solution)/shard_map/ppermute | solution.py:508
  7.2 11.2 %collective-permute-start.5 = (f32[2,264,128]{2,1,0:T(8,128)}, f32[2,264,128]{2,1,0:T(8,128)S(1)}, u32[]{:S(2)}, u32[]{:S(2)}) collective-permute-start(f32[2,264,128]{2,1,0:T(8,128)} %get-tuple-element.17), channel_id=1, source_target_pairs={{0,2},{2,0},{4,6},{6,4},{8,10},{10,8},{12,14},{14,12},{1,3},{3,1},... | collective-permute-start | bytes 811016 | tf_op jit(solution)/shard_map/ppermute | solution.py:508
  8.7 19.5 %collective-permute-start = (f32[2,2,2,3,4,2,8,128]{7,6,5,4,3,2,1,0:T(8,128)}, f32[2,2,2,3,4,2,8,128]{7,6,5,4,3,2,1,0:T(8,128)S(1)}, u32[]{:S(2)}, u32[]{:S(2)}) collective-permute-start(f32[2,2,2,3,4,2,8,128]{7,6,5,4,3,2,1,0:T(8,128)} %get-tuple-element.12.refs_0_), channel_id=1, source_target_pairs={{0,1},{1,0},{2,3},{3,2},{4,5},{5,4},{6,7},{7,6},{8,9},{9,8},{10,11... | collective-permute-start | bytes 2359304 | tf_op jit(solution)/shard_map/ppermute | solution.py:555
  8.7 13.7 %collective-permute-start.1 = (f32[2,352,128]{2,1,0:T(8,128)}, f32[2,352,128]{2,1,0:T(8,128)S(1)}, u32[]{:S(2)}, u32[]{:S(2)}) collective-permute-start(f32[2,352,128]{2,1,0:T(8,128)} %get-tuple-element.13), channel_id=1, source_target_pairs={{0,4},{2,6},{4,0},{6,2},{8,12},{10,14},{12,8},{14,10},{1,5},{3,7},... | collective-permute-start | bytes 1081352 | tf_op jit(solution)/shard_map/ppermute | solution.py:508
  13.1 15.1 %copy-start.1 = (f32[4,8,256]{2,1,0:T(8,128)S(1)}, f32[4,8,256]{2,1,0:T(8,128)}, u32[]{:S(2)}) copy-start(f32[4,8,256]{2,1,0:T(8,128)} %eps_ref.3) | copy-start | bytes 98308
  13.1 9.3 %collective-permute-start.2 = (f32[2,352,128]{2,1,0:T(8,128)}, f32[2,352,128]{2,1,0:T(8,128)S(1)}, u32[]{:S(2)}, u32[]{:S(2)}) collective-permute-start(f32[2,352,128]{2,1,0:T(8,128)} %get-tuple-element.14), channel_id=1, source_target_pairs={{4,8},{6,10},{8,4},{10,6},{5,9},{7,11},{9,5},{11,7},{20,24},{22,26... | collective-permute-start | bytes 1081352 | tf_op jit(solution)/shard_map/ppermute | solution.py:508
  14.0 14.3 %copy-start.2 = (f32[8,128]{1,0:T(8,128)S(1)}, f32[8,128]{1,0:T(8,128)}, u32[]{:S(2)}) copy-start(f32[8,128]{1,0:T(8,128)} %get-tuple-element.11.table_ref) | copy-start | bytes 12292
  14.0 4.3 %collective-permute-start.7 = (f32[2,64,128]{2,1,0:T(8,128)S(1)}, f32[2,64,128]{2,1,0:T(8,128)S(1)}, u32[]{:S(2)}, u32[]{:S(2)}) collective-permute-start(f32[2,64,128]{2,1,0:T(8,128)S(1)} %get-tuple-element.19), channel_id=1, source_target_pairs={{0,2},{2,0},{4,6},{6,4},{8,10},{10,8},{12,14},{14,12},{1,3},{3,1},... | collective-permute-start | bytes 196616 | tf_op jit(solution)/shard_map/ppermute | solution.py:508
  18.3 1.8 %collective-permute-start.10 = (f32[2,176,128]{2,1,0:T(8,128)S(1)}, f32[2,176,128]{2,1,0:T(8,128)S(1)}, u32[]{:S(2)}, u32[]{:S(2)}) collective-permute-start(f32[2,176,128]{2,1,0:T(8,128)S(1)} %collective-permute-done.3.even_ref.refs_4_), channel_id=1, source_target_pairs={{0,1},{1,0},{2,3},{3,2},{4,5},{5,4},{6,7},{7,6},{8,9},{9,8},{10,11... | collective-permute-start | bytes 540680 | tf_op jit(solution)/shard_map/ppermute | solution.py:555
  18.3 1.5 %collective-permute-start.14 = (f32[2,64,128]{2,1,0:T(8,128)S(1)}, f32[2,64,128]{2,1,0:T(8,128)S(1)}, u32[]{:S(2)}, u32[]{:S(2)}) collective-permute-start(f32[2,64,128]{2,1,0:T(8,128)S(1)} %collective-permute-done.7.refs_8_), channel_id=1, source_target_pairs={{0,1},{1,0},{2,3},{3,2},{4,5},{5,4},{6,7},{7,6},{8,9},{9,8},{10,11... | collective-permute-start | bytes 196616 | tf_op jit(solution)/shard_map/ppermute | solution.py:555
  19.8 3.1 %collective-permute-start.11 = (f32[2,176,128]{2,1,0:T(8,128)S(1)}, f32[2,176,128]{2,1,0:T(8,128)S(1)}, u32[]{:S(2)}, u32[]{:S(2)}) collective-permute-start(f32[2,176,128]{2,1,0:T(8,128)S(1)} %collective-permute-done.4.odd_ref.refs_5_), channel_id=1, source_target_pairs={{0,1},{1,0},{2,3},{3,2},{4,5},{5,4},{6,7},{7,6},{8,9},{9,8},{10,11... | collective-permute-start | bytes 540680 | tf_op jit(solution)/shard_map/ppermute | solution.py:555
  20.1 6.7 %collective-permute-start.6 = (f32[2,176,128]{2,1,0:T(8,128)S(1)}, f32[2,176,128]{2,1,0:T(8,128)S(1)}, u32[]{:S(2)}, u32[]{:S(2)}) collective-permute-start(f32[2,176,128]{2,1,0:T(8,128)S(1)} %get-tuple-element.18), channel_id=1, source_target_pairs={{0,2},{2,0},{4,6},{6,4},{8,10},{10,8},{12,14},{14,12},{1,3},{3,1},... | collective-permute-start | bytes 540680 | tf_op jit(solution)/shard_map/ppermute | solution.py:508
  22.4 5.8 %collective-permute-start.8 = (f32[2,352,128]{2,1,0:T(8,128)S(1)}, f32[2,352,128]{2,1,0:T(8,128)S(1)}, u32[]{:S(2)}, u32[]{:S(2)}) collective-permute-start(f32[2,352,128]{2,1,0:T(8,128)S(1)} %collective-permute-done.1.refs_2_), channel_id=1, source_target_pairs={{0,1},{1,0},{2,3},{3,2},{4,5},{5,4},{6,7},{7,6},{8,9},{9,8},{10,11... | collective-permute-start | bytes 1081352 | tf_op jit(solution)/shard_map/ppermute | solution.py:555
  22.4 5.8 %collective-permute-start.9 = (f32[2,352,128]{2,1,0:T(8,128)S(1)}, f32[2,352,128]{2,1,0:T(8,128)S(1)}, u32[]{:S(2)}, u32[]{:S(2)}) collective-permute-start(f32[2,352,128]{2,1,0:T(8,128)S(1)} %collective-permute-done.2.refs_3_), channel_id=1, source_target_pairs={{0,1},{1,0},{2,3},{3,2},{4,5},{5,4},{6,7},{7,6},{8,9},{9,8},{10,11... | collective-permute-start | bytes 1081352 | tf_op jit(solution)/shard_map/ppermute | solution.py:555
  22.9 5.3 %collective-permute-start.12 = (f32[2,264,128]{2,1,0:T(8,128)S(1)}, f32[2,264,128]{2,1,0:T(8,128)S(1)}, u32[]{:S(2)}, u32[]{:S(2)}) collective-permute-start(f32[2,264,128]{2,1,0:T(8,128)S(1)} %collective-permute-done.5.refs_6_), channel_id=1, source_target_pairs={{0,1},{1,0},{2,3},{3,2},{4,5},{5,4},{6,7},{7,6},{8,9},{9,8},{10,11... | collective-permute-start | bytes 811016 | tf_op jit(solution)/shard_map/ppermute | solution.py:555
  26.8 1.4 %collective-permute-start.13 = (f32[2,176,128]{2,1,0:T(8,128)S(1)}, f32[2,176,128]{2,1,0:T(8,128)S(1)}, u32[]{:S(2)}, u32[]{:S(2)}) collective-permute-start(f32[2,176,128]{2,1,0:T(8,128)S(1)} %collective-permute-done.6.refs_7_), channel_id=1, source_target_pairs={{0,1},{1,0},{2,3},{3,2},{4,5},{5,4},{6,7},{7,6},{8,9},{9,8},{10,11... | collective-permute-start | bytes 540680 | tf_op jit(solution)/shard_map/ppermute | solution.py:555
  28.3 1.1 %copy-start = (f32[2,2,2,3,4,2,8,128]{7,6,5,4,3,2,1,0:T(8,128)S(1)}, f32[2,2,2,3,4,2,8,128]{7,6,5,4,3,2,1,0:T(8,128)}, u32[]{:S(2)}) copy-start(f32[2,2,2,3,4,2,8,128]{7,6,5,4,3,2,1,0:T(8,128)} %get-tuple-element.12.refs_0_) | copy-start | bytes 2359300

commit v4 on v3

--- a/solution.py
+++ b/solution.py
@@ -138,7 +138,7 @@
     at_row = lax.broadcasted_iota(jnp.int32, (SUBS, LANES), 0)
     at_lane = lax.broadcasted_iota(jnp.int32, (SUBS, LANES), 1)
     table = jnp.zeros((SUBS, LANES), jnp.float32)
-    for row, lane, value in scalars(sz, freq_ref, mix_ref, pml_ref):
+    for row, lane, value in scalars(sz, freq_ref, mix_ref, pml_ref, tiles_ref):
         table = jnp.where((at_row == row) & (at_lane == lane), value, table)
     table_ref[...] = table
 
@@ -157,7 +157,7 @@
                         swap_ref[1, h, r, c, x, z] = masked
 
 
-def scalars(sz, freq_ref, mix_ref, pml_ref):
+def scalars(sz, freq_ref, mix_ref, pml_ref, tiles_ref):
     for h in range(sz.harmonics):
         yield 0, h, freq_ref[h] * freq_ref[h]
     for axis in range(3):
@@ -166,6 +166,10 @@
         for side in range(2):
             for h in range(sz.harmonics):
                 yield 2 + side, p * sz.harmonics + h, mix_ref[p, side, h].astype(jnp.float32)
+    cols = sz.cy // TILE
+    for row in range(sz.cx // TILE):
+        for col in range(cols):
+            yield 4, row * cols + col, tiles_ref[row, col].astype(jnp.float32)
 
 
 def relay_kernel(sz, colour, even_ref, odd_ref, anti_ref, main_ref):
@@ -192,7 +196,8 @@
 def sweep_kernel(sz, mixes, table_ref, eps_ref, *refs):
     cx, cy, cz, halves = sz.cx, sz.cy, sz.cz, sz.halves
     wide, harmonics = sz.wide, sz.harmonics
-    blocks, refs = refs[:2], refs[2:]
+    src_ref, fwd_ref, theirs = refs[:3]
+    refs = refs[3:]
     per_core = 2 + 5 * len(sz.colours)
     sides = [refs[per_core * s : per_core * (s + 1)] for s in range(sz.ha)]
     out_ref, grad_ref = refs[per_core * sz.ha : per_core * sz.ha + 2]
@@ -296,14 +301,22 @@
 
     lax.fori_loop(0, wide, scales, 0)
 
-    for s, block in enumerate(blocks):
+    rows = slice(DEEP, DEEP + cy)
+    place = lax.broadcasted_iota(jnp.int32, (cy, LANES), 0) // TILE
+    cols = cy // TILE
+    for x in range(cx):
+        mask = jnp.zeros((cy, LANES), jnp.float32)
+        for col in range(cols):
+            mask = jnp.where(place == col, kerr_coef * table[4, x // TILE * cols + col], mask)
         for h, r, c in sz.kinds:
-            g = s * sz.owned + h
-            for x in range(cx):
-                for z in range(halves):
-                    rows = slice(DEEP, DEEP + cy)
-                    base[g, r, c, DEEP + x, z, rows] = block[0, h, r, c, x, z]
-                    fwd[g, r, c, NEAR + x, z, rows] = block[1, h, r, c, x, z]
+            g = sz.owned + h
+            for z in range(halves):
+                base[h, r, c, DEEP + x, z, rows] = (
+                    src_ref[h, r, c, x, :, half(z)] * invs[h, DEEP + x, z, rows]
+                )
+                fwd[h, r, c, NEAR + x, z, rows] = fwd_ref[h, r, c, x, :, half(z)] * mask
+                base[g, r, c, DEEP + x, z, rows] = theirs[0, h, r, c, x, z]
+                fwd[g, r, c, NEAR + x, z, rows] = theirs[1, h, r, c, x, z]
     for s, side in enumerate(sides):
         for buffer, groups, (plane_of, row_of) in row_buffers(side):
             for field, kind, plane, low, high, at in groups:
@@ -554,7 +567,7 @@
     for buffer in own:
         other.append(lax.ppermute(buffer, "ha", flip))
 
-    buffers = own[:1] + other[:1] + own[1:] + other[1:]
+    buffers = [adjoint_source, forward_field, other[0]] + own[1:] + other[1:]
     adjoint, gradient = pl.pallas_call(
         functools.partial(sweep_kernel, sz, mix_pairs.shape[1]),
         out_shape=[
@@ -574,7 +587,9 @@
             pltpu.SMEM((SUBS, LANES), f32),
             pltpu.SemaphoreType.DMA,
         ],
-        compiler_params=pltpu.CompilerParams(vmem_limit_bytes=32 * 1024 * 1024),
+        compiler_params=pltpu.CompilerParams(
+            vmem_limit_bytes=32 * 1024 * 1024,
+        ),
         name="sweeps",
     )(table, permittivity, *buffers)
     return (adjoint, gradient)

time: 41.9 us -> 39.1 us (0.933)
  waiting for transfers between devices: 11.8 us -> 10.1 us
  local copies, waits for them, and re-layouts: 1.14 us -> 0.02 us
    ppermute x7, waiting for transfers between devices: 9.33 us -> 7.1 us  [send(): return lax.ppermute(buffer, ('gx', 'gy'), swaps(sz.gx, sz.gy, partner))]
    unnamed x6 -> x8, local copies, waits for them, and re-layouts: 1.14 us -> 0.02 us
    ppermute x8, waiting for transfers between devices: 2.43 us -> 3 us  [shards(): other.append(lax.ppermute(buffer, 'ha', flip))]
  transfers between devices with their start and end apart: 15 -> 15, of which waited for: 5 -> 6; matrix products, arithmetic and copies ran while one was open for 0% -> 0% of each run, Pallas kernels for 0% -> 0%
where the time goes in v4:
time: 39.1 us; the launch traced here: 38.9 us
  Pallas kernels  15.2 us (39%)
  starting transfers between devices  12.9 us (33%)
  waiting for transfers between devices  10.1 us (26%)
  between operations  0.74 us (2%)
    pallas_call x1, Pallas kernels, shards(): pl.pallas_call(functools.partial(sweep_kernel, sz, mix_pairs.shape[1]), o...  12.3 us
    ppermute x7, starting transfers between devices, send(): return lax.ppermute(buffer, ('gx', 'gy'), swaps(sz.gx, sz.gy, partner))  11.6 us
    ppermute x7, waiting for transfers between devices, send(): return lax.ppermute(buffer, ('gx', 'gy'), swaps(sz.gx, sz.gy, partner))  7.1 us
    ppermute x8, waiting for transfers between devices, shards(): other.append(lax.ppermute(buffer, 'ha', flip))  3 us
    pallas_call x1, Pallas kernels, shards(): pl.pallas_call(functools.partial(pack_kernel, sz), out_shape=shapes, in_s...  2.87 us
    ppermute x8, starting transfers between devices, shards(): other.append(lax.ppermute(buffer, 'ha', flip))  1.25 us
  transfers between devices with their start and end apart: 15, of which 6 were waited for; matrix products, arithmetic and copies ran while one was open for 0% of the time, Pallas kernels for 0%

profile of v4, /device:TPU:0, one launch (start us, length us, event | category | flops | bytes accessed | tf_op | source)
XLA Modules:
  0.0 38.9 jit_solution(5083646234288217941)
XLA Ops:
  0.7 2.9 %pack.1 = (f32[2,176,128]{2,1,0:T(8,128)}, f32[2,176,128]{2,1,0:T(8,128)}, f32[2,264,128]{2,1,0:T(8,128)}, f32[2,352,128]{2,1,0:T(8,128)}, f32[2,352,128]{2,1,0:...) custom-call(f32[2,2,3,4,8,256]{5,4,3,2,1,0:T(8,128)} %refs_0_.1, f32[2,2,3,4,8,256]{5,4,3,2,1,0:T(8,128)} %refs_1_.1, ...), custom_call_target="tpu_custom_call" | custom-call | tf_op jit(solution)/shard_map/pack/pallas_call | solution.py:537
  3.5 3.1 %collective-permute-start.3 = (f32[2,176,128]{2,1,0:T(8,128)}, f32[2,176,128]{2,1,0:T(8,128)S(1)}, u32[]{:S(2)}, u32[]{:S(2)}) collective-permute-start(f32[2,176,128]{2,1,0:T(8,128)} %get-tuple-element.15), channel_id=1, source_target_pairs={{0,4},{2,6},{4,0},{6,2},{8,12},{10,14},{12,8},{14,10},{1,5},{3,7},... | collective-permute-start | bytes 540680 | tf_op jit(solution)/shard_map/ppermute | solution.py:521
  6.6 0.7 %collective-permute-start.4 = (f32[2,176,128]{2,1,0:T(8,128)}, f32[2,176,128]{2,1,0:T(8,128)S(1)}, u32[]{:S(2)}, u32[]{:S(2)}) collective-permute-start(f32[2,176,128]{2,1,0:T(8,128)} %get-tuple-element.16), channel_id=1, source_target_pairs={{4,8},{6,10},{8,4},{10,6},{5,9},{7,11},{9,5},{11,7},{20,24},{22,26... | collective-permute-start | bytes 540680 | tf_op jit(solution)/shard_map/ppermute | solution.py:521
  7.2 1.6 %collective-permute-start.5 = (f32[2,264,128]{2,1,0:T(8,128)}, f32[2,264,128]{2,1,0:T(8,128)S(1)}, u32[]{:S(2)}, u32[]{:S(2)}) collective-permute-start(f32[2,264,128]{2,1,0:T(8,128)} %get-tuple-element.17), channel_id=1, source_target_pairs={{0,2},{2,0},{4,6},{6,4},{8,10},{10,8},{12,14},{14,12},{1,3},{3,1},... | collective-permute-start | bytes 811016 | tf_op jit(solution)/shard_map/ppermute | solution.py:521
  8.8 0.0 collective-permute-start
  8.8 4.4 %collective-permute-start.1 = (f32[2,352,128]{2,1,0:T(8,128)}, f32[2,352,128]{2,1,0:T(8,128)S(1)}, u32[]{:S(2)}, u32[]{:S(2)}) collective-permute-start(f32[2,352,128]{2,1,0:T(8,128)} %get-tuple-element.13), channel_id=1, source_target_pairs={{0,4},{2,6},{4,0},{6,2},{8,12},{10,14},{12,8},{14,10},{1,5},{3,7},... | collective-permute-start | bytes 1081352 | tf_op jit(solution)/shard_map/ppermute | solution.py:521
  13.2 0.0 collective-permute-done.3.even_ref.refs_5_
  13.2 0.8 %collective-permute-start.2 = (f32[2,352,128]{2,1,0:T(8,128)}, f32[2,352,128]{2,1,0:T(8,128)S(1)}, u32[]{:S(2)}, u32[]{:S(2)}) collective-permute-start(f32[2,352,128]{2,1,0:T(8,128)} %get-tuple-element.14), channel_id=1, source_target_pairs={{4,8},{6,10},{8,4},{10,6},{5,9},{7,11},{9,5},{11,7},{20,24},{22,26... | collective-permute-start | bytes 1081352 | tf_op jit(solution)/shard_map/ppermute | solution.py:521
  14.0 0.0 collective-permute-done.4.odd_ref.refs_6_
  14.1 0.0 copy-start.3
  14.1 0.6 %collective-permute-start.7 = (f32[2,64,128]{2,1,0:T(8,128)S(1)}, f32[2,64,128]{2,1,0:T(8,128)S(1)}, u32[]{:S(2)}, u32[]{:S(2)}) collective-permute-start(f32[2,64,128]{2,1,0:T(8,128)S(1)} %get-tuple-element.19), channel_id=1, source_target_pairs={{0,2},{2,0},{4,6},{6,4},{8,10},{10,8},{12,14},{14,12},{1,3},{3,1},... | collective-permute-start | bytes 196616 | tf_op jit(solution)/shard_map/ppermute | solution.py:521
  14.7 3.7 %collective-permute-done.7.refs_9_ = f32[2,64,128]{2,1,0:T(8,128)S(1)} collective-permute-done((f32[2,64,128]{2,1,0:T(8,128)S(1)}, f32[2,64,128]{2,1,0:T(8,128)S(1)}, u32[]{:S(2)}, u32[]{:S(2)}) %collective-permute-start.7) | collective-permute-done | bytes 65568 | tf_op jit(solution)/shard_map/ppermute | solution.py:521
  18.4 0.5 %collective-permute-start.6 = (f32[2,176,128]{2,1,0:T(8,128)S(1)}, f32[2,176,128]{2,1,0:T(8,128)S(1)}, u32[]{:S(2)}, u32[]{:S(2)}) collective-permute-start(f32[2,176,128]{2,1,0:T(8,128)S(1)} %get-tuple-element.18), channel_id=1, source_target_pairs={{0,2},{2,0},{4,6},{6,4},{8,10},{10,8},{12,14},{14,12},{1,3},{3,1},... | collective-permute-start | bytes 540680 | tf_op jit(solution)/shard_map/ppermute | solution.py:521
  19.0 0.0 collective-permute-done.5.refs_7_
  19.0 0.0 collective-permute-start.14
  19.0 1.3 %collective-permute-done.14.refs_16_ = f32[2,64,128]{2,1,0:T(8,128)S(1)} collective-permute-done((f32[2,64,128]{2,1,0:T(8,128)S(1)}, f32[2,64,128]{2,1,0:T(8,128)S(1)}, u32[]{:S(2)}, u32[]{:S(2)}) %collective-permute-start.14) | collective-permute-done | bytes 65568 | tf_op jit(solution)/shard_map/ppermute | solution.py:568
  20.2 0.2 collective-permute-start.10
  20.4 2.1 %collective-permute-done.1.refs_3_ = f32[2,352,128]{2,1,0:T(8,128)S(1)} collective-permute-done((f32[2,352,128]{2,1,0:T(8,128)}, f32[2,352,128]{2,1,0:T(8,128)S(1)}, u32[]{:S(2)}, u32[]{:S(2)}) %collective-permute-start.1) | collective-permute-done | bytes 360480 | tf_op jit(solution)/shard_map/ppermute | solution.py:521
  22.5 0.0 collective-permute-start.11
  22.5 0.0 collective-permute-done.2.refs_4_
  22.5 0.5 %collective-permute-start.8 = (f32[2,352,128]{2,1,0:T(8,128)S(1)}, f32[2,352,128]{2,1,0:T(8,128)S(1)}, u32[]{:S(2)}, u32[]{:S(2)}) collective-permute-start(f32[2,352,128]{2,1,0:T(8,128)S(1)} %collective-permute-done.1.refs_3_), channel_id=1, source_target_pairs={{0,1},{1,0},{2,3},{3,2},{4,5},{5,4},{6,7},{7,6},{8,9},{9,8},{10,11... | collective-permute-start | bytes 1081352 | tf_op jit(solution)/shard_map/ppermute | solution.py:568
  23.0 1.2 %collective-permute-done.6.refs_8_ = f32[2,176,128]{2,1,0:T(8,128)S(1)} collective-permute-done((f32[2,176,128]{2,1,0:T(8,128)S(1)}, f32[2,176,128]{2,1,0:T(8,128)S(1)}, u32[]{:S(2)}, u32[]{:S(2)}) %collective-permute-start.6) | collective-permute-done | bytes 180256 | tf_op jit(solution)/shard_map/ppermute | solution.py:521
  24.2 0.0 collective-permute-start.9
  24.2 0.0 collective-permute-done.10.refs_12_
  24.3 0.5 %collective-permute-start.12 = (f32[2,264,128]{2,1,0:T(8,128)S(1)}, f32[2,264,128]{2,1,0:T(8,128)S(1)}, u32[]{:S(2)}, u32[]{:S(2)}) collective-permute-start(f32[2,264,128]{2,1,0:T(8,128)S(1)} %collective-permute-done.5.refs_7_), channel_id=1, source_target_pairs={{0,1},{1,0},{2,3},{3,2},{4,5},{5,4},{6,7},{7,6},{8,9},{9,8},{10,11... | collective-permute-start | bytes 811016 | tf_op jit(solution)/shard_map/ppermute | solution.py:568
  24.8 0.0 collective-permute-done.11.refs_13_
  24.8 0.1 collective-permute-start.13
  24.8 1.5 %collective-permute-done.12.refs_14_ = f32[2,264,128]{2,1,0:T(8,128)S(1)} collective-permute-done((f32[2,264,128]{2,1,0:T(8,128)S(1)}, f32[2,264,128]{2,1,0:T(8,128)S(1)}, u32[]{:S(2)}, u32[]{:S(2)}) %collective-permute-start.12) | collective-permute-done | bytes 270368 | tf_op jit(solution)/shard_map/ppermute | solution.py:568
  26.3 0.3 collective-permute-done.13.refs_15_
  26.6 0.0 collective-permute-done.8.refs_10_
  26.6 0.0 collective-permute-done.refs_2_
  26.6 12.3 %sweeps.1 = (f32[2,2,3,4,8,256]{5,4,3,2,1,0:T(8,128)}, f32[4,8,256]{2,1,0:T(8,128)}) custom-call(f32[8,128]{1,0:T(8,128)S(1)} %copy-done.3, f32[4,8,256]{2,1,0:T(8,128)S(1)} %copy-done.2, f32[2,2,3,4,8,256]{5,4,3,2,1,0:T(8,128)S(1)} %copy-done, f32[2,2,3,4,8,256]{5,4,3,2,1,0:T(8,128)S(1)} %copy-done.1, ...), custom_call_target="tpu_custom_call" | custom-call | tf_op jit(solution)/shard_map/sweeps/pallas_call | solution.py:571
  (9 shorter events, 0.1 us)
Async XLA Ops:
  0.6 25.9 %copy-start = (f32[2,2,3,4,8,256]{5,4,3,2,1,0:T(8,128)S(1)}, f32[2,2,3,4,8,256]{5,4,3,2,1,0:T(8,128)}, u32[]{:S(2)}) copy-start(f32[2,2,3,4,8,256]{5,4,3,2,1,0:T(8,128)} %refs_0_.1) | copy-start | bytes 1179652
  0.6 25.9 %copy-start.1 = (f32[2,2,3,4,8,256]{5,4,3,2,1,0:T(8,128)S(1)}, f32[2,2,3,4,8,256]{5,4,3,2,1,0:T(8,128)}, u32[]{:S(2)}) copy-start(f32[2,2,3,4,8,256]{5,4,3,2,1,0:T(8,128)} %refs_1_.1) | copy-start | bytes 1179652
  3.5 9.7 %collective-permute-start.3 = (f32[2,176,128]{2,1,0:T(8,128)}, f32[2,176,128]{2,1,0:T(8,128)S(1)}, u32[]{:S(2)}, u32[]{:S(2)}) collective-permute-start(f32[2,176,128]{2,1,0:T(8,128)} %get-tuple-element.15), channel_id=1, source_target_pairs={{0,4},{2,6},{4,0},{6,2},{8,12},{10,14},{12,8},{14,10},{1,5},{3,7},... | collective-permute-start | bytes 540680 | tf_op jit(solution)/shard_map/ppermute | solution.py:521
  6.6 7.4 %collective-permute-start.4 = (f32[2,176,128]{2,1,0:T(8,128)}, f32[2,176,128]{2,1,0:T(8,128)S(1)}, u32[]{:S(2)}, u32[]{:S(2)}) collective-permute-start(f32[2,176,128]{2,1,0:T(8,128)} %get-tuple-element.16), channel_id=1, source_target_pairs={{4,8},{6,10},{8,4},{10,6},{5,9},{7,11},{9,5},{11,7},{20,24},{22,26... | collective-permute-start | bytes 540680 | tf_op jit(solution)/shard_map/ppermute | solution.py:521
  7.2 11.7 %collective-permute-start.5 = (f32[2,264,128]{2,1,0:T(8,128)}, f32[2,264,128]{2,1,0:T(8,128)S(1)}, u32[]{:S(2)}, u32[]{:S(2)}) collective-permute-start(f32[2,264,128]{2,1,0:T(8,128)} %get-tuple-element.17), channel_id=1, source_target_pairs={{0,2},{2,0},{4,6},{6,4},{8,10},{10,8},{12,14},{14,12},{1,3},{3,1},... | collective-permute-start | bytes 811016 | tf_op jit(solution)/shard_map/ppermute | solution.py:521
  8.8 17.8 %collective-permute-start = (f32[2,2,2,3,4,2,8,128]{7,6,5,4,3,2,1,0:T(8,128)}, f32[2,2,2,3,4,2,8,128]{7,6,5,4,3,2,1,0:T(8,128)S(1)}, u32[]{:S(2)}, u32[]{:S(2)}) collective-permute-start(f32[2,2,2,3,4,2,8,128]{7,6,5,4,3,2,1,0:T(8,128)} %get-tuple-element.12), channel_id=1, source_target_pairs={{0,1},{1,0},{2,3},{3,2},{4,5},{5,4},{6,7},{7,6},{8,9},{9,8},{10,11... | collective-permute-start | bytes 2359304 | tf_op jit(solution)/shard_map/ppermute | solution.py:568
  8.8 13.7 %collective-permute-start.1 = (f32[2,352,128]{2,1,0:T(8,128)}, f32[2,352,128]{2,1,0:T(8,128)S(1)}, u32[]{:S(2)}, u32[]{:S(2)}) collective-permute-start(f32[2,352,128]{2,1,0:T(8,128)} %get-tuple-element.13), channel_id=1, source_target_pairs={{0,4},{2,6},{4,0},{6,2},{8,12},{10,14},{12,8},{14,10},{1,5},{3,7},... | collective-permute-start | bytes 1081352 | tf_op jit(solution)/shard_map/ppermute | solution.py:521
  13.2 13.4 %copy-start.2 = (f32[4,8,256]{2,1,0:T(8,128)S(1)}, f32[4,8,256]{2,1,0:T(8,128)}, u32[]{:S(2)}) copy-start(f32[4,8,256]{2,1,0:T(8,128)} %eps_ref.3) | copy-start | bytes 98308
  13.2 9.3 %collective-permute-start.2 = (f32[2,352,128]{2,1,0:T(8,128)}, f32[2,352,128]{2,1,0:T(8,128)S(1)}, u32[]{:S(2)}, u32[]{:S(2)}) collective-permute-start(f32[2,352,128]{2,1,0:T(8,128)} %get-tuple-element.14), channel_id=1, source_target_pairs={{4,8},{6,10},{8,4},{10,6},{5,9},{7,11},{9,5},{11,7},{20,24},{22,26... | collective-permute-start | bytes 1081352 | tf_op jit(solution)/shard_map/ppermute | solution.py:521
  14.1 12.5 %copy-start.3 = (f32[8,128]{1,0:T(8,128)S(1)}, f32[8,128]{1,0:T(8,128)}, u32[]{:S(2)}) copy-start(f32[8,128]{1,0:T(8,128)} %get-tuple-element.11.table_ref) | copy-start | bytes 12292
  14.1 4.3 %collective-permute-start.7 = (f32[2,64,128]{2,1,0:T(8,128)S(1)}, f32[2,64,128]{2,1,0:T(8,128)S(1)}, u32[]{:S(2)}, u32[]{:S(2)}) collective-permute-start(f32[2,64,128]{2,1,0:T(8,128)S(1)} %get-tuple-element.19), channel_id=1, source_target_pairs={{0,2},{2,0},{4,6},{6,4},{8,10},{10,8},{12,14},{14,12},{1,3},{3,1},... | collective-permute-start | bytes 196616 | tf_op jit(solution)/shard_map/ppermute | solution.py:521
  18.4 5.8 %collective-permute-start.6 = (f32[2,176,128]{2,1,0:T(8,128)S(1)}, f32[2,176,128]{2,1,0:T(8,128)S(1)}, u32[]{:S(2)}, u32[]{:S(2)}) collective-permute-start(f32[2,176,128]{2,1,0:T(8,128)S(1)} %get-tuple-element.18), channel_id=1, source_target_pairs={{0,2},{2,0},{4,6},{6,4},{8,10},{10,8},{12,14},{14,12},{1,3},{3,1},... | collective-permute-start | bytes 540680 | tf_op jit(solution)/shard_map/ppermute | solution.py:521
  19.0 1.3 %collective-permute-start.14 = (f32[2,64,128]{2,1,0:T(8,128)S(1)}, f32[2,64,128]{2,1,0:T(8,128)S(1)}, u32[]{:S(2)}, u32[]{:S(2)}) collective-permute-start(f32[2,64,128]{2,1,0:T(8,128)S(1)} %collective-permute-done.7.refs_9_), channel_id=1, source_target_pairs={{0,1},{1,0},{2,3},{3,2},{4,5},{5,4},{6,7},{7,6},{8,9},{9,8},{10,11... | collective-permute-start | bytes 196616 | tf_op jit(solution)/shard_map/ppermute | solution.py:568
  20.2 4.0 %collective-permute-start.10 = (f32[2,176,128]{2,1,0:T(8,128)S(1)}, f32[2,176,128]{2,1,0:T(8,128)S(1)}, u32[]{:S(2)}, u32[]{:S(2)}) collective-permute-start(f32[2,176,128]{2,1,0:T(8,128)S(1)} %collective-permute-done.3.even_ref.refs_5_), channel_id=1, source_target_pairs={{0,1},{1,0},{2,3},{3,2},{4,5},{5,4},{6,7},{7,6},{8,9},{9,8},{10,11... | collective-permute-start | bytes 540680 | tf_op jit(solution)/shard_map/ppermute | solution.py:568
  22.5 2.3 %collective-permute-start.11 = (f32[2,176,128]{2,1,0:T(8,128)S(1)}, f32[2,176,128]{2,1,0:T(8,128)S(1)}, u32[]{:S(2)}, u32[]{:S(2)}) collective-permute-start(f32[2,176,128]{2,1,0:T(8,128)S(1)} %collective-permute-done.4.odd_ref.refs_6_), channel_id=1, source_target_pairs={{0,1},{1,0},{2,3},{3,2},{4,5},{5,4},{6,7},{7,6},{8,9},{9,8},{10,11... | collective-permute-start | bytes 540680 | tf_op jit(solution)/shard_map/ppermute | solution.py:568
  22.5 4.1 %collective-permute-start.8 = (f32[2,352,128]{2,1,0:T(8,128)S(1)}, f32[2,352,128]{2,1,0:T(8,128)S(1)}, u32[]{:S(2)}, u32[]{:S(2)}) collective-permute-start(f32[2,352,128]{2,1,0:T(8,128)S(1)} %collective-permute-done.1.refs_3_), channel_id=1, source_target_pairs={{0,1},{1,0},{2,3},{3,2},{4,5},{5,4},{6,7},{7,6},{8,9},{9,8},{10,11... | collective-permute-start | bytes 1081352 | tf_op jit(solution)/shard_map/ppermute | solution.py:568
  24.2 2.3 %collective-permute-start.9 = (f32[2,352,128]{2,1,0:T(8,128)S(1)}, f32[2,352,128]{2,1,0:T(8,128)S(1)}, u32[]{:S(2)}, u32[]{:S(2)}) collective-permute-start(f32[2,352,128]{2,1,0:T(8,128)S(1)} %collective-permute-done.2.refs_4_), channel_id=1, source_target_pairs={{0,1},{1,0},{2,3},{3,2},{4,5},{5,4},{6,7},{7,6},{8,9},{9,8},{10,11... | collective-permute-start | bytes 1081352 | tf_op jit(solution)/shard_map/ppermute | solution.py:568
  24.3 2.1 %collective-permute-start.12 = (f32[2,264,128]{2,1,0:T(8,128)S(1)}, f32[2,264,128]{2,1,0:T(8,128)S(1)}, u32[]{:S(2)}, u32[]{:S(2)}) collective-permute-start(f32[2,264,128]{2,1,0:T(8,128)S(1)} %collective-permute-done.5.refs_7_), channel_id=1, source_target_pairs={{0,1},{1,0},{2,3},{3,2},{4,5},{5,4},{6,7},{7,6},{8,9},{9,8},{10,11... | collective-permute-start | bytes 811016 | tf_op jit(solution)/shard_map/ppermute | solution.py:568
  24.8 1.8 %collective-permute-start.13 = (f32[2,176,128]{2,1,0:T(8,128)S(1)}, f32[2,176,128]{2,1,0:T(8,128)S(1)}, u32[]{:S(2)}, u32[]{:S(2)}) collective-permute-start(f32[2,176,128]{2,1,0:T(8,128)S(1)} %collective-permute-done.6.refs_8_), channel_id=1, source_target_pairs={{0,1},{1,0},{2,3},{3,2},{4,5},{5,4},{6,7},{7,6},{8,9},{9,8},{10,11... | collective-permute-start | bytes 540680 | tf_op jit(solution)/shard_map/ppermute | solution.py:568
